TPU v7x, 32 devices: a whole 2x2x4 slice. The times are simulated.
32 devices in a mesh: dp: 4 (over y, core), ctx: 4 (over z), tensor: 2 (over x).
Axes of the slice: x: 2, y: 2, z: 4, core: 2. Of those that a mesh axis runs over, the one named last changes fastest.
Arguments:
- layer_input: bfloat16 [4, 2048, 2304], P('dp', 'ctx'), may hold values from -6 to 6
- block_order: int32 [4, 8], P('dp'), may hold values from 0 to 7, each once within a row
- pre_attend: bfloat16 [2304], P(('dp', 'ctx')), may hold values from 0.5 to 1.5
- query_weight: bfloat16 [2304, 2048], P(('dp', 'ctx'), 'tensor'), may hold values from -0.25 to 0.25
- key_weight: bfloat16 [2304, 1024], P(('dp', 'ctx'), 'tensor'), may hold values from -0.125 to 0.125
- value_weight: bfloat16 [2304, 1024], P(('dp', 'ctx'), 'tensor'), may hold values from -0.125 to 0.125
- output_weight: bfloat16 [2048, 2304], P('tensor', ('dp', 'ctx')), may hold values from -0.125 to 0.125
- post_attend: bfloat16 [2304], P(('dp', 'ctx')), may hold values from 0.5 to 1.5
- pre_feed: bfloat16 [2304], P(('dp', 'ctx')), may hold values from 0.5 to 1.5
- gate_weight: bfloat16 [2304, 9216], P(('dp', 'ctx'), 'tensor'), may hold values from -0.125 to 0.125
- up_weight: bfloat16 [2304, 9216], P(('dp', 'ctx'), 'tensor'), may hold values from -0.125 to 0.125
- down_weight: bfloat16 [9216, 2304], P('tensor', ('dp', 'ctx')), may hold values from -0.0625 to 0.0625
- post_feed: bfloat16 [2304], P(('dp', 'ctx')), may hold values from 0.5 to 1.5
- cotangent: bfloat16 [4, 2048, 2304], P('dp', 'ctx'), may hold values from -6 to 6
Outputs:
- layer_output: bfloat16 [4, 2048, 2304], P('dp', 'ctx')
- input_grad: float32 [4, 2048, 2304], P('dp', 'ctx')
- pre_attend_grad: float32 [2304], P(('dp', 'ctx'))
- query_weight_grad: float32 [2304, 2048], P(('dp', 'ctx'), 'tensor')
- key_weight_grad: float32 [2304, 1024], P(('dp', 'ctx'), 'tensor')
- value_weight_grad: float32 [2304, 1024], P(('dp', 'ctx'), 'tensor')
- output_weight_grad: float32 [2048, 2304], P('tensor', ('dp', 'ctx'))
- post_attend_grad: float32 [2304], P(('dp', 'ctx'))
- pre_feed_grad: float32 [2304], P(('dp', 'ctx'))
- gate_weight_grad: float32 [2304, 9216], P(('dp', 'ctx'), 'tensor')
- up_weight_grad: float32 [2304, 9216], P(('dp', 'ctx'), 'tensor')
- down_weight_grad: float32 [9216, 2304], P('tensor', ('dp', 'ctx'))
- post_feed_grad: float32 [2304], P(('dp', 'ctx'))
Inputs may be any that keep to these rules, and one draw needn't show every extreme that they name: Each row of block_order names every one of the 8 blocks of a sequence once.
All inputs are finite; a program needn't handle non-finite values.
Results may differ from a plain program's by a relative error of at most 0.02.
Values may be sent and summed in bfloat16 or wider, within the bound.
No kernel may reach another device: no remote copies, remote signals or barrier semaphores. Data moves between devices by JAX's collectives and lax.ppermute only.
A program may use at most 320 MiB of HBM per device.

v0:
```python
import jax
import jax.numpy as jnp
from jax import lax
from jax.sharding import PartitionSpec as P

HQ = 8
KV = 4
HD = 256
LEN = 2048


epsilon = 1e-06
cap_value = 50.0
gelu_coef = 0.7978845608028654
masked_value = -1e30


def rms_norm(values, gain):
    factor = lax.rsqrt(jnp.mean(values * values, axis=-1, keepdims=True) + epsilon)
    return values * factor * gain


def gelu_tanh(values):
    return (
        0.5 * values * (1.0 + jnp.tanh(gelu_coef * (values + 0.044715 * values * values * values)))
    )


def gated_product(gate, upward):
    return gelu_tanh(gate) * upward


def rotary_tables(positions, head_size):
    half = head_size // 2
    freqs = 10000.0 ** (-(jnp.arange(half, dtype=jnp.float32) * 2.0) / head_size)
    angle = positions.astype(jnp.float32)[:, None] * freqs[None, :]
    return (jnp.cos(angle), jnp.sin(angle))


def rotate(values, cosine, sine):
    half = values.shape[-1] // 2
    first = values[..., :half]
    second = values[..., half:]
    cosine = cosine[:, None, :]
    sine = sine[:, None, :]
    return jnp.concatenate(
        [first * cosine - second * sine, second * cosine + first * sine], axis=-1
    )


def unrotate(grads, cosine, sine):
    half = grads.shape[-1] // 2
    first = grads[..., :half]
    second = grads[..., half:]
    cosine = cosine[:, None, :]
    sine = sine[:, None, :]
    return jnp.concatenate(
        [first * cosine + second * sine, second * cosine - first * sine], axis=-1
    )


def attend_probs(raw, visible):
    capped = cap_value * jnp.tanh(raw / cap_value)
    capped = jnp.where(visible, capped, masked_value)
    return jax.nn.softmax(capped, axis=-1)


def contract(left, right, left_dim, right_dim):
    return lax.dot_general(
        left, right, (((left_dim,), (right_dim,)), ((), ())), preferred_element_type=jnp.float32
    )


def body(
    layer_input,
    block_order,
    pre_attend,
    query_weight,
    key_weight,
    value_weight,
    output_weight,
    post_attend,
    pre_feed,
    gate_weight,
    up_weight,
    down_weight,
    post_feed,
    cotangent,
):
    seq_count, local_len, width = layer_input.shape
    block_len = LEN // block_order.shape[1]
    per_group = HQ // KV
    groups_here = KV // lax.axis_size("tensor")
    row_count = seq_count * local_len
    factor = HD ** (-0.5)
    data_count = lax.axis_size("dp")
    context_count = lax.axis_size("ctx")
    share_rows = width // (data_count * context_count)
    context_index = lax.axis_index("ctx")
    all_pos = (
        block_order[:, :, None] * block_len + jnp.arange(block_len, dtype=jnp.int32)[None, None, :]
    ).reshape(seq_count, LEN)
    local_pos = lax.dynamic_slice_in_dim(all_pos, context_index * local_len, local_len, 1)
    cosine, sine = rotary_tables(local_pos.reshape(row_count), HD)
    visible = local_pos[:, :, None] >= all_pos[:, None, :]
    inputs = layer_input.astype(jnp.float32).reshape(row_count, width)
    cot_rows = cotangent.astype(jnp.float32).reshape(row_count, width)

    def pick(matrix):
        shaped = matrix.reshape(matrix.shape[0], data_count, context_count, share_rows)
        return lax.dynamic_slice_in_dim(shaped, context_index, 1, 2).reshape(
            matrix.shape[0], data_count * share_rows
        )

    attend_set = (
        lax.all_gather(pre_attend, ("dp", "ctx"), axis=0, tiled=True),
        lax.all_gather(post_attend, ("dp", "ctx"), axis=0, tiled=True),
        lax.all_gather(query_weight, ("dp", "ctx"), axis=0, tiled=True),
        lax.all_gather(key_weight, ("dp", "ctx"), axis=0, tiled=True),
        lax.all_gather(value_weight, ("dp", "ctx"), axis=0, tiled=True),
        lax.all_gather(output_weight, ("dp", "ctx"), axis=1, tiled=True),
    )
    gain_in, gain_out, query_mat, key_mat, value_mat, out_mat = attend_set
    attend_in = rms_norm(inputs, gain_in.astype(jnp.float32)).astype(jnp.bfloat16)
    query_pre = jnp.dot(attend_in, query_mat, preferred_element_type=jnp.float32)
    key_pre = jnp.dot(attend_in, key_mat, preferred_element_type=jnp.float32)
    value_pre = jnp.dot(attend_in, value_mat, preferred_element_type=jnp.float32)
    queries = (
        rotate(query_pre.reshape(row_count, -1, HD), cosine, sine)
        .astype(jnp.bfloat16)
        .reshape(seq_count, local_len, groups_here, per_group, HD)
    )
    keys_local = (
        rotate(key_pre.reshape(row_count, groups_here, HD), cosine, sine)
        .astype(jnp.bfloat16)
        .reshape(seq_count, local_len, groups_here * HD)
    )
    values_local = value_pre.astype(jnp.bfloat16).reshape(seq_count, local_len, groups_here * HD)
    keys_all, values_all = (
        lax.all_gather(keys_local, "ctx", axis=1, tiled=True),
        lax.all_gather(values_local, "ctx", axis=1, tiled=True),
    )

    def forward_seq(items):
        query_seq, key_seq, value_seq, visible_seq = items
        key_heads = key_seq.reshape(LEN, groups_here, HD)
        value_heads = value_seq.reshape(LEN, groups_here, HD)
        raw = (
            jnp.einsum("qgrd,kgd->grqk", query_seq, key_heads, preferred_element_type=jnp.float32)
            * factor
        )
        weights_low = attend_probs(raw, visible_seq).astype(jnp.bfloat16)
        result = jnp.einsum(
            "grqk,kgd->qgrd", weights_low, value_heads, preferred_element_type=jnp.float32
        )
        return result.astype(jnp.bfloat16).reshape(local_len, groups_here * per_group * HD)

    attended = lax.map(forward_seq, (queries, keys_all, values_all, visible)).reshape(row_count, -1)
    attend_out = lax.psum(jnp.dot(attended, out_mat, preferred_element_type=jnp.float32), "tensor")
    hidden_mid = inputs + rms_norm(attend_out, gain_out.astype(jnp.float32))
    feed_set = (
        lax.all_gather(pre_feed, ("dp", "ctx"), axis=0, tiled=True),
        lax.all_gather(post_feed, ("dp", "ctx"), axis=0, tiled=True),
        lax.all_gather(gate_weight, ("dp", "ctx"), axis=0, tiled=True),
        lax.all_gather(up_weight, ("dp", "ctx"), axis=0, tiled=True),
        lax.all_gather(down_weight, ("dp", "ctx"), axis=1, tiled=True),
    )
    feed_gain, feed_post, gate_mat, up_mat, down_mat = feed_set
    feed_in = rms_norm(hidden_mid, feed_gain.astype(jnp.float32)).astype(jnp.bfloat16)
    gate = jnp.dot(feed_in, gate_mat, preferred_element_type=jnp.float32)
    upward = jnp.dot(feed_in, up_mat, preferred_element_type=jnp.float32)
    mixed = gated_product(gate, upward).astype(jnp.bfloat16)
    feed_out = lax.psum(jnp.dot(mixed, down_mat, preferred_element_type=jnp.float32), "tensor")
    layer_output = (
        (hidden_mid + rms_norm(feed_out, feed_post.astype(jnp.float32)))
        .astype(jnp.bfloat16)
        .reshape(seq_count, local_len, width)
    )
    back_set = (
        lax.all_gather(pre_feed, ("dp", "ctx"), axis=0, tiled=True),
        lax.all_gather(post_feed, ("dp", "ctx"), axis=0, tiled=True),
        lax.all_gather(gate_weight, ("dp", "ctx"), axis=0, tiled=True),
        lax.all_gather(up_weight, ("dp", "ctx"), axis=0, tiled=True),
        lax.all_gather(down_weight, ("dp", "ctx"), axis=1, tiled=True),
        lax.all_gather(pre_attend, ("dp", "ctx"), axis=0, tiled=True),
        lax.all_gather(post_attend, ("dp", "ctx"), axis=0, tiled=True),
        lax.all_gather(query_weight, ("dp", "ctx"), axis=0, tiled=True),
        lax.all_gather(key_weight, ("dp", "ctx"), axis=0, tiled=True),
        lax.all_gather(value_weight, ("dp", "ctx"), axis=0, tiled=True),
        lax.all_gather(output_weight, ("dp", "ctx"), axis=1, tiled=True),
    )
    feed_back = back_set[0:5]
    attend_back = back_set[5:11]
    feed_gain, feed_post, gate_mat, up_mat, down_mat = feed_back
    _, post_feed_back = jax.vjp(rms_norm, feed_out, feed_post.astype(jnp.float32))
    d_feed_out, post_feed_grad = post_feed_back(cot_rows)
    d_feed_low = d_feed_out.astype(jnp.bfloat16)
    d_mixed = contract(d_feed_low, down_mat, 1, 1)
    _, gate_back = jax.vjp(gated_product, gate, upward)
    d_gate, d_upward = gate_back(d_mixed)
    d_gate = d_gate.astype(jnp.bfloat16)
    d_upward = d_upward.astype(jnp.bfloat16)
    d_feed_in = lax.psum(
        contract(d_gate, gate_mat, 1, 1) + contract(d_upward, up_mat, 1, 1), "tensor"
    )
    _, mid_back = jax.vjp(rms_norm, hidden_mid, feed_gain.astype(jnp.float32))
    d_from_feed, pre_feed_grad = mid_back(d_feed_in)
    d_mid = cot_rows + d_from_feed
    feed_piece = lax.all_gather(feed_in, "ctx", axis=0, tiled=True)
    gate_piece = lax.all_gather(d_gate, "ctx", axis=0, tiled=True)
    upward_piece = lax.all_gather(d_upward, "ctx", axis=0, tiled=True)
    mixed_piece = lax.all_gather(mixed, "ctx", axis=0, tiled=True)
    out_piece = lax.all_gather(d_feed_low, "ctx", axis=0, tiled=True)
    feed_cols = pick(feed_piece)
    out_cols = pick(out_piece)
    feed_grads = (
        lax.psum_scatter(
            contract(feed_cols, gate_piece, 0, 0).astype(jnp.bfloat16),
            "dp",
            scatter_dimension=0,
            tiled=True,
        ).astype(jnp.float32),
        lax.psum_scatter(
            contract(feed_cols, upward_piece, 0, 0).astype(jnp.bfloat16),
            "dp",
            scatter_dimension=0,
            tiled=True,
        ).astype(jnp.float32),
        lax.psum_scatter(
            contract(mixed_piece, out_cols, 0, 0).astype(jnp.bfloat16),
            "dp",
            scatter_dimension=1,
            tiled=True,
        ).astype(jnp.float32),
    )
    gain_in, gain_out, query_mat, key_mat, value_mat, out_mat = attend_back
    _, post_attend_back = jax.vjp(rms_norm, attend_out, gain_out.astype(jnp.float32))
    d_attend_out, post_attend_grad = post_attend_back(d_mid)
    d_attend_low = d_attend_out.astype(jnp.bfloat16)
    d_attended = (
        contract(d_attend_low, out_mat, 1, 1)
        .astype(jnp.bfloat16)
        .reshape(seq_count, local_len, groups_here, per_group, HD)
    )

    def backward_seq(items):
        query_seq, key_seq, value_seq, visible_seq, d_seq = items
        key_heads = key_seq.reshape(LEN, groups_here, HD)
        value_heads = value_seq.reshape(LEN, groups_here, HD)
        raw = (
            jnp.einsum("qgrd,kgd->grqk", query_seq, key_heads, preferred_element_type=jnp.float32)
            * factor
        )
        probs, prob_back = jax.vjp(lambda inner: attend_probs(inner, visible_seq), raw)
        d_probs = jnp.einsum(
            "qgrd,kgd->grqk", d_seq, value_heads, preferred_element_type=jnp.float32
        )
        d_raw = prob_back(d_probs)[0].astype(jnp.bfloat16)
        d_query = (
            jnp.einsum("grqk,kgd->qgrd", d_raw, key_heads, preferred_element_type=jnp.float32)
            * factor
        )
        d_key = (
            jnp.einsum("grqk,qgrd->kgd", d_raw, query_seq, preferred_element_type=jnp.float32)
            * factor
        )
        d_value = jnp.einsum(
            "grqk,qgrd->kgd", probs.astype(jnp.bfloat16), d_seq, preferred_element_type=jnp.float32
        )
        return (d_query.reshape(local_len, -1), d_key.reshape(LEN, -1), d_value.reshape(LEN, -1))

    d_query, d_key_all, d_value_all = lax.map(
        backward_seq, (queries, keys_all, values_all, visible, d_attended)
    )
    d_key_local, d_value_local = (
        lax.psum_scatter(
            d_key_all.astype(jnp.bfloat16), "ctx", scatter_dimension=1, tiled=True
        ).astype(jnp.float32),
        lax.psum_scatter(
            d_value_all.astype(jnp.bfloat16), "ctx", scatter_dimension=1, tiled=True
        ).astype(jnp.float32),
    )
    d_query_pre = (
        unrotate(d_query.reshape(row_count, -1, HD), cosine, sine)
        .reshape(row_count, -1)
        .astype(jnp.bfloat16)
    )
    d_key_pre = (
        unrotate(d_key_local.reshape(row_count, groups_here, HD), cosine, sine)
        .reshape(row_count, -1)
        .astype(jnp.bfloat16)
    )
    d_value_pre = d_value_local.reshape(row_count, -1).astype(jnp.bfloat16)
    d_attend_in = lax.psum(
        (
            contract(d_query_pre, query_mat, 1, 1)
            + contract(d_key_pre, key_mat, 1, 1)
            + contract(d_value_pre, value_mat, 1, 1)
        ).astype(jnp.bfloat16),
        "tensor",
    ).astype(jnp.float32)
    _, in_back = jax.vjp(rms_norm, inputs, gain_in.astype(jnp.float32))
    d_from_attend, pre_attend_grad = in_back(d_attend_in)
    input_grad = (d_mid + d_from_attend).reshape(seq_count, local_len, width)
    in_piece = lax.all_gather(attend_in, "ctx", axis=0, tiled=True)
    query_piece = lax.all_gather(d_query_pre, "ctx", axis=0, tiled=True)
    key_piece = lax.all_gather(d_key_pre, "ctx", axis=0, tiled=True)
    value_piece = lax.all_gather(d_value_pre, "ctx", axis=0, tiled=True)
    att_piece = lax.all_gather(attended, "ctx", axis=0, tiled=True)
    out_piece = lax.all_gather(d_attend_low, "ctx", axis=0, tiled=True)
    in_cols = pick(in_piece)
    out_cols = pick(out_piece)
    attend_grads = (
        lax.psum_scatter(
            contract(in_cols, query_piece, 0, 0).astype(jnp.bfloat16),
            "dp",
            scatter_dimension=0,
            tiled=True,
        ).astype(jnp.float32),
        lax.psum_scatter(
            contract(in_cols, key_piece, 0, 0).astype(jnp.bfloat16),
            "dp",
            scatter_dimension=0,
            tiled=True,
        ).astype(jnp.float32),
        lax.psum_scatter(
            contract(in_cols, value_piece, 0, 0).astype(jnp.bfloat16),
            "dp",
            scatter_dimension=0,
            tiled=True,
        ).astype(jnp.float32),
        lax.psum_scatter(
            contract(att_piece, out_cols, 0, 0).astype(jnp.bfloat16),
            "dp",
            scatter_dimension=1,
            tiled=True,
        ).astype(jnp.float32),
    )
    gains = (
        lax.psum_scatter(pre_attend_grad, ("dp", "ctx"), scatter_dimension=0, tiled=True),
        lax.psum_scatter(post_attend_grad, ("dp", "ctx"), scatter_dimension=0, tiled=True),
        lax.psum_scatter(pre_feed_grad, ("dp", "ctx"), scatter_dimension=0, tiled=True),
        lax.psum_scatter(post_feed_grad, ("dp", "ctx"), scatter_dimension=0, tiled=True),
    )
    return (
        layer_output,
        input_grad,
        gains[0],
        attend_grads[0],
        attend_grads[1],
        attend_grads[2],
        attend_grads[3],
        gains[1],
        gains[2],
        feed_grads[0],
        feed_grads[1],
        feed_grads[2],
        gains[3],
    )


def solution(mesh):
    return jax.shard_map(
        body,
        mesh=mesh,
        in_specs=(
            P("dp", "ctx", None),
            P("dp", None),
            P(("dp", "ctx")),
            P(("dp", "ctx"), "tensor"),
            P(("dp", "ctx"), "tensor"),
            P(("dp", "ctx"), "tensor"),
            P("tensor", ("dp", "ctx")),
            P(("dp", "ctx")),
            P(("dp", "ctx")),
            P(("dp", "ctx"), "tensor"),
            P(("dp", "ctx"), "tensor"),
            P("tensor", ("dp", "ctx")),
            P(("dp", "ctx")),
            P("dp", "ctx", None),
        ),
        out_specs=(
            P("dp", "ctx", None),
            P("dp", "ctx", None),
            P(("dp", "ctx")),
            P(("dp", "ctx"), "tensor"),
            P(("dp", "ctx"), "tensor"),
            P(("dp", "ctx"), "tensor"),
            P("tensor", ("dp", "ctx")),
            P(("dp", "ctx")),
            P(("dp", "ctx")),
            P(("dp", "ctx"), "tensor"),
            P(("dp", "ctx"), "tensor"),
            P("tensor", ("dp", "ctx")),
            P(("dp", "ctx")),
        ),
        check_vma=False,
    )
```

profile of v0, /device:TPU:0, one launch (start us, length us, event | category | flops | bytes accessed | tf_op | source)
XLA Modules:
  0.0 3500.2 jit_solution(3145917364104461122)
XLA Ops:
  14.1 63.9 %all-reduce.9 = (bf16[2304]{0:T(1024)(128)(2,1)S(1)}, bf16[2304]{0:T(1024)(128)(2,1)S(1)}, bf16[2304]{0:T(1024)(128)(2,1)S(1)}, bf16[2304]{0:T(1024)(128)(2,1)S(1)}) all-reduce(bf16[2304]{0:T(1024)(128)(2,1)S(1)} %dynamic-update-slice, bf16[2304]{0:T(1024)(128)(2,1)S(1)} %dynamic-update-slice.1, ...), channel_id=1, replica_groups=mesh['dp'=4,'ctx'=4,'tensor'=2] {'dp','ctx'}, use_global_device_ids=true, to_apply=%add | all-reduce | flops 9216 | bytes 36864
  89.9 8.7 all-gather.25.cloned.1.call-done
  109.5 36.0 %all-gather.59.cloned.1.call-done = bf16[2048,512]{1,0:T(8,128)(2,1)} async-done(((bf16[512,512]{1,0:T(8,128)(2,1)}), bf16[2048,512]{1,0:T(8,128)(2,1)}) %all-gather.59.cloned.1.call-update) | async-done | bytes 2097168 | tf_op jit(solution)/shard_map/all_gather | solution.py:141
  149.5 50.3 %all-gather.29.cloned.1.call-done = bf16[2304,1024]{1,0:T(8,128)(2,1)} async-done(((bf16[144,1024]{1,0:T(8,128)(2,1)}), bf16[2304,1024]{1,0:T(8,128)(2,1)}) %all-gather.29.cloned.1.call-update) | async-done | bytes 4718608 | tf_op jit(solution)/shard_map/all_gather | solution.py:118
  214.8 31.5 all-gather.27.cloned.1.call-done
  246.3 13.6 fusion.79
  272.5 28.0 all-gather.31.cloned.1.call-done
  309.4 115.7 %all-reduce.15.cloned.1.call-done = f32[512,2304]{1,0:T(8,128)} async-done(((f32[512,2304]{1,0:T(8,128)}), f32[512,2304]{1,0:T(8,128)}) %all-reduce.15.cloned.1.call-update) | async-done | bytes 4718608 | tf_op jit(solution)/shard_map/psum | solution.py:159
  432.8 110.1 %all-gather.33.cloned.1.call-done = bf16[2304,4608]{1,0:T(8,128)(2,1)} async-done(((bf16[144,4608]{1,0:T(8,128)(2,1)}), bf16[2304,4608]{1,0:T(8,128)(2,1)}) %all-gather.33.cloned.1.call-update) | async-done | bytes 21233680 | tf_op jit(solution)/shard_map/all_gather | solution.py:164
  542.9 17.9 fusion.81
  560.8 99.8 %all-gather.35.cloned.1.call-done = bf16[2304,4608]{1,0:T(8,128)(2,1)} async-done(((bf16[144,4608]{1,0:T(8,128)(2,1)}), bf16[2304,4608]{1,0:T(8,128)(2,1)}) %all-gather.35.cloned.1.call-update) | async-done | bytes 21233680 | tf_op jit(solution)/shard_map/all_gather | solution.py:165
  660.6 20.5 multiply_convert_fusion.1
  681.1 97.0 %all-gather.37.cloned.1.call-done = bf16[4608,2304]{0,1:T(8,128)(2,1)} async-done(((bf16[4608,144]{0,1:T(8,128)(2,1)}), bf16[4608,2304]{0,1:T(8,128)(2,1)}) %all-gather.37.cloned.1.call-update) | async-done | bytes 21233680 | tf_op jit(solution)/shard_map/all_gather | solution.py:166
  778.1 17.1 fusion.82
  795.3 119.3 %all-reduce.17.cloned.1.call-done = f32[512,2304]{1,0:T(8,128)} async-done(((f32[512,2304]{1,0:T(8,128)}), f32[512,2304]{1,0:T(8,128)}) %all-reduce.17.cloned.1.call-update) | async-done | bytes 4718608 | tf_op jit(solution)/shard_map/psum | solution.py:173
  925.8 27.1 multiply_convert_fusion
  952.9 17.1 fusion.83
  969.9 17.7 convolution_add_fusion
  988.4 118.7 %all-reduce.19.cloned.1.call-done = f32[512,2304]{1,0:T(8,128)} async-done(((f32[512,2304]{1,0:T(8,128)}), f32[512,2304]{1,0:T(8,128)}) %all-reduce.19.cloned.1.call-update) | async-done | bytes 4718608 | tf_op jit(solution)/shard_map/psum | solution.py:203
  1130.4 11.4 fusion.8
  1141.8 17.9 fusion.2
  1159.7 7.2 fusion.42
  1175.1 35.8 %reduce-scatter.10.cloned.1.call-done = bf16[1,512,512]{1,2,0:T(8,128)(2,1)} async-done(((bf16[1,2048,512]{1,2,0:T(8,128)(2,1)}), bf16[1,512,512]{1,2,0:T(8,128)(2,1)}) %reduce-scatter.10.cloned.1.call-update) | async-done | bytes 524304 | tf_op jit(solution)/shard_map/reduce_scatter | solution.py:276
  1213.3 43.1 %reduce-scatter.12.cloned.1.call-done = bf16[1,512,512]{1,2,0:T(8,128)(2,1)} async-done(((bf16[1,2048,512]{1,2,0:T(8,128)(2,1)}), bf16[1,512,512]{1,2,0:T(8,128)(2,1)}) %reduce-scatter.12.cloned.1.call-update) | async-done | bytes 524304 | tf_op jit(solution)/shard_map/reduce_scatter | solution.py:279
  1279.5 145.1 %all-gather.39.cloned.1.call-done = bf16[2048,2304]{1,0:T(8,128)(2,1)} async-done(((bf16[512,2304]{1,0:T(8,128)(2,1)}), bf16[2048,2304]{1,0:T(8,128)(2,1)}) %all-gather.39.cloned.1.call-update) | async-done | bytes 9437200 | tf_op jit(solution)/shard_map/all_gather | solution.py:305
  1424.5 12.8 copy.73
  1439.1 31.6 all-gather.43.cloned.1.call-done
  1474.7 42.3 %all-gather.61.cloned.1.call-done = bf16[1,2048,512]{1,2,0:T(8,128)(2,1)} async-done(((bf16[1,512,512]{1,2,0:T(8,128)(2,1)}), bf16[1,2048,512]{1,2,0:T(8,128)(2,1)}) %all-gather.61.cloned.1.call-update) | async-done | bytes 2097168 | tf_op jit(solution)/shard_map/all_gather | solution.py:308
  1520.8 77.1 %all-gather.41.cloned.1.call-done = bf16[2048,1024]{0,1:T(8,128)(2,1)} async-done(((bf16[512,1024]{0,1:T(8,128)(2,1)}), bf16[2048,1024]{0,1:T(8,128)(2,1)}) %all-gather.41.cloned.1.call-update) | async-done | bytes 4194320 | tf_op jit(solution)/shard_map/all_gather | solution.py:306
  1603.9 161.7 %all-gather.57.cloned.1.call-done = bf16[2048,2304]{1,0:T(8,128)(2,1)} async-done(((bf16[512,2304]{1,0:T(8,128)(2,1)}), bf16[2048,2304]{1,0:T(8,128)(2,1)}) %all-gather.57.cloned.1.call-update) | async-done | bytes 9437200 | tf_op jit(solution)/shard_map/all_gather | solution.py:213
  1765.5 13.0 copy.76
  1780.5 151.5 %all-gather.47.cloned.1.call-done = bf16[2048,2304]{1,0:T(8,128)(2,1)} async-done(((bf16[512,2304]{1,0:T(8,128)(2,1)}), bf16[2048,2304]{1,0:T(8,128)(2,1)}) %all-gather.47.cloned.1.call-update) | async-done | bytes 9437200 | tf_op jit(solution)/shard_map/all_gather | solution.py:310
  1932.0 12.8 copy.74
  1948.1 64.5 %all-gather.45.cloned.1.call-done = bf16[2048,1024]{0,1:T(8,128)(2,1)} async-done(((bf16[512,1024]{0,1:T(8,128)(2,1)}), bf16[2048,1024]{0,1:T(8,128)(2,1)}) %all-gather.45.cloned.1.call-update) | async-done | bytes 4194320 | tf_op jit(solution)/shard_map/all_gather | solution.py:309
  2019.6 316.4 %all-gather.55.cloned.1.call-done = bf16[2048,4608]{1,0:T(8,128)(2,1)} async-done(((bf16[512,4608]{1,0:T(8,128)(2,1)}), bf16[2048,4608]{1,0:T(8,128)(2,1)}) %all-gather.55.cloned.1.call-update) | async-done | bytes 18874384 | tf_op jit(solution)/shard_map/all_gather | solution.py:212
  2336.1 16.5 convolution_convert_fusion
  2352.6 150.7 %all-gather.49.cloned.1.call-done = bf16[2048,2304]{1,0:T(8,128)(2,1)} async-done(((bf16[512,2304]{1,0:T(8,128)(2,1)}), bf16[2048,2304]{1,0:T(8,128)(2,1)}) %all-gather.49.cloned.1.call-update) | async-done | bytes 9437200 | tf_op jit(solution)/shard_map/all_gather | solution.py:209
  2503.4 13.0 copy.75
  2518.4 307.3 %all-gather.51.cloned.1.call-done = bf16[2048,4608]{1,0:T(8,128)(2,1)} async-done(((bf16[512,4608]{1,0:T(8,128)(2,1)}), bf16[2048,4608]{1,0:T(8,128)(2,1)}) %all-gather.51.cloned.1.call-update) | async-done | bytes 18874384 | tf_op jit(solution)/shard_map/all_gather | solution.py:210
  2825.7 16.5 convolution_convert_fusion.2
  2842.5 306.3 %all-gather.53.cloned.1.call-done = bf16[2048,4608]{1,0:T(8,128)(2,1)} async-done(((bf16[512,4608]{1,0:T(8,128)(2,1)}), bf16[2048,4608]{1,0:T(8,128)(2,1)}) %all-gather.53.cloned.1.call-update) | async-done | bytes 18874384 | tf_op jit(solution)/shard_map/all_gather | solution.py:211
  3148.8 16.5 convolution_convert_fusion.1
  3166.2 52.9 %all-reduce.21.cloned.1.call-done = bf16[512,2304]{1,0:T(8,128)(2,1)} async-done(((bf16[512,2304]{1,0:T(8,128)(2,1)}), bf16[512,2304]{1,0:T(8,128)(2,1)}) %all-reduce.21.cloned.1.call-update) | async-done | bytes 2359312 | tf_op jit(solution)/shard_map/psum | solution.py:294
  3222.8 61.8 %all-reduce.8 = (f32[2304]{0:T(1024)S(1)}, f32[2304]{0:T(1024)S(1)}, f32[2304]{0:T(1024)S(1)}, f32[2304]{0:T(1024)S(1)}) all-reduce(f32[2304]{0:T(1024)S(1)} %get-tuple-element.64, f32[2304]{0:T(1024)S(1)} %copy-done.33, f32[2304]{0:T(1024)S(1)} %copy-done.32, ...), channel_id=6, replica_groups=mesh['dp'=4,'ctx'=4,'tensor'=2] {'dp','ctx'}, use_global_device_ids=true, to_apply=%region_18.19.clone | all-reduce | flops 9216 | bytes 73728
  3300.2 26.5 reduce-scatter.20.cloned.1.call-done
  3328.5 52.6 %reduce-scatter.26.cloned.1.call-done = bf16[4608,144]{0,1:T(8,128)(2,1)} async-done(((bf16[4608,576]{0,1:T(8,128)(2,1)}), bf16[4608,144]{0,1:T(8,128)(2,1)}) %reduce-scatter.26.cloned.1.call-update) | async-done | bytes 1327120 | tf_op jit(solution)/shard_map/reduce_scatter | solution.py:229
  3384.2 51.5 %reduce-scatter.22.cloned.1.call-done = bf16[144,4608]{1,0:T(8,128)(2,1)} async-done(((bf16[576,4608]{1,0:T(8,128)(2,1)}), bf16[144,4608]{1,0:T(8,128)(2,1)}) %reduce-scatter.22.cloned.1.call-update) | async-done | bytes 1327120 | tf_op jit(solution)/shard_map/reduce_scatter | solution.py:217
  3438.8 51.2 %reduce-scatter.24.cloned.1.call-done = bf16[144,4608]{1,0:T(8,128)(2,1)} async-done(((bf16[576,4608]{1,0:T(8,128)(2,1)}), bf16[144,4608]{1,0:T(8,128)(2,1)}) %reduce-scatter.24.cloned.1.call-update) | async-done | bytes 1327120 | tf_op jit(solution)/shard_map/reduce_scatter | solution.py:223
  (270 shorter events, 205.6 us)
Async XLA Ops:
  7.2 75.7 %all-gather.23.cloned.1.call-start = ((), (), s32[]{:S(2)}) async-start(), calls=%async_computation.9 | async-start | bytes 2506752 | tf_op jit(solution)/shard_map/all_gather | solution.py:120
  7.9 90.7 %all-gather.25.cloned.1.call-start = ((), (), s32[]{:S(2)}) async-start(), calls=%async_computation.10 | async-start | bytes 2506752 | tf_op jit(solution)/shard_map/all_gather | solution.py:119
  8.7 136.9 %all-gather.59.cloned.1.call-start = ((), (), s32[]{:S(2)}) async-start(), calls=%async_computation.40 | async-start | bytes 2621440 | tf_op jit(solution)/shard_map/all_gather | solution.py:141
  78.0 128.4 %copy-start.30 = (f32[2304]{0:T(1024)}, f32[2304]{0:T(1024)S(1)}, u32[]{:S(2)}) copy-start(f32[2304]{0:T(1024)S(1)} %convert_element_type.190) | copy-start | bytes 27652
  80.3 126.2 %copy-start.35 = (f32[512]{0:T(512)}, f32[512]{0:T(512)S(1)}, u32[]{:S(2)}) copy-start(f32[512]{0:T(512)S(1)} %fusion.65) | copy-start | bytes 6148
  88.1 111.7 %all-gather.29.cloned.1.call-start = ((), (), s32[]{:S(2)}) async-start(), calls=%async_computation.12 | async-start | bytes 5013504 | tf_op jit(solution)/shard_map/all_gather | solution.py:118
  88.7 157.6 %all-gather.27.cloned.1.call-start = ((), (), s32[]{:S(2)}) async-start(), calls=%async_computation.11 | async-start | bytes 2621440 | tf_op jit(solution)/shard_map/all_gather | solution.py:140
  89.9 121.4 %copy-start.14 = (f32[512,128]{0,1:T(8,128)}, f32[512,128]{0,1:T(8,128)S(1)}, u32[]{:S(2)}) copy-start(f32[512,128]{0,1:T(8,128)S(1)} %get-tuple-element.89) | copy-start | bytes 786436
  89.9 121.4 %copy-start.16 = (f32[512,128]{0,1:T(8,128)}, f32[512,128]{0,1:T(8,128)S(1)}, u32[]{:S(2)}) copy-start(f32[512,128]{0,1:T(8,128)S(1)} %get-tuple-element.90) | copy-start | bytes 786436
  107.1 193.4 %all-gather.31.cloned.1.call-start = ((), (), s32[]{:S(2)}) async-start(), calls=%async_computation.13 | async-start | bytes 5013504 | tf_op jit(solution)/shard_map/all_gather | solution.py:121
  107.7 317.5 %all-reduce.15.cloned.1.call-start = ((), (), s32[]{:S(2)}) async-start(), calls=%async_computation.14 | async-start | bytes 9437184 | tf_op jit(solution)/shard_map/psum | solution.py:159
  307.3 235.6 %all-gather.33.cloned.1.call-start = ((), (), s32[]{:S(2)}) async-start(), calls=%async_computation.15 | async-start | bytes 22560768 | tf_op jit(solution)/shard_map/all_gather | solution.py:164
  308.0 352.6 %all-gather.35.cloned.1.call-start = ((), (), s32[]{:S(2)}) async-start(), calls=%async_computation.16 | async-start | bytes 22560768 | tf_op jit(solution)/shard_map/all_gather | solution.py:165
  308.8 469.4 %all-gather.37.cloned.1.call-start = ((), (), s32[]{:S(2)}) async-start(), calls=%async_computation.17 | async-start | bytes 22560768 | tf_op jit(solution)/shard_map/all_gather | solution.py:166
  309.4 605.2 %all-reduce.17.cloned.1.call-start = ((), (), s32[]{:S(2)}) async-start(), calls=%async_computation.18 | async-start | bytes 9437184 | tf_op jit(solution)/shard_map/psum | solution.py:173
  309.4 120.7 %copy-start.26 = (f32[2304]{0:T(1024)}, f32[2304]{0:T(1024)S(1)}, u32[]{:S(2)}) copy-start(f32[2304]{0:T(1024)S(1)} %convert_element_type.200) | copy-start | bytes 27652
  309.4 121.2 %copy-start.28 = (f32[2304]{0:T(1024)}, f32[2304]{0:T(1024)S(1)}, u32[]{:S(2)}) copy-start(f32[2304]{0:T(1024)S(1)} %convert_element_type.201) | copy-start | bytes 27652
  430.7 130.1 %copy-start.41 = (f32[512]{0:T(512)}, f32[512]{0:T(512)S(1)}, u32[]{:S(2)}) copy-start(f32[512]{0:T(512)S(1)} %fusion.67) | copy-start | bytes 6148
  432.8 227.8 %copy-start.10 = (bf16[512,2304]{1,0:T(8,128)(2,1)}, bf16[512,2304]{1,0:T(8,128)(2,1)S(1)}, u32[]{:S(2)}) copy-start(bf16[512,2304]{1,0:T(8,128)(2,1)S(1)} %multiply_convert_fusion.2) | copy-start | bytes 7077892
  795.2 122.3 %copy-start.6 = (bf16[1,512,2304]{2,1,0:T(8,128)(2,1)S(1)}, bf16[1,512,2304]{2,1,0:T(8,128)(2,1)}, u32[]{:S(2)}) copy-start(bf16[1,512,2304]{2,1,0:T(8,128)(2,1)} %param.27) | copy-start | bytes 7077892
  795.2 311.8 %all-reduce.19.cloned.1.call-start = ((), (), s32[]{:S(2)}) async-start(), calls=%async_computation.19 | async-start | bytes 9437184 | tf_op jit(solution)/shard_map/psum | solution.py:203
  987.7 119.4 %copy-start.29 = (f32[2304]{0:T(1024)S(1)}, f32[2304]{0:T(1024)}, u32[]{:S(2)}) copy-start(f32[2304]{0:T(1024)} %copy-done.28) | copy-start | bytes 27652
  987.7 119.4 %copy-start.42 = (f32[512]{0:T(512)S(1)}, f32[512]{0:T(512)}, u32[]{:S(2)}) copy-start(f32[512]{0:T(512)} %copy-done.41) | copy-start | bytes 6148
  987.7 223.2 %reduce-scatter.10.cloned.1.call-start = ((), (), s32[]{:S(2)}) async-start(), calls=%async_computation.20 | async-start | bytes 2621440 | tf_op jit(solution)/shard_map/reduce_scatter | solution.py:276
  988.4 124.4 %copy-start.46 = (f32[512]{0:T(512)S(1)}, f32[512]{0:T(512)}, u32[]{:S(2)}) copy-start(f32[512]{0:T(512)} %copy-done.45) | copy-start | bytes 6148
  988.4 124.4 %copy-start.27 = (f32[2304]{0:T(1024)S(1)}, f32[2304]{0:T(1024)}, u32[]{:S(2)}) copy-start(f32[2304]{0:T(1024)} %copy-done.26) | copy-start | bytes 27652
  988.4 124.4 %copy-start.40 = (f32[512]{0:T(512)S(1)}, f32[512]{0:T(512)}, u32[]{:S(2)}) copy-start(f32[512]{0:T(512)} %copy-done.39) | copy-start | bytes 6148
  1166.9 89.4 %reduce-scatter.12.cloned.1.call-start = ((), (), s32[]{:S(2)}) async-start(), calls=%async_computation.21 | async-start | bytes 2621440 | tf_op jit(solution)/shard_map/reduce_scatter | solution.py:279
  1174.5 250.1 %all-gather.39.cloned.1.call-start = ((), (), s32[]{:S(2)}) async-start(), calls=%async_computation.23 | async-start | bytes 11796480 | tf_op jit(solution)/shard_map/all_gather | solution.py:305
  1175.1 295.7 %all-gather.43.cloned.1.call-start = ((), (), s32[]{:S(2)}) async-start(), calls=%async_computation.26 | async-start | bytes 2621440 | tf_op jit(solution)/shard_map/all_gather | solution.py:307
  1213.2 303.7 %all-gather.61.cloned.1.call-start = ((), (), s32[]{:S(2)}) async-start(), calls=%async_computation.41 | async-start | bytes 2621440 | tf_op jit(solution)/shard_map/all_gather | solution.py:308
  1256.3 341.6 %all-gather.41.cloned.1.call-start = ((), (), s32[]{:S(2)}) async-start(), calls=%async_computation.24 | async-start | bytes 5242880 | tf_op jit(solution)/shard_map/all_gather | solution.py:306
  1263.6 502.0 %all-gather.57.cloned.1.call-start = ((), (), s32[]{:S(2)}) async-start(), calls=%async_computation.38 | async-start | bytes 11796480 | tf_op jit(solution)/shard_map/all_gather | solution.py:213
  1264.3 667.7 %all-gather.47.cloned.1.call-start = ((), (), s32[]{:S(2)}) async-start(), calls=%async_computation.30 | async-start | bytes 11796480 | tf_op jit(solution)/shard_map/all_gather | solution.py:310
  1264.9 747.7 %all-gather.45.cloned.1.call-start = ((), (), s32[]{:S(2)}) async-start(), calls=%async_computation.29 | async-start | bytes 5242880 | tf_op jit(solution)/shard_map/all_gather | solution.py:309
  1265.6 1070.4 %all-gather.55.cloned.1.call-start = ((), (), s32[]{:S(2)}) async-start(), calls=%async_computation.37 | async-start | bytes 23592960 | tf_op jit(solution)/shard_map/all_gather | solution.py:212
  1266.4 1237.0 %all-gather.49.cloned.1.call-start = ((), (), s32[]{:S(2)}) async-start(), calls=%async_computation.32 | async-start | bytes 11796480 | tf_op jit(solution)/shard_map/all_gather | solution.py:209
  1267.1 1558.6 %all-gather.51.cloned.1.call-start = ((), (), s32[]{:S(2)}) async-start(), calls=%async_computation.33 | async-start | bytes 23592960 | tf_op jit(solution)/shard_map/all_gather | solution.py:210
  1267.7 1881.1 %all-gather.53.cloned.1.call-start = ((), (), s32[]{:S(2)}) async-start(), calls=%async_computation.35 | async-start | bytes 23592960 | tf_op jit(solution)/shard_map/all_gather | solution.py:211
  1268.5 1950.7 %all-reduce.21.cloned.1.call-start = ((), (), s32[]{:S(2)}) async-start(), calls=%async_computation.22 | async-start | bytes 4718592 | tf_op jit(solution)/shard_map/psum | solution.py:294
  1279.2 2014.8 %reduce-scatter.16.cloned.1.call-start = ((), (), s32[]{:S(2)}) async-start(), calls=%async_computation.27 | async-start | bytes 737280 | tf_op jit(solution)/shard_map/reduce_scatter | solution.py:320
  1474.6 1821.1 %reduce-scatter.18.cloned.1.call-start = ((), (), s32[]{:S(2)}) async-start(), calls=%async_computation.28 | async-start | bytes 737280 | tf_op jit(solution)/shard_map/reduce_scatter | solution.py:326
  1520.8 1777.6 %reduce-scatter.14.cloned.1.call-start = ((), (), s32[]{:S(2)}) async-start(), calls=%async_computation.25 | async-start | bytes 1474560 | tf_op jit(solution)/shard_map/reduce_scatter | solution.py:314
  1603.8 1722.9 %reduce-scatter.20.cloned.1.call-start = ((), (), s32[]{:S(2)}) async-start(), calls=%async_computation.31 | async-start | bytes 1474560 | tf_op jit(solution)/shard_map/reduce_scatter | solution.py:332
  2019.3 1361.8 %reduce-scatter.26.cloned.1.call-start = ((), (), s32[]{:S(2)}) async-start(), calls=%async_computation.39 | async-start | bytes 6635520 | tf_op jit(solution)/shard_map/reduce_scatter | solution.py:229
  2352.6 1083.1 %reduce-scatter.22.cloned.1.call-start = ((), (), s32[]{:S(2)}) async-start(), calls=%async_computation.34 | async-start | bytes 6635520 | tf_op jit(solution)/shard_map/reduce_scatter | solution.py:217
  2842.2 647.8 %reduce-scatter.24.cloned.1.call-start = ((), (), s32[]{:S(2)}) async-start(), calls=%async_computation.36 | async-start | bytes 6635520 | tf_op jit(solution)/shard_map/reduce_scatter | solution.py:223
  3165.4 121.8 %copy-start.48 = (f32[512]{0:T(512)S(1)}, f32[512]{0:T(512)}, u32[]{:S(2)}) copy-start(f32[512]{0:T(512)} %copy-done.47) | copy-start | bytes 6148
  (38 other events, 728.1 us)
Sparse Core Ops, SparseCore 0:
  10.3 44.9 all-gather.22
  57.6 40.9 all-gather.24
  100.8 44.7 all-gather.58
  147.7 52.0 all-gather.28
  201.8 44.4 all-gather.26
  248.5 52.0 all-gather.30
  307.4 117.7 all-reduce.14
  426.8 116.0 all-gather.32
  544.5 116.0 all-gather.34
  662.1 116.0 all-gather.36
  795.4 119.1 all-reduce.16
  987.8 119.2 all-reduce.18
  1167.0 43.8 reduce-scatter.9
  1213.1 43.1 reduce-scatter.11
  1258.4 166.0 all-gather.38
  1426.6 44.1 all-gather.42
  1472.3 44.6 all-gather.60
  1518.4 79.4 all-gather.40
  1600.2 165.2 all-gather.56
  1767.0 164.9 all-gather.46
  1933.7 78.9 all-gather.44
  2014.9 321.1 all-gather.54
  2337.7 165.6 all-gather.48
  2504.9 320.7 all-gather.50
  2827.4 321.4 all-gather.52
  3151.7 67.4 all-reduce.20
  3222.1 22.1 reduce-scatter.15
  3247.3 22.0 reduce-scatter.17
  3272.5 25.7 reduce-scatter.13
  3300.9 25.7 reduce-scatter.19
  3329.3 51.8 reduce-scatter.25
  3383.9 51.7 reduce-scatter.21
  3438.1 51.8 reduce-scatter.23
where the time goes:
time: 3510 us; the launch traced here: 3500 us
  waiting for transfers between devices  2890 us (82%)
  matrix products  288 us (8%)
  blocking collectives  126 us (4%)
  local copies, waits for them, and re-layouts  98.6 us (3%)
  other arithmetic  74.2 us (2%)
    all_gather x1, waiting for transfers between devices, body(): mixed_piece = lax.all_gather(mixed, 'ctx', axis=0, tiled=True)  316 us
    all_gather x1, waiting for transfers between devices, body(): gate_piece = lax.all_gather(d_gate, 'ctx', axis=0, tiled=True)  307 us
    all_gather x1, waiting for transfers between devices, body(): upward_piece = lax.all_gather(d_upward, 'ctx', axis=0, tiled=True)  306 us
    all_gather x1, waiting for transfers between devices, body(): out_piece = lax.all_gather(d_feed_low, 'ctx', axis=0, tiled=True)  162 us
    all_gather x1, waiting for transfers between devices, body(): out_piece = lax.all_gather(d_attend_low, 'ctx', axis=0, tiled=True)  152 us
    all_gather x1, waiting for transfers between devices, body(): feed_piece = lax.all_gather(feed_in, 'ctx', axis=0, tiled=True)  151 us
    dot_general x14, matrix products, contract(): lax.dot_general(left, right, (((left_dim,), (right_dim,)), ((), ())), pre...  149 us
    all_gather x1, waiting for transfers between devices, body(): in_piece = lax.all_gather(attend_in, 'ctx', axis=0, tiled=True)  145 us
  transfers between devices with their start and end apart: 33, of which 30 were waited for; matrix products, arithmetic and copies ran while one was open for 8% of the time, Pallas kernels for 0%

commit v1 on v0

v1 whole, which is shorter than its diff:
```python
import jax
import jax.numpy as jnp
from jax import lax
from jax.sharding import PartitionSpec as P

HQ = 8
KV = 4
HD = 256
LEN = 2048

epsilon = 1e-06
cap_value = 50.0
gelu_coef = 0.7978845608028654
masked_value = -1e30
cores = 2
pad_lanes = 128

f32 = jnp.float32
bf16 = jnp.bfloat16


def rms_norm(values, gain):
    factor = lax.rsqrt(jnp.mean(values * values, axis=-1, keepdims=True) + epsilon)
    return values * factor * gain


def gelu_tanh(values):
    return (
        0.5 * values * (1.0 + jnp.tanh(gelu_coef * (values + 0.044715 * values * values * values)))
    )


def gated_product(gate, upward):
    return gelu_tanh(gate) * upward


def rotary_tables(positions, head_size):
    half = head_size // 2
    freqs = 10000.0 ** (-(jnp.arange(half, dtype=f32) * 2.0) / head_size)
    angle = positions.astype(f32)[:, None] * freqs[None, :]
    return (jnp.cos(angle), jnp.sin(angle))


def rotate(values, cosine, sine):
    half = values.shape[-1] // 2
    first = values[..., :half]
    second = values[..., half:]
    cosine = cosine[:, None, :]
    sine = sine[:, None, :]
    return jnp.concatenate(
        [first * cosine - second * sine, second * cosine + first * sine], axis=-1
    )


def unrotate(grads, cosine, sine):
    half = grads.shape[-1] // 2
    first = grads[..., :half]
    second = grads[..., half:]
    cosine = cosine[:, None, :]
    sine = sine[:, None, :]
    return jnp.concatenate(
        [first * cosine + second * sine, second * cosine - first * sine], axis=-1
    )


def attend_probs(raw, visible):
    capped = cap_value * jnp.tanh(raw / cap_value)
    capped = jnp.where(visible, capped, masked_value)
    return jax.nn.softmax(capped, axis=-1)


def contract(left, right, left_dim, right_dim):
    return lax.dot_general(
        left, right, (((left_dim,), (right_dim,)), ((), ())), preferred_element_type=f32
    )


def body(
    layer_input,
    block_order,
    pre_attend,
    query_weight,
    key_weight,
    value_weight,
    output_weight,
    post_attend,
    pre_feed,
    gate_weight,
    up_weight,
    down_weight,
    post_feed,
    cotangent,
):
    _, rows, width = layer_input.shape
    block_len = LEN // block_order.shape[1]
    per_group = HQ // KV
    tensor_count = lax.axis_size("tensor")
    groups = KV // tensor_count
    factor = HD ** (-0.5)
    dp_count = lax.axis_size("dp")
    ctx_count = lax.axis_size("ctx")
    tensor_index = lax.axis_index("tensor")
    ctx_index = lax.axis_index("ctx")
    dp_index = lax.axis_index("dp")
    y_count = dp_count // cores
    y_index = dp_index // cores
    core_index = dp_index % cores
    share = width // (dp_count * ctx_count)
    quarter = share * ctx_count
    half = rows // tensor_count
    x_swap = [(0, 1), (1, 0)]

    def relative(values):
        first, second = values[:half], values[half:]
        flip = tensor_index == 1
        return jnp.concatenate(
            [jnp.where(flip, second, first), jnp.where(flip, first, second)], axis=0
        )

    def join(own):
        return jnp.concatenate([own, lax.ppermute(own, "tensor", x_swap)], axis=0)

    def join_absolute(own):
        return relative(join(own))

    def sum_half(left, right, left_dim, right_dim):
        other = contract(left[half:], right, left_dim, right_dim).astype(bf16)
        got = lax.ppermute(other, "tensor", x_swap)
        return contract(left[:half], right, left_dim, right_dim) + got.astype(f32)

    all_pos = (
        block_order[0][:, None] * block_len + jnp.arange(block_len, dtype=jnp.int32)[None, :]
    ).reshape(ctx_count, tensor_count, half)
    all_pos = jnp.where(tensor_index == 1, all_pos[:, ::-1], all_pos).reshape(ctx_count, rows)
    source = (ctx_index - jnp.arange(ctx_count, dtype=jnp.int32)) % ctx_count
    key_pos = jnp.take(all_pos, source, axis=0)
    local_pos = key_pos[0]
    key_pos = key_pos.reshape(LEN)
    cosine, sine = rotary_tables(local_pos, HD)
    visible = local_pos[:, None] >= key_pos[None, :]

    gain_pack = jnp.stack([pre_attend, post_attend, pre_feed, post_feed], axis=1)
    gain_pack = jnp.pad(gain_pack, ((0, 0), (0, pad_lanes - 4)))
    first_pack = jnp.concatenate([query_weight, key_weight, value_weight, gain_pack], axis=1)
    both = ("dp", "ctx")
    first_all = lax.all_gather(first_pack, both, axis=0, tiled=True)
    out_mat = lax.all_gather(output_weight.T, both, axis=0, tiled=True)
    gate_mat = lax.all_gather(gate_weight, both, axis=0, tiled=True)
    up_mat = lax.all_gather(up_weight, both, axis=0, tiled=True)
    down_mat = lax.all_gather(down_weight.T, both, axis=0, tiled=True)

    query_width = query_weight.shape[1]
    key_width = key_weight.shape[1]
    attend_width = query_width + 2 * key_width
    attend_mat = first_all[:, :attend_width]
    gains = first_all[:, attend_width : attend_width + 8].T.astype(f32)
    gain_in, gain_out, feed_gain, feed_post = gains[0], gains[1], gains[2], gains[3]

    inputs = relative(layer_input[0].astype(f32))
    own_inputs = inputs[:half]
    cot = lax.dynamic_slice_in_dim(cotangent[0], tensor_index * half, half, 0).astype(f32)

    attend_in = rms_norm(inputs, gain_in).astype(bf16)
    projected = jnp.dot(attend_in, attend_mat, preferred_element_type=f32)
    query_pre = projected[:, :query_width]
    key_pre = projected[:, query_width : query_width + key_width]
    value_pre = projected[:, query_width + key_width :]
    keys_local = (
        rotate(key_pre.reshape(rows, groups, HD), cosine, sine).astype(bf16).reshape(rows, -1)
    )
    values_local = value_pre.astype(bf16)
    kv_local = jnp.concatenate([keys_local, values_local], axis=1)
    kv_parts = [kv_local]
    for step in range(1, ctx_count):
        pairs = [(i, (i + step) % ctx_count) for i in range(ctx_count)]
        kv_parts.append(lax.ppermute(kv_local, "ctx", pairs))
    kv_all = jnp.concatenate(kv_parts, axis=0)
    key_heads = kv_all[:, :key_width].reshape(LEN, groups, HD)
    value_heads = kv_all[:, key_width:].reshape(LEN, groups, HD)
    queries = (
        rotate(query_pre.reshape(rows, -1, HD), cosine, sine)
        .astype(bf16)
        .reshape(rows, groups, per_group, HD)
    )

    raw = (
        jnp.einsum("qgrd,kgd->grqk", queries, key_heads, preferred_element_type=f32) * factor
    )
    probs, prob_back = jax.vjp(lambda inner: attend_probs(inner, visible), raw)
    probs_low = probs.astype(bf16)
    attended = (
        jnp.einsum("grqk,kgd->qgrd", probs_low, value_heads, preferred_element_type=f32)
        .astype(bf16)
        .reshape(rows, -1)
    )
    attend_out = sum_half(attended, out_mat, 1, 1)
    hidden_mid = own_inputs + rms_norm(attend_out, gain_out)
    feed_in = join(rms_norm(hidden_mid, feed_gain).astype(bf16))
    gate = jnp.dot(feed_in, gate_mat, preferred_element_type=f32)
    upward = jnp.dot(feed_in, up_mat, preferred_element_type=f32)
    mixed = gated_product(gate, upward).astype(bf16)
    feed_out = sum_half(mixed, down_mat, 1, 1)
    layer_output = join_absolute(
        (hidden_mid + rms_norm(feed_out, feed_post)).astype(bf16)
    )[None]

    def pick(matrix, dy, dc):
        index = ((y_index + dy) % y_count) * cores + (core_index + dc) % cores
        return lax.dynamic_slice_in_dim(matrix, index * quarter, quarter, 1)

    def along(dy, dc):
        pairs = []
        for y in range(y_count):
            for core in range(cores):
                target = ((y + dy) % y_count) * cores + (core + dc) % cores
                pairs.append((y * cores + core, target))
        return pairs

    def reduce_rows(left, right, extra=None):
        def piece(dy, dc):
            result = contract(pick(left, dy, dc), right, 0, 0)
            if extra is not None:
                result = jnp.concatenate([result, pick(extra, dy, dc).T], axis=1)
            return result

        swapped = [
            lax.ppermute(piece(dy, 1).astype(bf16), "dp", along(0, 1)) for dy in range(y_count)
        ]
        total = piece(0, 0) + swapped[0].astype(f32)
        arrived = []
        for dy in range(1, y_count):
            partial = (piece(dy, 0) + swapped[dy].astype(f32)).astype(bf16)
            arrived.append(lax.ppermute(partial, "dp", along(dy, 0)))
        for item in arrived:
            total = total + item.astype(f32)
        return lax.psum_scatter(
            total.astype(bf16), "ctx", scatter_dimension=0, tiled=True
        ).astype(f32)

    def norm_back(values, gain, incoming):
        _, back = jax.vjp(rms_norm, values, gain)
        return back(incoming)

    d_feed_out, post_feed_part = norm_back(feed_out, feed_post, cot)
    d_feed_low = join(d_feed_out.astype(bf16))
    down_grad = reduce_rows(d_feed_low, mixed).T
    d_mixed = jnp.dot(d_feed_low, down_mat, preferred_element_type=f32)
    _, gate_back = jax.vjp(gated_product, gate, upward)
    d_gate, d_upward = gate_back(d_mixed)
    d_gate = d_gate.astype(bf16)
    d_upward = d_upward.astype(bf16)

    other = (
        contract(d_gate[half:], gate_mat, 1, 1) + contract(d_upward[half:], up_mat, 1, 1)
    ).astype(bf16)
    got = lax.ppermute(other, "tensor", x_swap)
    d_feed_in = (
        contract(d_gate[:half], gate_mat, 1, 1)
        + contract(d_upward[:half], up_mat, 1, 1)
        + got.astype(f32)
    )
    gate_grad = reduce_rows(feed_in, d_gate)
    up_grad = reduce_rows(feed_in, d_upward)

    d_from_feed, pre_feed_part = norm_back(hidden_mid, feed_gain, d_feed_in)
    d_mid = cot + d_from_feed
    d_attend_out, post_attend_part = norm_back(attend_out, gain_out, d_mid)
    d_attend_low = join(d_attend_out.astype(bf16))
    d_attended = (
        jnp.dot(d_attend_low, out_mat, preferred_element_type=f32)
        .astype(bf16)
        .reshape(rows, groups, per_group, HD)
    )
    d_probs = jnp.einsum("qgrd,kgd->grqk", d_attended, value_heads, preferred_element_type=f32)
    d_raw = prob_back(d_probs)[0].astype(bf16)
    d_query = jnp.einsum("grqk,kgd->qgrd", d_raw, key_heads, preferred_element_type=f32) * factor
    d_key = jnp.einsum("grqk,qgrd->kgd", d_raw, queries, preferred_element_type=f32) * factor
    d_value = jnp.einsum("grqk,qgrd->kgd", probs_low, d_attended, preferred_element_type=f32)
    d_kv = jnp.concatenate([d_key.reshape(LEN, -1), d_value.reshape(LEN, -1)], axis=1)
    d_kv_local = d_kv[:rows]
    for step in range(1, ctx_count):
        pairs = [(i, (i - step) % ctx_count) for i in range(ctx_count)]
        sent = d_kv[step * rows : (step + 1) * rows].astype(bf16)
        d_kv_local = d_kv_local + lax.ppermute(sent, "ctx", pairs).astype(f32)
    d_query_pre = (
        unrotate(d_query.reshape(rows, -1, HD), cosine, sine).reshape(rows, -1).astype(bf16)
    )
    d_key_pre = (
        unrotate(d_kv_local[:, :key_width].reshape(rows, groups, HD), cosine, sine)
        .reshape(rows, -1)
        .astype(bf16)
    )
    d_value_pre = d_kv_local[:, key_width:].astype(bf16)
    d_projected = jnp.concatenate([d_query_pre, d_key_pre, d_value_pre], axis=1)
    d_attend_part = contract(d_projected, attend_mat, 1, 1)

    in_factor = lax.rsqrt(jnp.mean(inputs * inputs, axis=-1, keepdims=True) + epsilon)
    pre_attend_part = jnp.sum(d_attend_part * inputs * in_factor, axis=0)
    gain_parts = jnp.stack([pre_attend_part, post_attend_part, pre_feed_part, post_feed_part])
    gain_parts = jnp.pad(gain_parts, ((0, pad_lanes - 4), (0, 0)))

    out_grad = reduce_rows(d_attend_low, attended).T
    attend_grad = reduce_rows(attend_in, d_projected, gain_parts)
    query_grad = attend_grad[:, :query_width]
    key_grad = attend_grad[:, query_width : query_width + key_width]
    value_grad = attend_grad[:, query_width + key_width : attend_width]
    gain_grads = attend_grad[:, attend_width:]
    gain_grads = (gain_grads + lax.ppermute(gain_grads, "tensor", x_swap)).T

    got = lax.ppermute(d_attend_part[half:].astype(bf16), "tensor", x_swap)
    d_attend_in = d_attend_part[:half] + got.astype(f32)
    d_from_attend, _ = norm_back(own_inputs, gain_in, d_attend_in)
    input_grad = join_absolute((d_mid + d_from_attend).astype(bf16)).astype(f32)[None]

    return (
        layer_output,
        input_grad,
        gain_grads[0],
        query_grad,
        key_grad,
        value_grad,
        out_grad,
        gain_grads[1],
        gain_grads[2],
        gate_grad,
        up_grad,
        down_grad,
        gain_grads[3],
    )


def solution(mesh):
    both = ("dp", "ctx")
    return jax.shard_map(
        body,
        mesh=mesh,
        in_specs=(
            P("dp", "ctx", None),
            P("dp", None),
            P(both),
            P(both, "tensor"),
            P(both, "tensor"),
            P(both, "tensor"),
            P("tensor", both),
            P(both),
            P(both),
            P(both, "tensor"),
            P(both, "tensor"),
            P("tensor", both),
            P(both),
            P("dp", "ctx", None),
        ),
        out_specs=(
            P("dp", "ctx", None),
            P("dp", "ctx", None),
            P(both),
            P(both, "tensor"),
            P(both, "tensor"),
            P(both, "tensor"),
            P("tensor", both),
            P(both),
            P(both),
            P(both, "tensor"),
            P(both, "tensor"),
            P("tensor", both),
            P(both),
        ),
        check_vma=False,
    )
```

time: 3510 us -> 1590 us (0.45)
  waiting for transfers between devices: 2890 us -> 1010 us
  blocking collectives: 126 us -> 0 us
  matrix products: 288 us -> 340 us
  other arithmetic: 74.2 us -> 111 us
    all_gather x20 -> x5, waiting for transfers between devices: 2220 us -> 259 us  [the longest x1 96.8 us: body(): down_mat = lax.all_gather(down_weight.T, both, axis=0, tiled=True)]
    ppermute x0 -> x31, waiting for transfers between devices: none -> 727 us  [the longest x5 371 us: reduce_rows(): arrived.append(lax.ppermute(partial, 'dp', along(dy, 0)))]
    psum x4 -> x0, waiting for transfers between devices: 407 us -> none  [the longest x1 119 us: body(): lax.psum(jnp.dot(mixed, down_mat, preferred_element_type=jnp.float32), 't...]
    reduce_scatter x9 -> x5, waiting for transfers between devices: 262 us -> 19.7 us  [reduce_rows(): lax.psum_scatter(total.astype(bf16), 'ctx', scatter_dimension=0, tiled=True)]
    unnamed x2 -> x0, blocking collectives: 126 us -> none
    all_gather x4 -> x0, local copies, waits for them, and re-layouts: 51.5 us -> none  [the longest x1 13 us: body(): feed_piece = lax.all_gather(feed_in, 'ctx', axis=0, tiled=True)]
    dot_general x14 -> x29, matrix products: 149 us -> 196 us  [contract(): lax.dot_general(left, right, (((left_dim,), (right_dim,)), ((), ())), pre...]
    dot_general x13 -> x11, matrix products: 126 us -> 130 us  [the longest x1 25.4 us: body(): d_mixed = jnp.dot(d_feed_low, down_mat, preferred_element_type=f32)]
  transfers between devices with their start and end apart: 33 -> 41, of which waited for: 30 -> 22; matrix products, arithmetic and copies ran while one was open for 8% -> 25% of each run, Pallas kernels for 0% -> 0%
where the time goes in v1:
time: 1590 us; the launch traced here: 1580 us
  waiting for transfers between devices  1010 us (64%)
  matrix products  340 us (21%)
  other arithmetic  111 us (7%)
  local copies, waits for them, and re-layouts  70.9 us (4%)
  starting transfers between devices  34.3 us (2%)
    ppermute x5, waiting for transfers between devices, reduce_rows(): arrived.append(lax.ppermute(partial, 'dp', along(dy, 0)))  371 us
    dot_general x29, matrix products, contract(): lax.dot_general(left, right, (((left_dim,), (right_dim,)), ((), ())), pre...  196 us
    ppermute x3, waiting for transfers between devices, body(): kv_parts.append(lax.ppermute(kv_local, 'ctx', pairs))  109 us
    ppermute x5, waiting for transfers between devices, join(): return jnp.concatenate([own, lax.ppermute(own, 'tensor', x_swap)], axis=0)  104 us
    all_gather x1, waiting for transfers between devices, body(): down_mat = lax.all_gather(down_weight.T, both, axis=0, tiled=True)  96.8 us
    all_gather x1, waiting for transfers between devices, body(): up_mat = lax.all_gather(up_weight, both, axis=0, tiled=True)  85.9 us
    all_gather x1, waiting for transfers between devices, body(): first_all = lax.all_gather(first_pack, both, axis=0, tiled=True)  76.5 us
    ppermute x2, waiting for transfers between devices, sum_half(): got = lax.ppermute(other, 'tensor', x_swap)  52.3 us
  transfers between devices with their start and end apart: 41, of which 22 were waited for; matrix products, arithmetic and copies ran while one was open for 25% of the time, Pallas kernels for 0%

profile of v1, /device:TPU:0, one launch (start us, length us, event | category | flops | bytes accessed | tf_op | source)
XLA Modules:
  0.0 1580.3 jit_solution(11362400559725124565)
XLA Ops:
  23.5 76.5 %all-gather.6.cloned.1.call-done = bf16[2304,2176]{1,0:T(8,128)(2,1)} async-done(((bf16[144,2176]{1,0:T(8,128)(2,1)}), bf16[2304,2176]{1,0:T(8,128)(2,1)}) %all-gather.6.cloned.1.call-update) | async-done | bytes 10027024 | tf_op jit(solution)/shard_map/all_gather | solution.py:146
  103.9 8.6 fusion.23
  136.7 30.4 %collective-permute-done.2 = bf16[512,1024]{1,0:T(8,128)(2,1)} collective-permute-done((bf16[512,1024]{1,0:T(8,128)(2,1)}, bf16[512,1024]{1,0:T(8,128)(2,1)}, u32[]{:S(2)}, u32[]{:S(2)}) %collective-permute-start.2) | collective-permute-done | bytes 1048608 | tf_op jit(solution)/shard_map/ppermute | solution.py:176
  167.1 78.8 %collective-permute-done.1 = bf16[512,1024]{1,0:T(8,128)(2,1)} collective-permute-done((bf16[512,1024]{1,0:T(8,128)(2,1)}, bf16[512,1024]{1,0:T(8,128)(2,1)}, u32[]{:S(2)}, u32[]{:S(2)}) %collective-permute-start.1) | collective-permute-done | bytes 1048608 | tf_op jit(solution)/shard_map/ppermute | solution.py:176
  268.0 13.4 fusion.157
  281.4 7.5 divide_convert_fusion
  298.8 25.3 %collective-permute-done.3 = bf16[256,2304]{1,0:T(8,128)(2,1)S(1)} collective-permute-done((bf16[256,2304]{1,0:T(8,128)(2,1)S(1)}, bf16[256,2304]{1,0:T(8,128)(2,1)S(1)}, u32[]{:S(2)}, u32[]{:S(2)}) %collective-permute-start.3) | collective-permute-done | bytes 1179680 | tf_op jit(solution)/shard_map/ppermute | solution.py:128
  330.1 24.5 %collective-permute-done.4 = bf16[256,2304]{1,0:T(8,128)(2,1)S(1)} collective-permute-done((bf16[256,2304]{1,0:T(8,128)(2,1)S(1)}, bf16[256,2304]{1,0:T(8,128)(2,1)S(1)}, u32[]{:S(2)}, u32[]{:S(2)}) %collective-permute-start.4) | collective-permute-done | bytes 1179680 | tf_op jit(solution)/shard_map/ppermute | solution.py:121
  354.6 18.2 %fusion.58 = f32[512,4608]{1,0:T(8,128)} fusion(bf16[2304,4608]{1,0:T(8,128)(2,1)} %all-gather.10.cloned.1.call-done, bf16[256,2304]{1,0:T(8,128)(2,1)S(1)} %collective-permute-done.4, bf16[256,2304]{1,0:T(8,128)(2,1)S(1)} %multiply_convert_fusion.3), kind=kOutput, calls=%fused_computation.167 | convolution fusion | flops 10876354560 | bytes 33030144 | tf_op jit(solution)/shard_map/dot_general | solution.py:199
  372.8 85.9 %all-gather.12.cloned.1.call-done = bf16[2304,4608]{1,0:T(8,128)(2,1)} async-done(((bf16[144,4608]{1,0:T(8,128)(2,1)}), bf16[2304,4608]{1,0:T(8,128)(2,1)}) %all-gather.12.cloned.1.call-update) | async-done | bytes 21233680 | tf_op jit(solution)/shard_map/all_gather | solution.py:149
  458.7 20.7 %multiply_convert_fusion.1 = (bf16[512,4608]{1,0:T(8,128)(2,1)}, f32[512,4608]{1,0:T(8,128)}) fusion(f32[512,4608]{1,0:T(8,128)} %fusion.58, bf16[2304,4608]{1,0:T(8,128)(2,1)} %all-gather.12.cloned.1.call-done, bf16[256,2304]{1,0:T(8,128)(2,1)S(1)} %collective-permute-done.4, bf16[256,2304]{1,0:T(8,128)(2,1)S(1)} %multiply_convert_fusion.3), kind=kOutput, calls=%fused_computation.37 | convolution fusion | flops 10899947520 | bytes 47185920 | tf_op jit(solution)/shard_map/dot_general | solution.py:200
  479.4 96.8 %all-gather.14.cloned.1.call-done = bf16[2304,4608]{1,0:T(8,128)(2,1)} async-done(((bf16[144,4608]{1,0:T(8,128)(2,1)}), bf16[2304,4608]{1,0:T(8,128)(2,1)}) %all-gather.14.cloned.1.call-update) | async-done | bytes 21233680 | tf_op jit(solution)/shard_map/all_gather | solution.py:150
  576.2 12.0 convolution_convert_fusion.6
  589.7 27.0 %collective-permute-done.5 = bf16[256,2304]{1,0:T(8,128)(2,1)} collective-permute-done((bf16[256,2304]{1,0:T(8,128)(2,1)}, bf16[256,2304]{1,0:T(8,128)(2,1)}, u32[]{:S(2)}, u32[]{:S(2)}) %collective-permute-start.5) | collective-permute-done | bytes 1179680 | tf_op jit(solution)/shard_map/ppermute | solution.py:128
  616.6 11.7 multiply_reduce_fusion.8
  636.4 25.8 %collective-permute-done.7 = bf16[256,2304]{1,0:T(8,128)(2,1)S(1)} collective-permute-done((bf16[256,2304]{1,0:T(8,128)(2,1)S(1)}, bf16[256,2304]{1,0:T(8,128)(2,1)S(1)}, u32[]{:S(2)}, u32[]{:S(2)}) %collective-permute-start.7) | collective-permute-done | bytes 1179680 | tf_op jit(solution)/shard_map/ppermute | solution.py:121
  662.2 25.4 %multiply_convert_fusion = (bf16[512,4608]{1,0:T(8,128)(2,1)S(1)}, bf16[512,4608]{1,0:T(8,128)(2,1)}) fusion(f32[512,4608]{1,0:T(8,128)} %fusion.58, f32[512,4608]{1,0:T(8,128)} %get-tuple-element.76, bf16[2304,4608]{1,0:T(8,128)(2,1)} %all-gather.14.cloned.1.call-done, bf16[256,2304]{1,0:T(8,128)(2,1)S(1)} %collective-permute-done.7, ...), kind=kOutput, calls=%fused_computation.36 | convolution fusion | flops 10942414848 | bytes 51904512 | tf_op jit(solution)/shard_map/dot_general | solution.py:247
  687.6 13.9 fusion.41
  701.5 11.9 fusion.28
  714.8 12.2 fusion.44
  727.0 13.0 collective-permute-done.8
  740.0 14.2 multiply_reduce_fusion.2
  765.4 7.9 convolution_convert_fusion.4
  774.5 12.9 collective-permute-done.9
  795.2 8.0 fusion.158
  803.2 10.9 fusion.8
  814.1 18.3 %fusion.2 = bf16[2,2,512,2048]{2,3,1,0:T(8,128)(2,1)} fusion(f32[2,2,512,2048]{2,3,1,0:T(8,128)} %get-tuple-element.72, f32[2,2048,512,2]{2,1,3,0:T(8,128)} %get-tuple-element.81, f32[2,2,512]{2,1,0:T(2,128)S(1)} %neg.14, f32[2,2,512]{2,1,0:T(2,128)S(1)} %copy-done.77, pred[512,2048]{0,1:T(8,128)(4,1)S(1)} %copy-done.56, ...), kind=kOutput, calls=%fused_computation.4 | convolution fusion | flops 2199912448 | bytes 46153728 | tf_op jit(solution)/shard_map/qgrd,kgd->grqk/dot_general | solution.py:187
  864.8 9.0 collective-permute-done.12
  873.7 40.7 %collective-permute-done.11 = bf16[512,1024]{0,1:T(8,128)(2,1)} collective-permute-done((bf16[512,1024]{0,1:T(8,128)(2,1)}, bf16[512,1024]{0,1:T(8,128)(2,1)}, u32[]{:S(2)}, u32[]{:S(2)}) %collective-permute-start.11) | collective-permute-done | bytes 1048608 | tf_op jit(solution)/shard_map/ppermute | solution.py:284
  923.2 11.8 multiply_reduce_fusion
  943.5 7.9 convolution_convert_fusion.5
  974.7 20.9 %collective-permute-done.21 = bf16[576,1024]{1,0:T(8,128)(2,1)S(1)} collective-permute-done((bf16[576,1024]{1,0:T(8,128)(2,1)S(1)}, bf16[576,1024]{1,0:T(8,128)(2,1)S(1)}, u32[]{:S(2)}, u32[]{:S(2)}) %collective-permute-start.21) | collective-permute-done | bytes 1179680 | tf_op jit(solution)/shard_map/ppermute | solution.py:233
  997.6 9.7 add_convert_fusion.5
  1012.1 37.3 %collective-permute-done.17 = bf16[576,2176]{1,0:T(8,128)(2,1)} collective-permute-done((bf16[576,2176]{1,0:T(8,128)(2,1)}, bf16[576,2176]{1,0:T(8,128)(2,1)}, u32[]{:S(2)}, u32[]{:S(2)}) %collective-permute-start.17) | collective-permute-done | bytes 2506784 | tf_op jit(solution)/shard_map/ppermute | solution.py:233
  1054.3 7.9 convolution_convert_fusion.2
  1068.0 94.7 %collective-permute-done.24 = bf16[576,4608]{1,0:T(8,128)(2,1)} collective-permute-done((bf16[576,4608]{1,0:T(8,128)(2,1)}, bf16[576,4608]{1,0:T(8,128)(2,1)}, u32[]{:S(2)}, u32[]{:S(2)}) %collective-permute-start.24) | collective-permute-done | bytes 5308448 | tf_op jit(solution)/shard_map/ppermute | solution.py:233
  1162.6 8.0 add_convert_fusion.4
  1171.0 8.0 convolution_convert_fusion.3
  1179.1 9.6 add_convert_fusion.3
  1199.4 106.2 %collective-permute-done.27 = bf16[576,4608]{1,0:T(8,128)(2,1)S(1)} collective-permute-done((bf16[576,4608]{1,0:T(8,128)(2,1)}, bf16[576,4608]{1,0:T(8,128)(2,1)S(1)}, u32[]{:S(2)}, u32[]{:S(2)}) %collective-permute-start.27) | collective-permute-done | bytes 5308448 | tf_op jit(solution)/shard_map/ppermute | solution.py:233
  1305.6 6.8 add_convert_fusion.2
  1319.5 9.5 add_convert_fusion.1
  1333.9 112.1 %collective-permute-done.30 = bf16[576,4608]{1,0:T(8,128)(2,1)S(1)} collective-permute-done((bf16[576,4608]{1,0:T(8,128)(2,1)}, bf16[576,4608]{1,0:T(8,128)(2,1)S(1)}, u32[]{:S(2)}, u32[]{:S(2)}) %collective-permute-start.30) | collective-permute-done | bytes 5308448 | tf_op jit(solution)/shard_map/ppermute | solution.py:233
  1446.0 6.8 add_convert_fusion
  1456.8 26.8 %collective-permute-done.13 = bf16[256,2304]{1,0:T(8,128)(2,1)S(1)} collective-permute-done((bf16[256,2304]{1,0:T(8,128)(2,1)S(1)}, bf16[256,2304]{1,0:T(8,128)(2,1)S(1)}, u32[]{:S(2)}, u32[]{:S(2)}) %collective-permute-start.13) | collective-permute-done | bytes 1179680 | tf_op jit(solution)/shard_map/ppermute | solution.py:310
  1489.9 19.1 %collective-permute-done.6 = bf16[256,2304]{1,0:T(8,128)(2,1)S(1)} collective-permute-done((bf16[256,2304]{1,0:T(8,128)(2,1)S(1)}, bf16[256,2304]{1,0:T(8,128)(2,1)S(1)}, u32[]{:S(2)}, u32[]{:S(2)}) %collective-permute-start.6) | collective-permute-done | bytes 1179680 | tf_op jit(solution)/shard_map/ppermute | solution.py:121
  1510.7 22.2 %collective-permute-done.14 = bf16[256,2304]{1,0:T(8,128)(2,1)S(1)} collective-permute-done((bf16[256,2304]{1,0:T(8,128)(2,1)S(1)}, bf16[256,2304]{1,0:T(8,128)(2,1)S(1)}, u32[]{:S(2)}, u32[]{:S(2)}) %collective-permute-start.14) | collective-permute-done | bytes 1179680 | tf_op jit(solution)/shard_map/ppermute | solution.py:121
  1550.5 19.7 %reduce-scatter.14.cloned.1.call-done = bf16[144,4608]{1,0:T(8,128)(2,1)} async-done(((bf16[576,4608]{1,0:T(8,128)(2,1)}), bf16[144,4608]{1,0:T(8,128)(2,1)}) %reduce-scatter.14.cloned.1.call-update) | async-done | bytes 1327120 | tf_op jit(solution)/shard_map/reduce_scatter | solution.py:236
  (398 shorter events, 258.6 us)
Async XLA Ops:
  7.2 92.8 %all-gather.6.cloned.1.call-start = ((), (), s32[]{:S(2)}) async-start(), calls=%async_computation.5 | async-start | bytes 10653696 | tf_op jit(solution)/shard_map/all_gather | solution.py:146
  12.0 281.2 %all-gather.8.cloned.1.call-start = ((), (), s32[]{:S(2)}) async-start(), calls=%async_computation.6 | async-start | bytes 5013504 | tf_op jit(solution)/shard_map/all_gather | solution.py:147
  12.8 341.8 %all-gather.10.cloned.1.call-start = ((), (), s32[]{:S(2)}) async-start(), calls=%async_computation.7 | async-start | bytes 22560768 | tf_op jit(solution)/shard_map/all_gather | solution.py:148
  13.5 445.2 %all-gather.12.cloned.1.call-start = ((), (), s32[]{:S(2)}) async-start(), calls=%async_computation.8 | async-start | bytes 22560768 | tf_op jit(solution)/shard_map/all_gather | solution.py:149
  14.1 562.1 %all-gather.14.cloned.1.call-start = ((), (), s32[]{:S(2)}) async-start(), calls=%async_computation.9 | async-start | bytes 22560768 | tf_op jit(solution)/shard_map/all_gather | solution.py:150
  14.7 1520.9 %reduce-scatter.8.cloned.1.call-start = ((), (), s32[]{:S(2)}) async-start(), calls=%async_computation.11 | async-start | bytes 1474560 | tf_op jit(solution)/shard_map/reduce_scatter | solution.py:236
  21.0 304.8 %copy-start.2 = (f32[256,2304]{1,0:T(8,128)}, f32[256,2304]{1,0:T(8,128)S(1)}, u32[]{:S(2)}) copy-start(f32[256,2304]{1,0:T(8,128)S(1)} %get-tuple-element.35) | copy-start | bytes 7077892
  23.4 109.4 %copy-start.39 = (f32[512,128]{1,0:T(8,128)}, f32[512,128]{1,0:T(8,128)S(1)}, u32[]{:S(2)}) copy-start(f32[512,128]{1,0:T(8,128)S(1)} %get-tuple-element.67) | copy-start | bytes 786436
  23.4 109.3 %copy-start.41 = (f32[512,128]{1,0:T(8,128)}, f32[512,128]{1,0:T(8,128)S(1)}, u32[]{:S(2)}) copy-start(f32[512,128]{1,0:T(8,128)S(1)} %get-tuple-element.68) | copy-start | bytes 786436
  103.3 222.5 %copy-start.68 = (f32[2304]{0:T(1024)}, f32[2304]{0:T(1024)S(1)}, u32[]{:S(2)}) copy-start(f32[2304]{0:T(1024)S(1)} %get-tuple-element.23) | copy-start | bytes 27652
  103.4 223.9 %copy-start.72 = (f32[2304]{0:T(1024)}, f32[2304]{0:T(1024)S(1)}, u32[]{:S(2)}) copy-start(f32[2304]{0:T(1024)S(1)} %get-tuple-element.21) | copy-start | bytes 27652
  122.8 44.3 %collective-permute-start.2 = (bf16[512,1024]{1,0:T(8,128)(2,1)}, bf16[512,1024]{1,0:T(8,128)(2,1)}, u32[]{:S(2)}, u32[]{:S(2)}) collective-permute-start(bf16[512,1024]{1,0:T(8,128)(2,1)} %pad_maximum_fusion.15), channel_id=1, source_target_pairs={{0,6},{2,0},{4,2},{6,4},{1,7},{3,1},{5,3},{7,5},{8,14},{10,8},{12,... | collective-permute-start | bytes 3145736 | tf_op jit(solution)/shard_map/ppermute | solution.py:176
  124.2 121.7 %collective-permute-start.1 = (bf16[512,1024]{1,0:T(8,128)(2,1)}, bf16[512,1024]{1,0:T(8,128)(2,1)}, u32[]{:S(2)}, u32[]{:S(2)}) collective-permute-start(bf16[512,1024]{1,0:T(8,128)(2,1)} %pad_maximum_fusion.15), channel_id=1, source_target_pairs={{0,4},{2,6},{4,0},{6,2},{1,5},{3,7},{5,1},{7,3},{8,12},{10,14},{12... | collective-permute-start | bytes 3145736 | tf_op jit(solution)/shard_map/ppermute | solution.py:176
  124.8 121.1 %collective-permute-start = (bf16[512,1024]{1,0:T(8,128)(2,1)}, bf16[512,1024]{1,0:T(8,128)(2,1)}, u32[]{:S(2)}, u32[]{:S(2)}) collective-permute-start(bf16[512,1024]{1,0:T(8,128)(2,1)} %pad_maximum_fusion.15), channel_id=1, source_target_pairs={{0,2},{2,4},{4,6},{6,0},{1,3},{3,5},{5,7},{7,1},{8,10},{10,12},{12... | collective-permute-start | bytes 3145736 | tf_op jit(solution)/shard_map/ppermute | solution.py:176
  132.8 113.1 %copy-start.47 = (bf16[64,8,2,256]{3,1,2,0:T(8,128)(2,1)S(1)}, bf16[64,8,2,256]{3,1,2,0:T(8,128)(2,1)}, u32[]{:S(2)}) copy-start(bf16[64,8,2,256]{3,1,2,0:T(8,128)(2,1)} %copy-done.46) | copy-start | bytes 1572868
  297.3 26.8 %collective-permute-start.3 = (bf16[256,2304]{1,0:T(8,128)(2,1)S(1)}, bf16[256,2304]{1,0:T(8,128)(2,1)S(1)}, u32[]{:S(2)}, u32[]{:S(2)}) collective-permute-start(bf16[256,2304]{1,0:T(8,128)(2,1)S(1)} %convolution_convert_fusion.7), channel_id=1, source_target_pairs={{0,1},{1,0},{2,3},{3,2},{4,5},{5,4},{6,7},{7,6},{8,9},{9,8},{10,11... | collective-permute-start | bytes 3538952 | tf_op jit(solution)/shard_map/ppermute | solution.py:128
  328.6 130.1 %copy-start = (bf16[256,2304]{1,0:T(8,128)(2,1)}, bf16[256,2304]{1,0:T(8,128)(2,1)S(1)}, u32[]{:S(2)}) copy-start(bf16[256,2304]{1,0:T(8,128)(2,1)S(1)} %multiply_convert_fusion.3) | copy-start | bytes 3538948
  328.6 26.0 %collective-permute-start.4 = (bf16[256,2304]{1,0:T(8,128)(2,1)S(1)}, bf16[256,2304]{1,0:T(8,128)(2,1)S(1)}, u32[]{:S(2)}, u32[]{:S(2)}) collective-permute-start(bf16[256,2304]{1,0:T(8,128)(2,1)S(1)} %multiply_convert_fusion.3), channel_id=1, source_target_pairs={{0,1},{1,0},{2,3},{3,2},{4,5},{5,4},{6,7},{7,6},{8,9},{9,8},{10,11... | collective-permute-start | bytes 3538952 | tf_op jit(solution)/shard_map/ppermute | solution.py:121
  588.2 28.4 %collective-permute-start.5 = (bf16[256,2304]{1,0:T(8,128)(2,1)}, bf16[256,2304]{1,0:T(8,128)(2,1)}, u32[]{:S(2)}, u32[]{:S(2)}) collective-permute-start(bf16[256,2304]{1,0:T(8,128)(2,1)} %convolution_convert_fusion.6), channel_id=1, source_target_pairs={{0,1},{1,0},{2,3},{3,2},{4,5},{5,4},{6,7},{7,6},{8,9},{9,8},{10,11... | collective-permute-start | bytes 3538952 | tf_op jit(solution)/shard_map/ppermute | solution.py:128
  634.9 27.3 %collective-permute-start.7 = (bf16[256,2304]{1,0:T(8,128)(2,1)S(1)}, bf16[256,2304]{1,0:T(8,128)(2,1)S(1)}, u32[]{:S(2)}, u32[]{:S(2)}) collective-permute-start(bf16[256,2304]{1,0:T(8,128)(2,1)S(1)} %get-tuple-element.41), channel_id=1, source_target_pairs={{0,1},{1,0},{2,3},{3,2},{4,5},{5,4},{6,7},{7,6},{8,9},{9,8},{10,11... | collective-permute-start | bytes 3538952 | tf_op jit(solution)/shard_map/ppermute | solution.py:121
  713.4 26.7 %collective-permute-start.8 = (bf16[256,2304]{1,0:T(8,128)(2,1)}, bf16[256,2304]{1,0:T(8,128)(2,1)}, u32[]{:S(2)}, u32[]{:S(2)}) collective-permute-start(bf16[256,2304]{1,0:T(8,128)(2,1)} %fusion.28), channel_id=1, source_target_pairs={{0,1},{1,0},{2,3},{3,2},{4,5},{5,4},{6,7},{7,6},{8,9},{9,8},{10,11... | collective-permute-start | bytes 3538952 | tf_op jit(solution)/shard_map/ppermute | solution.py:256
  761.9 25.5 %collective-permute-start.9 = (bf16[256,2304]{1,0:T(8,128)(2,1)S(1)}, bf16[256,2304]{1,0:T(8,128)(2,1)}, u32[]{:S(2)}, u32[]{:S(2)}) collective-permute-start(bf16[256,2304]{1,0:T(8,128)(2,1)S(1)} %fusion.33), channel_id=1, source_target_pairs={{0,1},{1,0},{2,3},{3,2},{4,5},{5,4},{6,7},{7,6},{8,9},{9,8},{10,11... | collective-permute-start | bytes 3538952 | tf_op jit(solution)/shard_map/ppermute | solution.py:121
  773.3 224.4 %collective-permute-start.23 = (bf16[576,4608]{1,0:T(8,128)(2,1)}, bf16[576,4608]{1,0:T(8,128)(2,1)}, u32[]{:S(2)}, u32[]{:S(2)}) collective-permute-start(bf16[576,4608]{1,0:T(8,128)(2,1)} %convolution_convert_fusion.4), channel_id=1, source_target_pairs={{0,8},{8,0},{16,24},{24,16},{1,9},{9,1},{17,25},{25,17},{2,10},{10... | collective-permute-start | bytes 15925256 | tf_op jit(solution)/shard_map/ppermute | solution.py:227
  845.5 28.3 %collective-permute-start.12 = (bf16[512,1024]{0,1:T(8,128)(2,1)}, bf16[512,1024]{0,1:T(8,128)(2,1)}, u32[]{:S(2)}, u32[]{:S(2)}) collective-permute-start(bf16[512,1024]{0,1:T(8,128)(2,1)} %get-tuple-element.37), channel_id=1, source_target_pairs={{0,2},{2,4},{4,6},{6,0},{1,3},{3,5},{5,7},{7,1},{8,10},{10,12},{12... | collective-permute-start | bytes 3145736 | tf_op jit(solution)/shard_map/ppermute | solution.py:284
  845.5 68.9 %collective-permute-start.11 = (bf16[512,1024]{0,1:T(8,128)(2,1)}, bf16[512,1024]{0,1:T(8,128)(2,1)}, u32[]{:S(2)}, u32[]{:S(2)}) collective-permute-start(bf16[512,1024]{0,1:T(8,128)(2,1)} %get-tuple-element.38), channel_id=1, source_target_pairs={{0,4},{2,6},{4,0},{6,2},{1,5},{3,7},{5,1},{7,3},{8,12},{10,14},{12... | collective-permute-start | bytes 3145736 | tf_op jit(solution)/shard_map/ppermute | solution.py:284
  846.3 68.1 %collective-permute-start.10 = (bf16[512,1024]{0,1:T(8,128)(2,1)}, bf16[512,1024]{0,1:T(8,128)(2,1)}, u32[]{:S(2)}, u32[]{:S(2)}) collective-permute-start(bf16[512,1024]{0,1:T(8,128)(2,1)} %get-tuple-element.36), channel_id=1, source_target_pairs={{0,6},{2,0},{4,2},{6,4},{1,7},{3,1},{5,3},{7,5},{8,14},{10,8},{12,... | collective-permute-start | bytes 3145736 | tf_op jit(solution)/shard_map/ppermute | solution.py:284
  942.5 27.1 %collective-permute-start.16 = (bf16[576,2176]{1,0:T(8,128)(2,1)S(1)}, bf16[576,2176]{1,0:T(8,128)(2,1)S(1)}, u32[]{:S(2)}, u32[]{:S(2)}) collective-permute-start(bf16[576,2176]{1,0:T(8,128)(2,1)S(1)} %pad_maximum_fusion.7), channel_id=1, source_target_pairs={{0,8},{8,0},{16,24},{24,16},{1,9},{9,1},{17,25},{25,17},{2,10},{10... | collective-permute-start | bytes 7520264 | tf_op jit(solution)/shard_map/ppermute | solution.py:227
  953.8 8.2 collective-permute-start.20
  956.4 17.8 %collective-permute-start.19 = (bf16[576,1024]{1,0:T(8,128)(2,1)S(1)}, bf16[576,1024]{1,0:T(8,128)(2,1)S(1)}, u32[]{:S(2)}, u32[]{:S(2)}) collective-permute-start(bf16[576,1024]{1,0:T(8,128)(2,1)S(1)} %convolution_convert_fusion.11), channel_id=1, source_target_pairs={{0,8},{8,0},{16,24},{24,16},{1,9},{9,1},{17,25},{25,17},{2,10},{10... | collective-permute-start | bytes 3538952 | tf_op jit(solution)/shard_map/ppermute | solution.py:227
  964.4 31.2 %collective-permute-start.21 = (bf16[576,1024]{1,0:T(8,128)(2,1)S(1)}, bf16[576,1024]{1,0:T(8,128)(2,1)S(1)}, u32[]{:S(2)}, u32[]{:S(2)}) collective-permute-start(bf16[576,1024]{1,0:T(8,128)(2,1)S(1)} %add_convert_fusion.7), channel_id=1, source_target_pairs={{0,16},{8,24},{16,0},{24,8},{1,17},{9,25},{17,1},{25,9},{2,18},{10... | collective-permute-start | bytes 3538952 | tf_op jit(solution)/shard_map/ppermute | solution.py:233
  969.6 42.5 %collective-permute-start.15 = (bf16[576,2176]{1,0:T(8,128)(2,1)}, bf16[576,2176]{1,0:T(8,128)(2,1)}, u32[]{:S(2)}, u32[]{:S(2)}) collective-permute-start(bf16[576,2176]{1,0:T(8,128)(2,1)} %pad_maximum_fusion.6), channel_id=1, source_target_pairs={{0,8},{8,0},{16,24},{24,16},{1,9},{9,1},{17,25},{25,17},{2,10},{10... | collective-permute-start | bytes 7520264 | tf_op jit(solution)/shard_map/ppermute | solution.py:227
  971.8 77.7 %collective-permute-start.17 = (bf16[576,2176]{1,0:T(8,128)(2,1)}, bf16[576,2176]{1,0:T(8,128)(2,1)}, u32[]{:S(2)}, u32[]{:S(2)}) collective-permute-start(bf16[576,2176]{1,0:T(8,128)(2,1)} %fusion.27), channel_id=1, source_target_pairs={{0,16},{8,24},{16,0},{24,8},{1,17},{9,25},{17,1},{25,9},{2,18},{10... | collective-permute-start | bytes 7520264 | tf_op jit(solution)/shard_map/ppermute | solution.py:233
  974.2 93.8 %collective-permute-start.22 = (bf16[576,4608]{1,0:T(8,128)(2,1)}, bf16[576,4608]{1,0:T(8,128)(2,1)}, u32[]{:S(2)}, u32[]{:S(2)}) collective-permute-start(bf16[576,4608]{1,0:T(8,128)(2,1)} %convolution_convert_fusion.5), channel_id=1, source_target_pairs={{0,8},{8,0},{16,24},{24,16},{1,9},{9,1},{17,25},{25,17},{2,10},{10... | collective-permute-start | bytes 15925256 | tf_op jit(solution)/shard_map/ppermute | solution.py:227
  997.6 539.8 %reduce-scatter.6.cloned.1.call-start = ((), (), s32[]{:S(2)}) async-start(), calls=%async_computation.10 | async-start | bytes 3133440 | tf_op jit(solution)/shard_map/reduce_scatter | solution.py:236
  1007.3 155.3 %collective-permute-start.24 = (bf16[576,4608]{1,0:T(8,128)(2,1)}, bf16[576,4608]{1,0:T(8,128)(2,1)}, u32[]{:S(2)}, u32[]{:S(2)}) collective-permute-start(bf16[576,4608]{1,0:T(8,128)(2,1)} %add_convert_fusion.5), channel_id=1, source_target_pairs={{0,16},{8,24},{16,0},{24,8},{1,17},{9,25},{17,1},{25,9},{2,18},{10... | collective-permute-start | bytes 15925256 | tf_op jit(solution)/shard_map/ppermute | solution.py:233
  1054.2 490.1 %reduce-scatter.10.cloned.1.call-start = ((), (), s32[]{:S(2)}) async-start(), calls=%async_computation.12 | async-start | bytes 6635520 | tf_op jit(solution)/shard_map/reduce_scatter | solution.py:236
  1062.2 116.9 %collective-permute-start.26 = (bf16[576,4608]{1,0:T(8,128)(2,1)}, bf16[576,4608]{1,0:T(8,128)(2,1)}, u32[]{:S(2)}, u32[]{:S(2)}) collective-permute-start(bf16[576,4608]{1,0:T(8,128)(2,1)} %convolution_convert_fusion.2), channel_id=1, source_target_pairs={{0,8},{8,0},{16,24},{24,16},{1,9},{9,1},{17,25},{25,17},{2,10},{10... | collective-permute-start | bytes 15925256 | tf_op jit(solution)/shard_map/ppermute | solution.py:227
  1170.7 376.7 %reduce-scatter.12.cloned.1.call-start = ((), (), s32[]{:S(2)}) async-start(), calls=%async_computation.13 | async-start | bytes 6635520 | tf_op jit(solution)/shard_map/reduce_scatter | solution.py:236
  1179.0 20.3 %collective-permute-start.25 = (bf16[576,4608]{1,0:T(8,128)(2,1)}, bf16[576,4608]{1,0:T(8,128)(2,1)}, u32[]{:S(2)}, u32[]{:S(2)}) collective-permute-start(bf16[576,4608]{1,0:T(8,128)(2,1)} %convolution_convert_fusion.3), channel_id=1, source_target_pairs={{0,8},{8,0},{16,24},{24,16},{1,9},{9,1},{17,25},{25,17},{2,10},{10... | collective-permute-start | bytes 15925256 | tf_op jit(solution)/shard_map/ppermute | solution.py:227
  1188.7 116.9 %collective-permute-start.27 = (bf16[576,4608]{1,0:T(8,128)(2,1)}, bf16[576,4608]{1,0:T(8,128)(2,1)S(1)}, u32[]{:S(2)}, u32[]{:S(2)}) collective-permute-start(bf16[576,4608]{1,0:T(8,128)(2,1)} %add_convert_fusion.3), channel_id=1, source_target_pairs={{0,16},{8,24},{16,0},{24,8},{1,17},{9,25},{17,1},{25,9},{2,18},{10... | collective-permute-start | bytes 15925256 | tf_op jit(solution)/shard_map/ppermute | solution.py:233
  1196.1 123.4 %collective-permute-start.29 = (bf16[576,4608]{1,0:T(8,128)(2,1)}, bf16[576,4608]{1,0:T(8,128)(2,1)}, u32[]{:S(2)}, u32[]{:S(2)}) collective-permute-start(bf16[576,4608]{1,0:T(8,128)(2,1)} %convolution_convert_fusion), channel_id=1, source_target_pairs={{0,8},{8,0},{16,24},{24,16},{1,9},{9,1},{17,25},{25,17},{2,10},{10... | collective-permute-start | bytes 15925256 | tf_op jit(solution)/shard_map/ppermute | solution.py:227
  1312.4 257.8 %reduce-scatter.14.cloned.1.call-start = ((), (), s32[]{:S(2)}) async-start(), calls=%async_computation.14 | async-start | bytes 6635520 | tf_op jit(solution)/shard_map/reduce_scatter | solution.py:236
  1319.4 14.5 collective-permute-start.28
  1329.0 117.0 %collective-permute-start.30 = (bf16[576,4608]{1,0:T(8,128)(2,1)}, bf16[576,4608]{1,0:T(8,128)(2,1)S(1)}, u32[]{:S(2)}, u32[]{:S(2)}) collective-permute-start(bf16[576,4608]{1,0:T(8,128)(2,1)} %add_convert_fusion.1), channel_id=1, source_target_pairs={{0,16},{8,24},{16,0},{24,8},{1,17},{9,25},{17,1},{25,9},{2,18},{10... | collective-permute-start | bytes 15925256 | tf_op jit(solution)/shard_map/ppermute | solution.py:233
  1454.7 28.9 %collective-permute-start.13 = (bf16[256,2304]{1,0:T(8,128)(2,1)S(1)}, bf16[256,2304]{1,0:T(8,128)(2,1)S(1)}, u32[]{:S(2)}, u32[]{:S(2)}) collective-permute-start(bf16[256,2304]{1,0:T(8,128)(2,1)S(1)} %slice.309), channel_id=1, source_target_pairs={{0,1},{1,0},{2,3},{3,2},{4,5},{5,4},{6,7},{7,6},{8,9},{9,8},{10,11... | collective-permute-start | bytes 3538952 | tf_op jit(solution)/shard_map/ppermute | solution.py:310
  1456.0 52.9 %collective-permute-start.6 = (bf16[256,2304]{1,0:T(8,128)(2,1)S(1)}, bf16[256,2304]{1,0:T(8,128)(2,1)S(1)}, u32[]{:S(2)}, u32[]{:S(2)}) collective-permute-start(bf16[256,2304]{1,0:T(8,128)(2,1)S(1)} %copy-done.45), channel_id=1, source_target_pairs={{0,1},{1,0},{2,3},{3,2},{4,5},{5,4},{6,7},{7,6},{8,9},{9,8},{10,11... | collective-permute-start | bytes 3538952 | tf_op jit(solution)/shard_map/ppermute | solution.py:121
  1488.6 44.3 %collective-permute-start.14 = (bf16[256,2304]{1,0:T(8,128)(2,1)S(1)}, bf16[256,2304]{1,0:T(8,128)(2,1)S(1)}, u32[]{:S(2)}, u32[]{:S(2)}) collective-permute-start(bf16[256,2304]{1,0:T(8,128)(2,1)S(1)} %fusion.35), channel_id=1, source_target_pairs={{0,1},{1,0},{2,3},{3,2},{4,5},{5,4},{6,7},{7,6},{8,9},{9,8},{10,11... | collective-permute-start | bytes 3538952 | tf_op jit(solution)/shard_map/ppermute | solution.py:121
  1538.3 5.1 collective-permute-start.18
  (89 other events, 1166.5 us)
Sparse Core Ops, SparseCore 0:
  12.2 87.7 all-gather.5
  102.3 96.8 all-gather.7
  200.7 141.4 all-gather.9
  343.6 115.0 all-gather.11
  460.1 116.0 all-gather.13
  997.7 51.0 reduce-scatter.7
  1054.3 72.3 reduce-scatter.5
  1170.8 116.3 reduce-scatter.9
  1312.5 116.7 reduce-scatter.11
  1452.9 117.1 reduce-scatter.13

commit v2 on v1

v2 whole, which is shorter than its diff:
```python
import functools

import jax
import jax.numpy as jnp
from jax import lax
from jax.experimental import pallas as pl
from jax.experimental.pallas import tpu as pltpu
from jax.sharding import PartitionSpec as P

HQ = 8
KV = 4
HD = 256
LEN = 2048

epsilon = 1e-06
cap_value = 50.0
gelu_coef = 0.7978845608028654
cores = 2
pad_lanes = 128

f32 = jnp.float32
bf16 = jnp.bfloat16


def rms_norm(values, gain):
    factor = lax.rsqrt(jnp.mean(values * values, axis=-1, keepdims=True) + epsilon)
    return values * factor * gain


def gelu_tanh(values):
    return (
        0.5 * values * (1.0 + jnp.tanh(gelu_coef * (values + 0.044715 * values * values * values)))
    )


def gated_product(gate, upward):
    return gelu_tanh(gate) * upward


def rotary_tables(positions, head_size):
    half = head_size // 2
    freqs = 10000.0 ** (-(jnp.arange(half, dtype=f32) * 2.0) / head_size)
    angle = positions.astype(f32)[:, None] * freqs[None, :]
    return (jnp.cos(angle), jnp.sin(angle))


attend_limit = 48 * 1024 * 1024


def dotted(left, right, left_dim, right_dim, precision=None):
    return lax.dot_general(
        left,
        right,
        (((left_dim,), (right_dim,)), ((), ())),
        precision=precision,
        preferred_element_type=f32,
    )


def turn(values, cosine, sine):
    half = HD // 2
    first, second = values[:, :half], values[:, half:]
    return jnp.concatenate(
        [first * cosine - second * sine, second * cosine + first * sine], axis=1
    )


def forward_kernel(chunks, pre_ref, kv_ref, cos_ref, sin_ref, qpos_ref, kpos_ref, q_ref, out_ref, low_ref, inv_ref):
    rows = pre_ref.shape[0]
    size = kv_ref.shape[0] // chunks
    q = turn(pre_ref[...], cos_ref[...], sin_ref[...]).astype(bf16)
    q_ref[...] = q
    qpos = qpos_ref[...]
    total = jnp.zeros((1, rows), f32)
    acc = jnp.zeros((HD, rows), f32)
    for c in range(chunks):
        part = pl.ds(c * size, size)
        raw = dotted(kv_ref[part, :HD], q, 1, 1)
        level = jnp.tanh(raw * (HD ** (-0.5) / cap_value))
        weight = jnp.where(qpos >= kpos_ref[part, :], jnp.exp(cap_value * level), 0.0)
        total = total + jnp.sum(weight, axis=0, keepdims=True)
        acc = acc + dotted(kv_ref[part, HD:], weight.astype(bf16), 0, 0)
    inverse = 1.0 / total
    inv_ref[0] = inverse
    out = (acc * inverse).T
    out_ref[...] = out
    low_ref[...] = out.astype(bf16)


def attend_forward(query_pre, kv_all, cosine, sine, qpos, kpos, groups, per_group, chunks):
    rows, width = query_pre.shape
    length = kv_all.shape[0]
    heads = groups * per_group
    by_head = pl.BlockSpec((rows, HD), lambda g, r: (0, g * per_group + r))
    fixed = lambda shape: pl.BlockSpec(shape, lambda g, r: (0, 0))
    return pl.pallas_call(
        functools.partial(forward_kernel, chunks),
        grid=(groups, per_group),
        in_specs=[
            by_head,
            pl.BlockSpec((length, 2 * HD), lambda g, r: (0, g)),
            fixed((rows, HD // 2)),
            fixed((rows, HD // 2)),
            fixed((1, rows)),
            fixed((length, 1)),
        ],
        out_specs=[
            by_head,
            by_head,
            by_head,
            pl.BlockSpec((1, 1, rows), lambda g, r: (g * per_group + r, 0, 0)),
        ],
        out_shape=[
            jax.ShapeDtypeStruct((rows, width), bf16),
            jax.ShapeDtypeStruct((rows, width), f32),
            jax.ShapeDtypeStruct((rows, width), bf16),
            jax.ShapeDtypeStruct((heads, 1, rows), f32),
        ],
        compiler_params=pltpu.CompilerParams(vmem_limit_bytes=attend_limit),
        cost_estimate=pl.CostEstimate(
            flops=4 * rows * length * width,
            bytes_accessed=14 * rows * width + 4 * length * groups * HD,
            transcendentals=2 * rows * length * heads,
        ),
        name="attend_forward",
    )(query_pre, kv_all, cosine, sine, qpos, kpos)


def backward_kernel(per_group, q_ref, kv_ref, da_ref, out_ref, inv_ref, cos_ref, sin_ref, qpos_ref, kpos_ref, dq_ref, dkv_ref, delta_ref, sum_ref):
    c, r = pl.program_id(1), pl.program_id(2)
    q, da = q_ref[...], da_ref[...]
    k, v = kv_ref[:, :HD], kv_ref[:, HD:]

    @pl.when(c == 0)
    def _():
        delta_ref[r] = dotted(
            jnp.ones((8, HD), f32), da.astype(f32) * out_ref[...], 1, 1, lax.Precision.HIGHEST
        )

    delta = delta_ref[r][0:1]
    level = jnp.tanh(dotted(k, q, 1, 1) * (HD ** (-0.5) / cap_value))
    seen = qpos_ref[...] >= kpos_ref[...]
    prob = jnp.where(seen, jnp.exp(cap_value * level), 0.0) * inv_ref[0]
    d_prob = dotted(v, da, 1, 1)
    d_raw = (prob * (d_prob - delta) * (1.0 - level * level)).astype(bf16)
    d_key = dotted(d_raw, q, 1, 0) * HD ** (-0.5)
    d_value = dotted(prob.astype(bf16), da, 1, 0)
    d_query = dotted(d_raw, k, 0, 0)

    @pl.when(r == 0)
    def _():
        dkv_ref[:, :HD] = d_key
        dkv_ref[:, HD:] = d_value

    @pl.when(r > 0)
    def _():
        dkv_ref[:, :HD] += d_key
        dkv_ref[:, HD:] += d_value

    @pl.when(c == 0)
    def _():
        sum_ref[r] = d_query

    @pl.when(c > 0)
    def _():
        sum_ref[r] += d_query

    for head in range(per_group):

        @pl.when((c == pl.num_programs(1) - 1) & (r == head))
        def _():
            whole = sum_ref[head] * HD ** (-0.5)
            dq_ref[:, head * HD : (head + 1) * HD] = turn(
                whole, cos_ref[...], -sin_ref[...]
            ).astype(bf16)


def attend_backward(queries, kv_all, d_attended, out, inverse, cosine, sine, qpos, kpos, groups, per_group, chunks):
    rows, width = queries.shape
    length = kv_all.shape[0]
    size = length // chunks
    heads = groups * per_group
    by_head = pl.BlockSpec((rows, HD), lambda g, c, r: (0, g * per_group + r))
    fixed = lambda shape: pl.BlockSpec(shape, lambda g, c, r: (0, 0))
    by_chunk = pl.BlockSpec((size, 2 * HD), lambda g, c, r: (c, g))
    return pl.pallas_call(
        functools.partial(backward_kernel, per_group),
        grid=(groups, chunks, per_group),
        in_specs=[
            by_head,
            by_chunk,
            by_head,
            by_head,
            pl.BlockSpec((1, 1, rows), lambda g, c, r: (g * per_group + r, 0, 0)),
            fixed((rows, HD // 2)),
            fixed((rows, HD // 2)),
            fixed((1, rows)),
            pl.BlockSpec((size, 1), lambda g, c, r: (c, 0)),
        ],
        out_specs=[
            pl.BlockSpec((rows, per_group * HD), lambda g, c, r: (0, g)),
            by_chunk,
        ],
        out_shape=[
            jax.ShapeDtypeStruct((rows, width), bf16),
            jax.ShapeDtypeStruct((length, groups * 2 * HD), f32),
        ],
        scratch_shapes=[
            pltpu.VMEM((per_group, 8, rows), f32),
            pltpu.VMEM((per_group, rows, HD), f32),
        ],
        compiler_params=pltpu.CompilerParams(vmem_limit_bytes=attend_limit),
        cost_estimate=pl.CostEstimate(
            flops=10 * rows * length * width,
            bytes_accessed=10 * rows * width + 12 * length * groups * HD,
            transcendentals=2 * rows * length * heads,
        ),
        name="attend_backward",
    )(queries, kv_all, d_attended, out, inverse, cosine, sine, qpos, kpos)


def contract(left, right, left_dim, right_dim):
    return lax.dot_general(
        left, right, (((left_dim,), (right_dim,)), ((), ())), preferred_element_type=f32
    )


def body(
    layer_input,
    block_order,
    pre_attend,
    query_weight,
    key_weight,
    value_weight,
    output_weight,
    post_attend,
    pre_feed,
    gate_weight,
    up_weight,
    down_weight,
    post_feed,
    cotangent,
):
    _, rows, width = layer_input.shape
    block_len = LEN // block_order.shape[1]
    per_group = HQ // KV
    tensor_count = lax.axis_size("tensor")
    groups = KV // tensor_count
    factor = HD ** (-0.5)
    dp_count = lax.axis_size("dp")
    ctx_count = lax.axis_size("ctx")
    tensor_index = lax.axis_index("tensor")
    ctx_index = lax.axis_index("ctx")
    dp_index = lax.axis_index("dp")
    y_count = dp_count // cores
    y_index = dp_index // cores
    core_index = dp_index % cores
    share = width // (dp_count * ctx_count)
    quarter = share * ctx_count
    half = rows // tensor_count
    pair = 2
    far_count = ctx_count // pair
    far_index = ctx_index // pair
    near_index = ctx_index % pair
    x_swap = [(0, 1), (1, 0)]
    all_swaps = {}
    for bz, bx in ((0, 1), (1, 0), (1, 1)):
        all_swaps[bz, bx] = [
            (c * 2 + t, (c ^ bz) * 2 + (t ^ bx)) for c in range(ctx_count) for t in range(2)
        ]
    near_swap = [(c, c ^ 1) for c in range(ctx_count)]

    def far_shift(step):
        return [
            (c, ((c // pair + step) % far_count) * pair + c % pair) for c in range(ctx_count)
        ]

    def along(dy, dc):
        pairs = []
        for y in range(y_count):
            for core in range(cores):
                target = ((y + dy) % y_count) * cores + (core + dc) % cores
                pairs.append((y * cores + core, target))
        return pairs

    def after(value, *others):
        return lax.optimization_barrier((value, *others))[0]

    def chosen(parts, index, place):
        count = len(parts)
        result = parts[0]
        for step in range(1, count):
            result = jnp.where((index - place) % count == step, parts[step], result)
        return result

    def in_order(parts, index):
        return jnp.concatenate([chosen(parts, index, k) for k in range(len(parts))], axis=0)

    def relative(values):
        first, second = values[:half], values[half:]
        flip = tensor_index == 1
        return jnp.concatenate(
            [jnp.where(flip, second, first), jnp.where(flip, first, second)], axis=0
        )

    def join(own):
        return jnp.concatenate([own, lax.ppermute(own, "tensor", x_swap)], axis=0)

    def join_absolute(own):
        return relative(join(own))

    def join_all(own):
        parts = [own]
        for pairs in all_swaps.values():
            parts.append(lax.ppermute(own, ("ctx", "tensor"), pairs))
        return jnp.concatenate(parts, axis=0)

    def pack_all(product):
        return [product[(k + 1) * half : (k + 2) * half].astype(bf16) for k in range(3)]

    def send_all(parts):
        return [
            lax.ppermute(part, ("ctx", "tensor"), pairs)
            for part, pairs in zip(parts, all_swaps.values())
        ]

    def sum_of(own, parts):
        for item in parts:
            own = own + item.astype(f32)
        return own

    all_pos = (
        block_order[0][:, None] * block_len + jnp.arange(block_len, dtype=jnp.int32)[None, :]
    ).reshape(ctx_count, tensor_count, half)
    all_pos = jnp.where(tensor_index == 1, all_pos[:, ::-1], all_pos).reshape(ctx_count, rows)
    source = (ctx_index - jnp.arange(ctx_count, dtype=jnp.int32)) % ctx_count
    key_pos = jnp.take(all_pos, source, axis=0)
    local_pos = key_pos[0]
    cosine, sine = rotary_tables(local_pos, HD)
    query_places = local_pos[None, :]
    key_places = key_pos.reshape(LEN, 1)

    both = ("dp", "ctx")
    gain_pack = jnp.stack([pre_attend, post_attend, pre_feed, post_feed], axis=1)
    gain_pack = jnp.pad(gain_pack, ((0, 0), (0, pad_lanes - 4)))
    heads_in_turn = []
    for g in range(groups):
        heads_in_turn += [
            key_weight[:, g * HD : (g + 1) * HD],
            value_weight[:, g * HD : (g + 1) * HD],
        ]
    keyvalue_pack = jnp.concatenate([*heads_in_turn, gain_pack], axis=1)
    keyvalue_all = lax.all_gather(keyvalue_pack, both, axis=0, tiled=True)
    query_mat = lax.all_gather(query_weight, both, axis=0, tiled=True)
    out_mat = lax.all_gather(output_weight.T, both, axis=0, tiled=True)

    hidden = gate_weight.shape[1] // pair
    is_high = near_index == 1

    def split(weight):
        low, high = weight[:, :hidden], weight[:, hidden:]
        return jnp.where(is_high, high, low), jnp.where(is_high, low, high)

    def far_pack(mine, got):
        return jnp.concatenate(
            [jnp.where(is_high, got, mine), jnp.where(is_high, mine, got)], axis=0
        )

    def far_start(block):
        return [lax.ppermute(block, "ctx", far_shift(s)) for s in range(1, far_count)]

    gate_mine, gate_other = split(gate_weight)
    up_mine, up_other = split(up_weight)
    down_mine, down_other = split(down_weight.T)
    gate_got = lax.ppermute(gate_other, "ctx", near_swap)
    rest_got = lax.ppermute(jnp.concatenate([up_other, down_other], axis=0), "ctx", near_swap)
    gate_block = far_pack(gate_mine, gate_got)
    gate_far = far_start(gate_block)
    up_block = far_pack(up_mine, rest_got[: rest_got.shape[0] // 2])
    down_block = far_pack(down_mine, rest_got[rest_got.shape[0] // 2 :])

    keyvalue_width = 2 * key_weight.shape[1]
    keyvalue_all = after(keyvalue_all, up_block, down_block)
    keyvalue_mat = keyvalue_all[:, :keyvalue_width]
    gains = keyvalue_all[:, keyvalue_width : keyvalue_width + 8].T.astype(f32)
    gain_in, gain_out, feed_gain, feed_post = gains[0], gains[1], gains[2], gains[3]

    inputs = relative(layer_input[0].astype(f32))
    own_inputs = inputs[:half]
    cot = lax.dynamic_slice_in_dim(cotangent[0], tensor_index * half, half, 0).astype(f32)

    attend_in = rms_norm(inputs, gain_in).astype(bf16)
    keyvalue_pre = jnp.dot(attend_in, keyvalue_mat, preferred_element_type=f32)
    turned = []
    for g in range(groups):
        middle = (2 * g + 1) * HD
        turned += [
            turn(keyvalue_pre[:, middle - HD : middle], cosine, sine),
            keyvalue_pre[:, middle : middle + HD],
        ]
    kv_local = jnp.concatenate(turned, axis=1).astype(bf16)

    from_left, from_right = [kv_local], [kv_local]

    def line_step(step, left_block, right_block):
        right_pairs = [(i, i + 1) for i in range(step - 1, ctx_count - 1)]
        left_pairs = [(i, i - 1) for i in range(1, ctx_count - step + 1)]
        from_left.append(lax.ppermute(left_block, "ctx", right_pairs))
        from_right.append(lax.ppermute(right_block, "ctx", left_pairs))

    line_step(1, kv_local, kv_local)
    gate_far = [after(part, kv_local) for part in gate_far]
    gate_rows = in_order([gate_block] + gate_far, far_index)
    gate_mat = lax.all_gather(gate_rows, "dp", axis=0, tiled=True)
    up_far = far_start(after(up_block, gate_rows))
    for step in range(2, ctx_count):
        left_block, right_block = from_left[-1], from_right[-1]
        if step == 2:
            left_block, right_block = after(left_block, gate_rows), after(right_block, gate_rows)
        line_step(step, left_block, right_block)
    last_blocks = (from_left[-2], from_right[-2])
    query_pre = jnp.dot(
        after(attend_in, *last_blocks), query_mat, preferred_element_type=f32
    )
    kv_parts = [kv_local]
    for step in range(1, ctx_count):
        kv_parts.append(
            jnp.where(ctx_index >= step, from_left[step], from_right[ctx_count - step])
        )
    kv_all = jnp.concatenate(kv_parts, axis=0)
    up_far = [after(part, *last_blocks) for part in up_far]
    up_rows = in_order([up_block] + up_far, far_index)
    up_mat = lax.all_gather(up_rows, "dp", axis=0, tiled=True)
    down_far = far_start(after(down_block, up_rows))
    kv_all = after(kv_all, up_rows)
    queries, attended_wide, attended, inverse_sums = attend_forward(
        query_pre, kv_all, cosine, sine, query_places, key_places, groups, per_group, ctx_count
    )
    down_far = [after(part, attended) for part in down_far]
    down_rows = in_order([down_block] + down_far, far_index)
    down_mat = lax.all_gather(down_rows, "dp", axis=0, tiled=True)
    other = contract(attended[half:], out_mat, 1, 1).astype(bf16)
    got = after(lax.ppermute(other, "tensor", x_swap), down_rows)
    attend_out = contract(attended[:half], out_mat, 1, 1) + got.astype(f32)
    hidden_mid = own_inputs + rms_norm(attend_out, gain_out)
    feed_own = rms_norm(hidden_mid, feed_gain).astype(bf16)
    feed_in = join_all(feed_own)
    gate = jnp.dot(feed_in, gate_mat, preferred_element_type=f32)
    upward = jnp.dot(feed_in, up_mat, preferred_element_type=f32)
    mixed = gated_product(gate, upward).astype(bf16)
    feed_part = contract(mixed, down_mat, 1, 1)
    sent = send_all(pack_all(feed_part))
    feed_out = sum_of(feed_part[:half], sent)
    layer_output = join_absolute(
        (hidden_mid + rms_norm(feed_out, feed_post)).astype(bf16)
    )[None]

    class Reduction:
        def __init__(self, left, right, extra=None):
            result = contract(left, right, 0, 0).astype(bf16)
            if extra is not None:
                result = jnp.concatenate([result, extra.T.astype(bf16)], axis=1)
            self.whole = result

        def piece(self, dy, dc):
            index = ((y_index + dy) % y_count) * cores + (core_index + dc) % cores
            return lax.dynamic_slice_in_dim(self.whole, index * quarter, quarter, 0)

        def core_pack(self):
            self.packed = [self.piece(dy, 1) for dy in range(y_count)]
            return self.packed

        def core_send(self):
            self.swapped = [lax.ppermute(p, "dp", along(0, 1)) for p in self.packed]

        def y_pack(self, *before):
            swapped = self.swapped
            if before:
                swapped = [after(item, *before) for item in swapped]
            self.packed = [
                (self.piece(dy, 0).astype(f32) + swapped[dy].astype(f32)).astype(bf16)
                for dy in range(1, y_count)
            ]
            return self.packed

        def y_send(self):
            self.arrived = [
                lax.ppermute(p, "dp", along(dy + 1, 0)) for dy, p in enumerate(self.packed)
            ]

        def column(self):
            total = self.piece(0, 0).astype(f32) + self.swapped[0].astype(f32)
            return sum_of(total, self.arrived)

        def finish_ctx(self):
            return lax.psum_scatter(
                self.column().astype(bf16), "ctx", scatter_dimension=0, tiled=True
            ).astype(f32)

        def far_pack(self, *before):
            if before:
                self.arrived = [after(item, *before) for item in self.arrived]
            total = self.column().astype(bf16)
            self.blocks = [total[k * pair * share : (k + 1) * pair * share] for k in range(far_count)]
            self.packed = [
                self.block_of((far_index + step) % far_count) for step in range(1, far_count)
            ]
            return self.packed

        def block_of(self, index):
            result = self.blocks[0]
            for k in range(1, far_count):
                result = jnp.where(index == k, self.blocks[k], result)
            return result

        def far_send(self):
            self.arrived = [
                lax.ppermute(p, "ctx", far_shift(s + 1)) for s, p in enumerate(self.packed)
            ]

        def near_pack(self, *before):
            if before:
                self.arrived = [after(item, *before) for item in self.arrived]
            total = sum_of(self.block_of(far_index).astype(f32), self.arrived)
            low, high = total[:share], total[share:]
            self.own = jnp.where(is_high, high, low)
            self.packed = jnp.where(is_high, low, high).astype(bf16)
            return [self.packed]

        def near_send(self):
            self.got = lax.ppermute(self.packed, "ctx", near_swap).astype(f32)

        def finish_near(self):
            return jnp.concatenate(
                [
                    jnp.where(is_high, self.got, self.own),
                    jnp.where(is_high, self.own, self.got),
                ],
                axis=1,
            )

    def norm_back(values, gain, incoming):
        _, back = jax.vjp(rms_norm, values, gain)
        return back(incoming)

    d_feed_out, post_feed_part = norm_back(feed_out, feed_post, cot)
    d_feed_low = join_all(d_feed_out.astype(bf16))
    down_sum = Reduction(d_feed_low, mixed)
    down_sum.core_pack()
    down_sum.core_send()
    d_mixed = jnp.dot(
        after(d_feed_low, *down_sum.packed), down_mat, preferred_element_type=f32
    )
    _, gate_back = jax.vjp(gated_product, gate, upward)
    d_gate, d_upward = gate_back(d_mixed)
    d_gate = d_gate.astype(bf16)
    d_upward = d_upward.astype(bf16)

    down_sum.y_pack(d_gate, d_upward)
    down_sum.y_send()
    d_feed_part = contract(after(d_gate, *down_sum.packed), gate_mat, 1, 1) + contract(
        after(d_upward, *down_sum.packed), up_mat, 1, 1
    )
    packed = pack_all(d_feed_part)
    sent = send_all(packed)
    gate_sum = Reduction(after(feed_in, *packed), d_gate)
    gate_sum.core_pack()
    gate_sum.core_send()
    down_sum.far_pack(*gate_sum.packed)
    down_sum.far_send()
    up_sum = Reduction(after(feed_in, *down_sum.packed), d_upward)
    up_sum.core_pack()
    up_sum.core_send()
    gate_sum.y_pack(*up_sum.packed)
    gate_sum.y_send()
    own_feed = after(d_feed_part[:half], *gate_sum.packed)
    d_feed_in = sum_of(own_feed, sent)

    d_from_feed, pre_feed_part = norm_back(hidden_mid, feed_gain, d_feed_in)
    d_mid = cot + d_from_feed
    d_attend_out, post_attend_part = norm_back(attend_out, gain_out, d_mid)
    d_attend_own = d_attend_out.astype(bf16)
    d_attend_got = lax.ppermute(d_attend_own, "tensor", x_swap)
    up_sum.y_pack(d_attend_own)
    up_sum.y_send()
    d_attend_got = after(d_attend_got, *up_sum.packed)
    d_attend_low = jnp.concatenate([d_attend_own, d_attend_got], axis=0)
    d_attended = jnp.dot(d_attend_low, out_mat, preferred_element_type=f32).astype(bf16)
    out_sum = Reduction(after(d_attend_low, d_attended), attended)
    out_sum.core_pack()
    out_sum.core_send()
    gate_sum.far_pack(*out_sum.packed)
    gate_sum.far_send()
    d_attended = after(d_attended, *gate_sum.packed)
    d_query_pre, d_kv = attend_backward(
        queries,
        kv_all,
        d_attended,
        attended_wide,
        inverse_sums,
        cosine,
        sine,
        query_places,
        key_places,
        groups,
        per_group,
        ctx_count,
    )

    def slot(index, carried):
        block = d_kv[index * rows : (index + 1) * rows]
        if carried is not None:
            block = block + carried.astype(f32)
        return block.astype(bf16)

    def line_sum(step, left_block, right_block):
        right_pairs = [(i, i + 1) for i in range(0, step)]
        left_pairs = [(i, i - 1) for i in range(ctx_count - step, ctx_count)]
        return (
            lax.ppermute(left_block, "ctx", right_pairs),
            lax.ppermute(right_block, "ctx", left_pairs),
        )

    sent_blocks = (slot(1, None), slot(ctx_count - 1, None))
    carried = line_sum(1, *sent_blocks)
    out_sum.y_pack(*sent_blocks)
    out_sum.y_send()
    query_sum = Reduction(after(attend_in, *out_sum.packed), d_query_pre)
    query_sum.core_pack()
    query_sum.core_send()
    down_sum.near_pack(*query_sum.packed)
    down_sum.near_send()
    before = (*query_sum.packed, *out_sum.packed, down_sum.packed)
    for step in range(2, ctx_count):
        carried = [after(item, *before) for item in carried]
        sent_blocks = (slot(step, carried[0]), slot(ctx_count - step, carried[1]))
        carried = line_sum(step, *sent_blocks)
        before = ()
        if step == 2:
            query_sum.y_pack(*sent_blocks)
            query_sum.y_send()
            up_sum.far_pack(*query_sum.packed)
            up_sum.far_send()
            before = (*query_sum.packed, *up_sum.packed)
    query_part = contract(after(d_query_pre, *sent_blocks), query_mat, 1, 1)
    gate_sum.near_pack(query_part)
    gate_sum.near_send()
    carried = [after(item, query_part, gate_sum.packed) for item in carried]
    d_kv_local = sum_of(d_kv[:rows], carried)
    turned = []
    for g in range(groups):
        middle = (2 * g + 1) * HD
        turned += [
            turn(d_kv_local[:, middle - HD : middle], cosine, -sine),
            d_kv_local[:, middle : middle + HD],
        ]
    d_keyvalue = jnp.concatenate(turned, axis=1).astype(bf16)

    in_factor = lax.rsqrt(jnp.mean(inputs * inputs, axis=-1, keepdims=True) + epsilon)
    d_attend_part = query_part + contract(d_keyvalue, keyvalue_mat, 1, 1)
    pre_attend_part = jnp.sum(d_attend_part * inputs * in_factor, axis=0)
    gain_parts = jnp.stack([pre_attend_part, post_attend_part, pre_feed_part, post_feed_part])
    gain_parts = jnp.pad(gain_parts, ((0, pad_lanes - 4), (0, 0)))
    got = lax.ppermute(d_attend_part[half:].astype(bf16), "tensor", x_swap)

    keyvalue_sum = Reduction(attend_in, d_keyvalue, gain_parts)
    keyvalue_sum.core_pack()
    keyvalue_sum.core_send()
    keyvalue_sum.y_pack()
    keyvalue_sum.y_send()
    d_attend_in = d_attend_part[:half] + got.astype(f32)
    up_sum.near_pack(*keyvalue_sum.packed)
    up_sum.near_send()
    out_grad = out_sum.finish_ctx().T
    query_grad = query_sum.finish_ctx()
    attend_grad = keyvalue_sum.finish_ctx()
    down_grad = down_sum.finish_near().T
    gate_grad = gate_sum.finish_near()
    up_grad = up_sum.finish_near()
    key_grad = jnp.concatenate(
        [attend_grad[:, 2 * g * HD : (2 * g + 1) * HD] for g in range(groups)], axis=1
    )
    value_grad = jnp.concatenate(
        [attend_grad[:, (2 * g + 1) * HD : (2 * g + 2) * HD] for g in range(groups)], axis=1
    )
    gain_grads = attend_grad[:, keyvalue_width:]
    gain_grads = (gain_grads + lax.ppermute(gain_grads, "tensor", x_swap)).T

    d_from_attend, _ = norm_back(own_inputs, gain_in, d_attend_in)
    input_grad = join_absolute((d_mid + d_from_attend).astype(bf16)).astype(f32)[None]

    return (
        layer_output,
        input_grad,
        gain_grads[0],
        query_grad,
        key_grad,
        value_grad,
        out_grad,
        gain_grads[1],
        gain_grads[2],
        gate_grad,
        up_grad,
        down_grad,
        gain_grads[3],
    )


def solution(mesh):
    both = ("dp", "ctx")
    return jax.shard_map(
        body,
        mesh=mesh,
        in_specs=(
            P("dp", "ctx", None),
            P("dp", None),
            P(both),
            P(both, "tensor"),
            P(both, "tensor"),
            P(both, "tensor"),
            P("tensor", both),
            P(both),
            P(both),
            P(both, "tensor"),
            P(both, "tensor"),
            P("tensor", both),
            P(both),
            P("dp", "ctx", None),
        ),
        out_specs=(
            P("dp", "ctx", None),
            P("dp", "ctx", None),
            P(both),
            P(both, "tensor"),
            P(both, "tensor"),
            P(both, "tensor"),
            P("tensor", both),
            P(both),
            P(both),
            P(both, "tensor"),
            P(both, "tensor"),
            P("tensor", both),
            P(both),
        ),
        check_vma=False,
    )
```

time: 1590 us -> 1240 us (0.78)
  waiting for transfers between devices: 1010 us -> 648 us
  matrix products: 340 us -> 213 us
  starting transfers between devices: 34.3 us -> 104 us
  other arithmetic: 111 us -> 152 us
  Pallas kernels: 0 us -> 40.9 us
    all_gather x4 -> x5, waiting for transfers between devices: 259 us -> 0.05 us  [the longest x1 0.02 us: body(): query_mat = lax.all_gather(query_weight, both, axis=0, tiled=True)]
    ppermute x5 -> x2, waiting for transfers between devices: 104 us -> 0.01 us  [join(): return jnp.concatenate([own, lax.ppermute(own, 'tensor', x_swap)], axis=0)]
    ppermute x24 -> x55, starting transfers between devices: 24.3 us -> 97.7 us  [the longest x3 28.3 us: far_start(): lax.ppermute(block, 'ctx', far_shift(s))]
    dot_general x29 -> x13, matrix products: 196 us -> 127 us  [contract(): lax.dot_general(left, right, (((left_dim,), (right_dim,)), ((), ())), pre...]
    dot_general x8 -> x3, matrix products: 85.2 us -> 39.5 us  [the longest x1 29.8 us: body(): jnp.dot(after(d_feed_low, *down_sum.packed), down_mat, preferred_element_...]
    pallas_call x0 -> x2, Pallas kernels: none -> 40.9 us  [the longest x1 28.8 us: attend_backward(): pl.pallas_call(functools.partial(backward_kernel, per_group), grid=(group...]
    reshape x6 -> x0, local copies, waits for them, and re-layouts: 21.8 us -> none  [the longest x2 10.3 us: body(): key_heads = kv_all[:, :key_width].reshape(LEN, groups, HD)]
    unnamed x10, waiting for transfers between devices: 2.53 us -> 24.3 us
  transfers between devices with their start and end apart: 41 -> 68, of which waited for: 22 -> 27; matrix products, arithmetic and copies ran while one was open for 25% -> 30% of each run, Pallas kernels for 0% -> 3%
where the time goes in v2:
time: 1240 us; the launch traced here: 1230 us
  waiting for transfers between devices  648 us (52%)
  matrix products  213 us (17%)
  other arithmetic  152 us (12%)
  starting transfers between devices  104 us (8%)
  local copies, waits for them, and re-layouts  61.1 us (5%)
  Pallas kernels  40.9 us (3%)
  between operations  16.1 us (1%)
    ppermute x3, waiting for transfers between devices, far_start(): lax.ppermute(block, 'ctx', far_shift(s))  155 us
    dot_general x13, matrix products, contract(): lax.dot_general(left, right, (((left_dim,), (right_dim,)), ((), ())), pre...  127 us
    ppermute x6, waiting for transfers between devices, join_all(): parts.append(lax.ppermute(own, ('ctx', 'tensor'), pairs))  91.7 us
    ppermute x3, waiting for transfers between devices, line_sum(): lax.ppermute(left_block, 'ctx', right_pairs)  84.2 us
    ppermute x1, waiting for transfers between devices, body(): gate_got = lax.ppermute(gate_other, 'ctx', near_swap)  64.5 us
    ppermute x6, waiting for transfers between devices, send_all(): lax.ppermute(part, ('ctx', 'tensor'), pairs)  48.6 us
    ppermute x3, waiting for transfers between devices, line_step(): from_right.append(lax.ppermute(right_block, 'ctx', left_pairs))  39.7 us
    ppermute x6, waiting for transfers between devices, y_send(): lax.ppermute(p, 'dp', along(dy + 1, 0))  37.9 us
  transfers between devices with their start and end apart: 68, of which 27 were waited for; matrix products, arithmetic and copies ran while one was open for 30% of the time, Pallas kernels for 3%

profile of v2, /device:TPU:0, one launch (start us, length us, event | category | flops | bytes accessed | tf_op | source)
XLA Modules:
  0.0 1234.4 jit_solution(5382562702655301723)
XLA Ops:
  32.4 64.5 %collective-permute-done.2 = bf16[144,2304]{1,0:T(8,128)(2,1)S(1)} collective-permute-done((bf16[144,2304]{1,0:T(8,128)(2,1)}, bf16[144,2304]{1,0:T(8,128)(2,1)S(1)}, u32[]{:S(2)}, u32[]{:S(2)}) %collective-permute-start.2) | collective-permute-done | bytes 663584 | tf_op jit(solution)/shard_map/ppermute | solution.py:375
  118.5 68.1 %collective-permute-done.3 = bf16[288,2304]{1,0:T(8,128)(2,1)} collective-permute-done((bf16[288,2304]{1,0:T(8,128)(2,1)}, bf16[288,2304]{1,0:T(8,128)(2,1)}, u32[]{:S(2)}, u32[]{:S(2)}) %collective-permute-start.3) | collective-permute-done | bytes 1327136 | tf_op jit(solution)/shard_map/ppermute | solution.py:370
  191.6 4.6 collective-permute-start.1
  196.8 29.7 %collective-permute-done.5 = bf16[512,1024]{1,0:T(8,128)(2,1)S(1)} collective-permute-done((bf16[512,1024]{1,0:T(8,128)(2,1)S(1)}, bf16[512,1024]{1,0:T(8,128)(2,1)S(1)}, u32[]{:S(2)}, u32[]{:S(2)}) %collective-permute-start.5) | collective-permute-done | bytes 1048608 | tf_op jit(solution)/shard_map/ppermute | solution.py:409
  227.9 5.8 collective-permute-done.1
  235.4 67.3 %collective-permute-done.9 = bf16[288,2304]{1,0:T(8,128)(2,1)S(1)} collective-permute-done((bf16[288,2304]{1,0:T(8,128)(2,1)}, bf16[288,2304]{1,0:T(8,128)(2,1)S(1)}, u32[]{:S(2)}, u32[]{:S(2)}) %collective-permute-start.9) | collective-permute-done | bytes 1327136 | tf_op jit(solution)/shard_map/ppermute | solution.py:370
  307.9 25.7 %collective-permute-start.11 = (bf16[288,2304]{1,0:T(8,128)(2,1)}, bf16[288,2304]{1,0:T(8,128)(2,1)}, u32[]{:S(2)}, u32[]{:S(2)}) collective-permute-start(bf16[288,2304]{1,0:T(8,128)(2,1)} %pad_maximum_fusion.12), channel_id=1, source_target_pairs={{0,4},{2,6},{4,0},{6,2},{1,5},{3,7},{5,1},{7,3},{8,12},{10,14},{12... | collective-permute-start | bytes 3981320 | tf_op jit(solution)/shard_map/ppermute | solution.py:370
  336.7 7.1 fusion.88.pre_ref
  343.7 10.0 collective-permute-done.7
  358.6 12.1 attend_forward.1
  370.7 19.6 %collective-permute-done.11 = bf16[288,2304]{1,0:T(8,128)(2,1)} collective-permute-done((bf16[288,2304]{1,0:T(8,128)(2,1)}, bf16[288,2304]{1,0:T(8,128)(2,1)}, u32[]{:S(2)}, u32[]{:S(2)}) %collective-permute-start.11) | collective-permute-done | bytes 1327136 | tf_op jit(solution)/shard_map/ppermute | solution.py:370
  399.5 25.6 %collective-permute-done.10 = bf16[256,2304]{1,0:T(8,128)(2,1)S(1)} collective-permute-done((bf16[256,2304]{1,0:T(8,128)(2,1)S(1)}, bf16[256,2304]{1,0:T(8,128)(2,1)S(1)}, u32[]{:S(2)}, u32[]{:S(2)}) %collective-permute-start.10) | collective-permute-done | bytes 1179680 | tf_op jit(solution)/shard_map/ppermute | solution.py:443
  433.4 24.5 %collective-permute-done.12 = bf16[256,2304]{1,0:T(8,128)(2,1)S(1)} collective-permute-done((bf16[256,2304]{1,0:T(8,128)(2,1)S(1)}, bf16[256,2304]{1,0:T(8,128)(2,1)S(1)}, u32[]{:S(2)}, u32[]{:S(2)}) %collective-permute-start.12) | collective-permute-done | bytes 1179680 | tf_op jit(solution)/shard_map/ppermute | solution.py:315
  461.3 21.5 %collective-permute-done.14 = bf16[256,2304]{1,0:T(8,128)(2,1)} collective-permute-done((bf16[256,2304]{1,0:T(8,128)(2,1)S(1)}, bf16[256,2304]{1,0:T(8,128)(2,1)}, u32[]{:S(2)}, u32[]{:S(2)}) %collective-permute-start.14) | collective-permute-done | bytes 1179680 | tf_op jit(solution)/shard_map/ppermute | solution.py:315
  482.8 20.2 %fusion.76 = f32[1024,2304]{1,0:T(8,128)} fusion(bf16[2304,2304]{1,0:T(8,128)(2,1)} %all-gather.13.cloned.1.call-done, bf16[256,2304]{1,0:T(8,128)(2,1)} %collective-permute-done.14, bf16[256,2304]{1,0:T(8,128)(2,1)} %copy-done.52, bf16[256,2304]{1,0:T(8,128)(2,1)} %copy-done.51, bf16[256,2304]{1,0:T(8,128)(2,1)S(1)} %multiply_convert_fusion.3), kind=kOutput, calls=%fused_computation.268 | convolution fusion | flops 10890510336 | bytes 24772608 | tf_op jit(solution)/shard_map/dot_general | solution.py:448
  503.0 23.3 %multiply_convert_fusion.1 = (bf16[1024,2304]{1,0:T(8,128)(2,1)}, f32[1024,2304]{1,0:T(8,128)}) fusion(f32[1024,2304]{1,0:T(8,128)} %fusion.76, bf16[2304,2304]{1,0:T(8,128)(2,1)} %all-gather.15.cloned.1.call-done, bf16[256,2304]{1,0:T(8,128)(2,1)} %collective-permute-done.14, bf16[256,2304]{1,0:T(8,128)(2,1)} %copy-done.52, ...), kind=kOutput, calls=%fused_computation.19 | convolution fusion | flops 10914103296 | bytes 38928384 | tf_op jit(solution)/shard_map/dot_general | solution.py:449
  526.4 17.1 %fusion.86 = (bf16[1024,2304]{1,0:T(8,128)(2,1)S(1)}, f32[1024,2304]{1,0:T(8,128)}) fusion(bf16[1024,2304]{1,0:T(8,128)(2,1)} %get-tuple-element.273, bf16[2304,2304]{1,0:T(8,128)(2,1)} %all-gather.17.cloned.1.call-done), kind=kOutput, calls=%fused_computation.277 | convolution fusion | flops 10873995264 | bytes 29491200 | tf_op jit(solution)/shard_map/dot_general | solution.py:223
  548.8 24.7 %collective-permute-done.15 = bf16[256,2304]{1,0:T(8,128)(2,1)S(1)} collective-permute-done((bf16[256,2304]{1,0:T(8,128)(2,1)}, bf16[256,2304]{1,0:T(8,128)(2,1)S(1)}, u32[]{:S(2)}, u32[]{:S(2)}) %collective-permute-start.15) | collective-permute-done | bytes 1179680 | tf_op jit(solution)/shard_map/ppermute | solution.py:323
  576.1 21.4 %collective-permute-done.17 = bf16[256,2304]{1,0:T(8,128)(2,1)} collective-permute-done((bf16[256,2304]{1,0:T(8,128)(2,1)}, bf16[256,2304]{1,0:T(8,128)(2,1)}, u32[]{:S(2)}, u32[]{:S(2)}) %collective-permute-start.17) | collective-permute-done | bytes 1179680 | tf_op jit(solution)/shard_map/ppermute | solution.py:323
  607.8 5.4 pad_maximum_fusion.1
  615.3 43.3 %collective-permute-done.19 = bf16[256,2304]{1,0:T(8,128)(2,1)} collective-permute-done((bf16[256,2304]{1,0:T(8,128)(2,1)S(1)}, bf16[256,2304]{1,0:T(8,128)(2,1)}, u32[]{:S(2)}, u32[]{:S(2)}) %collective-permute-start.19) | collective-permute-done | bytes 1179680 | tf_op jit(solution)/shard_map/ppermute | solution.py:315
  658.6 14.4 %convolution_convert_fusion.2 = bf16[2304,2304]{1,0:T(8,128)(2,1)S(1)} fusion(bf16[1024,2304]{1,0:T(8,128)(2,1)} %get-tuple-element.273, bf16[256,2304]{1,0:T(8,128)(2,1)} %collective-permute-done.21, bf16[256,2304]{1,0:T(8,128)(2,1)} %collective-permute-done.20, bf16[256,2304]{1,0:T(8,128)(2,1)} %collective-permute-done.19, ...), kind=kOutput, calls=%fused_computation.3 | convolution fusion | flops 10895818752 | bytes 20054016 | tf_op jit(solution)/shard_map/dot_general | solution.py:223
  679.1 4.8 pad_maximum_fusion.2
  683.9 29.8 %multiply_convert_fusion = (bf16[1024,2304]{1,0:T(8,128)(2,1)}, bf16[1024,2304]{1,0:T(8,128)(2,1)}) fusion(f32[1024,2304]{1,0:T(8,128)} %fusion.76, f32[1024,2304]{1,0:T(8,128)} %get-tuple-element.274, bf16[1024,2304]{1,0:T(8,128)(2,1)} %pad_maximum_fusion.2, bf16[2304,2304]{1,0:T(8,128)(2,1)} %all-gather.17.cloned.1.call-done), kind=kOutput, calls=%fused_computation.18 | convolution fusion | flops 10937696256 | bytes 43646976 | tf_op jit(solution)/shard_map/dot_general | solution.py:551
  713.7 4.8 add_convert_fusion.5
  720.1 15.3 %fusion.89 = f32[1024,2304]{1,0:T(8,128)} fusion(bf16[1024,2304]{1,0:T(8,128)(2,1)S(1)} %copy-done.83, bf16[2304,2304]{1,0:T(8,128)(2,1)} %all-gather.13.cloned.1.call-done), kind=kOutput, calls=%fused_computation.280 | convolution fusion | flops 10871635968 | bytes 24772608 | tf_op jit(solution)/shard_map/dot_general | solution.py:223
  735.4 20.6 %fusion.87 = (bf16[1024,2304]{1,0:T(8,128)(2,1)}, f32[1024,2304]{1,0:T(8,128)}) fusion(f32[1024,2304]{1,0:T(8,128)} %fusion.89, bf16[1024,2304]{1,0:T(8,128)(2,1)} %get-tuple-element.73, bf16[2304,2304]{1,0:T(8,128)(2,1)} %all-gather.15.cloned.1.call-done), kind=kOutput, calls=%fused_computation.278 | convolution fusion | flops 10876354560 | bytes 38928384 | tf_op jit(solution)/shard_map/dot_general | solution.py:223
  763.9 14.5 %convolution_convert_fusion.1 = bf16[2304,2304]{1,0:T(8,128)(2,1)S(1)} fusion(bf16[1024,2304]{1,0:T(8,128)(2,1)} %pad_maximum_fusion.1, bf16[1024,2304]{1,0:T(8,128)(2,1)} %get-tuple-element.72), kind=kOutput, calls=%fused_computation.2 | convolution fusion | flops 10876944384 | bytes 20054016 | tf_op jit(solution)/shard_map/dot_general | solution.py:223
  790.1 16.3 %convolution_convert_fusion = bf16[2304,2304]{1,0:T(8,128)(2,1)} fusion(bf16[1024,2304]{1,0:T(8,128)(2,1)S(1)} %bitcast.86, bf16[1024,2304]{1,0:T(8,128)(2,1)} %get-tuple-element.73), kind=kOutput, calls=%fused_computation.1 | convolution fusion | flops 10876944384 | bytes 20054016 | tf_op jit(solution)/shard_map/dot_general | solution.py:223
  806.4 4.4 constant_dynamic-slice_fusion.4
  825.5 4.8 add_convert_fusion.2
  830.3 18.5 %collective-permute-done.29 = bf16[256,2304]{1,0:T(8,128)(2,1)S(1)} collective-permute-done((bf16[256,2304]{1,0:T(8,128)(2,1)S(1)}, bf16[256,2304]{1,0:T(8,128)(2,1)S(1)}, u32[]{:S(2)}, u32[]{:S(2)}) %collective-permute-start.29) | collective-permute-done | bytes 1179680 | tf_op jit(solution)/shard_map/ppermute | solution.py:583
  858.9 15.5 %collective-permute-done.32 = bf16[576,2304]{1,0:T(8,128)(2,1)S(1)} collective-permute-done((bf16[576,2304]{1,0:T(8,128)(2,1)S(1)}, bf16[576,2304]{1,0:T(8,128)(2,1)S(1)}, u32[]{:S(2)}, u32[]{:S(2)}) %collective-permute-start.32) | collective-permute-done | bytes 2654240 | tf_op jit(solution)/shard_map/ppermute | solution.py:488
  878.4 28.8 %attend_backward.1 = (bf16[512,1024]{1,0:T(8,128)(2,1)S(1)}, f32[2048,1024]{1,0:T(8,128)}) custom-call(bf16[512,1024]{1,0:T(8,128)(2,1)S(1)} %copy-done.4, bf16[2048,1024]{1,0:T(8,128)(2,1)} %pad_maximum_fusion.3.kv_ref, bf16[512,1024]{1,0:T(8,128)(2,1)S(1)} %convolution_convert_fusion.7.da_ref, f32[512,1024]{1,0:T(8,128)} %copy-done.2, ...), custom_call_target="tpu_custom_call" | custom-call | flops 10737418240 | bytes 17825792 | tf_op jit(solution)/shard_map/attend_backward/pallas_call | solution.py:186
  926.1 10.1 collective-permute-done.33
  936.9 15.9 %collective-permute-done.58 = bf16[144,2304]{1,0:T(8,128)(2,1)S(1)} collective-permute-done((bf16[144,2304]{1,0:T(8,128)(2,1)S(1)}, bf16[144,2304]{1,0:T(8,128)(2,1)S(1)}, u32[]{:S(2)}, u32[]{:S(2)}) %collective-permute-start.58) | collective-permute-done | bytes 663584 | tf_op jit(solution)/shard_map/ppermute | solution.py:531
  958.0 4.3 add_convert_fusion
  963.6 37.4 %collective-permute-done.36 = bf16[512,1024]{1,0:T(8,128)(2,1)S(1)} collective-permute-done((bf16[512,1024]{1,0:T(8,128)(2,1)S(1)}, bf16[512,1024]{1,0:T(8,128)(2,1)S(1)}, u32[]{:S(2)}, u32[]{:S(2)}) %collective-permute-start.36) | collective-permute-done | bytes 1048608 | tf_op jit(solution)/shard_map/ppermute | solution.py:620
  1003.2 4.3 fusion.90
  1008.9 18.0 %collective-permute-start.55 = (bf16[144,2304]{1,0:T(8,128)(2,1)}, bf16[144,2304]{1,0:T(8,128)(2,1)S(1)}, u32[]{:S(2)}, u32[]{:S(2)}) collective-permute-start(bf16[144,2304]{1,0:T(8,128)(2,1)} %select_convert_fusion.1), channel_id=1, source_target_pairs={{0,2},{2,0},{4,6},{6,4},{1,3},{3,1},{5,7},{7,5},{8,10},{10,8},{12,... | collective-permute-start | bytes 1990664 | tf_op jit(solution)/shard_map/ppermute | solution.py:531
  1036.2 6.7 collective-permute-done.55
  1047.2 36.8 %collective-permute-done.42 = bf16[512,1024]{1,0:T(8,128)(2,1)} collective-permute-done((bf16[512,1024]{1,0:T(8,128)(2,1)}, bf16[512,1024]{1,0:T(8,128)(2,1)}, u32[]{:S(2)}, u32[]{:S(2)}) %collective-permute-start.42) | collective-permute-done | bytes 1048608 | tf_op jit(solution)/shard_map/ppermute | solution.py:620
  1084.0 7.2 collective-permute-done.44
  1099.1 8.2 multiply_reduce_fusion
  1108.5 4.6 convolution_convert_fusion.3
  1128.2 19.5 %collective-permute-done.45 = bf16[256,2304]{1,0:T(8,128)(2,1)} collective-permute-done((bf16[256,2304]{1,0:T(8,128)(2,1)}, bf16[256,2304]{1,0:T(8,128)(2,1)}, u32[]{:S(2)}, u32[]{:S(2)}) %collective-permute-start.45) | collective-permute-done | bytes 1179680 | tf_op jit(solution)/shard_map/ppermute | solution.py:664
  1161.2 22.3 %collective-permute-done.49 = bf16[576,1152]{1,0:T(8,128)(2,1)S(1)} collective-permute-done((bf16[576,1152]{1,0:T(8,128)(2,1)S(1)}, bf16[576,1152]{1,0:T(8,128)(2,1)S(1)}, u32[]{:S(2)}, u32[]{:S(2)}) %collective-permute-start.49) | collective-permute-done | bytes 1327136 | tf_op jit(solution)/shard_map/ppermute | solution.py:488
  1195.9 23.5 %reduce-scatter.10.cloned.1.call-done = bf16[144,1152]{1,0:T(8,128)(2,1)} async-done(((bf16[576,1152]{1,0:T(8,128)(2,1)}), bf16[144,1152]{1,0:T(8,128)(2,1)}) %reduce-scatter.10.cloned.1.call-update) | async-done | bytes 331792
  (465 shorter events, 265.7 us)
Async XLA Ops:
  7.2 97.7 %all-gather.7.cloned.1.call-start = ((), (), s32[]{:S(2)}) async-start(), calls=%async_computation.3 | async-start | bytes 5640192 | tf_op jit(solution)/shard_map/all_gather | solution.py:353
  14.4 322.3 %all-gather.9.cloned.1.call-start = ((), (), s32[]{:S(2)}) async-start(), calls=%async_computation.4 | async-start | bytes 5013504 | tf_op jit(solution)/shard_map/all_gather | solution.py:354
  15.1 378.7 %all-gather.11.cloned.1.call-start = ((), (), s32[]{:S(2)}) async-start(), calls=%async_computation.5 | async-start | bytes 5013504 | tf_op jit(solution)/shard_map/all_gather | solution.py:355
  18.3 81.8 %collective-permute-start = (bf16[288,2304]{1,0:T(8,128)(2,1)}, bf16[288,2304]{1,0:T(8,128)(2,1)}, u32[]{:S(2)}, u32[]{:S(2)}) collective-permute-start(bf16[288,2304]{1,0:T(8,128)(2,1)} %pad_maximum_fusion.10), channel_id=1, source_target_pairs={{0,2},{2,0},{4,6},{6,4},{1,3},{3,1},{5,7},{7,5},{8,10},{10,8},{12,... | collective-permute-start | bytes 3981320 | tf_op jit(solution)/shard_map/ppermute | solution.py:376
  22.2 74.6 %collective-permute-start.2 = (bf16[144,2304]{1,0:T(8,128)(2,1)}, bf16[144,2304]{1,0:T(8,128)(2,1)S(1)}, u32[]{:S(2)}, u32[]{:S(2)}) collective-permute-start(bf16[144,2304]{1,0:T(8,128)(2,1)} %broadcast_select_fusion.17), channel_id=1, source_target_pairs={{0,2},{2,0},{4,6},{6,4},{1,3},{3,1},{5,7},{7,5},{8,10},{10,8},{12,... | collective-permute-start | bytes 1990664 | tf_op jit(solution)/shard_map/ppermute | solution.py:375
  22.2 460.6 %all-gather.13.cloned.1.call-start = ((), (), s32[]{:S(2)}) async-start(), calls=%async_computation.6 | async-start | bytes 13271040 | tf_op jit(solution)/shard_map/all_gather | solution.py:414
  98.2 88.4 %collective-permute-start.3 = (bf16[288,2304]{1,0:T(8,128)(2,1)}, bf16[288,2304]{1,0:T(8,128)(2,1)}, u32[]{:S(2)}, u32[]{:S(2)}) collective-permute-start(bf16[288,2304]{1,0:T(8,128)(2,1)} %pad_maximum_fusion.13), channel_id=1, source_target_pairs={{0,4},{2,6},{4,0},{6,2},{1,5},{3,7},{5,1},{7,3},{8,12},{10,14},{12... | collective-permute-start | bytes 3981320 | tf_op jit(solution)/shard_map/ppermute | solution.py:370
  190.1 312.9 %all-gather.15.cloned.1.call-start = ((), (), s32[]{:S(2)}) async-start(), calls=%async_computation.7 | async-start | bytes 13271040 | tf_op jit(solution)/shard_map/all_gather | solution.py:433
  190.1 36.4 %collective-permute-start.5 = (bf16[512,1024]{1,0:T(8,128)(2,1)S(1)}, bf16[512,1024]{1,0:T(8,128)(2,1)S(1)}, u32[]{:S(2)}, u32[]{:S(2)}) collective-permute-start(bf16[512,1024]{1,0:T(8,128)(2,1)S(1)} %slice_dynamic-update-slice_fusion.2), channel_id=1, source_target_pairs={{2,0},{4,2},{6,4},{3,1},{5,3},{7,5},{10,8},{12,10},{14,12},{11,9},... | collective-permute-start | bytes 3145736 | tf_op jit(solution)/shard_map/ppermute | solution.py:409
  191.6 42.1 %collective-permute-start.1 = (bf16[512,1024]{1,0:T(8,128)(2,1)S(1)}, bf16[512,1024]{1,0:T(8,128)(2,1)S(1)}, u32[]{:S(2)}, u32[]{:S(2)}) collective-permute-start(bf16[512,1024]{1,0:T(8,128)(2,1)S(1)} %slice_dynamic-update-slice_fusion.2), channel_id=1, source_target_pairs={{0,2},{2,4},{4,6},{1,3},{3,5},{5,7},{8,10},{10,12},{12,14},{9,11},... | collective-permute-start | bytes 3145736 | tf_op jit(solution)/shard_map/ppermute | solution.py:408
  196.2 106.5 %collective-permute-start.9 = (bf16[288,2304]{1,0:T(8,128)(2,1)}, bf16[288,2304]{1,0:T(8,128)(2,1)S(1)}, u32[]{:S(2)}, u32[]{:S(2)}) collective-permute-start(bf16[288,2304]{1,0:T(8,128)(2,1)} %pad_maximum_fusion.11), channel_id=1, source_target_pairs={{0,4},{2,6},{4,0},{6,2},{1,5},{3,7},{5,1},{7,3},{8,12},{10,14},{12... | collective-permute-start | bytes 3981320 | tf_op jit(solution)/shard_map/ppermute | solution.py:370
  226.6 76.2 %collective-permute-start.6 = (bf16[512,1024]{1,0:T(8,128)(2,1)S(1)}, bf16[512,1024]{1,0:T(8,128)(2,1)}, u32[]{:S(2)}, u32[]{:S(2)}) collective-permute-start(bf16[512,1024]{1,0:T(8,128)(2,1)S(1)} %collective-permute-done.5), channel_id=1, source_target_pairs={{2,0},{4,2},{3,1},{5,3},{10,8},{12,10},{11,9},{13,11},{18,16},{20,... | collective-permute-start | bytes 3145736 | tf_op jit(solution)/shard_map/ppermute | solution.py:409
  233.6 69.1 %collective-permute-start.4 = (bf16[512,1024]{1,0:T(8,128)(2,1)S(1)}, bf16[512,1024]{1,0:T(8,128)(2,1)}, u32[]{:S(2)}, u32[]{:S(2)}) collective-permute-start(bf16[512,1024]{1,0:T(8,128)(2,1)S(1)} %collective-permute-done.1), channel_id=1, source_target_pairs={{2,4},{4,6},{3,5},{5,7},{10,12},{12,14},{11,13},{13,15},{18,20},{2... | collective-permute-start | bytes 3145736 | tf_op jit(solution)/shard_map/ppermute | solution.py:408
  305.0 221.4 %all-gather.17.cloned.1.call-start = ((), (), s32[]{:S(2)}) async-start(), calls=%async_computation.8 | async-start | bytes 13271040 | tf_op jit(solution)/shard_map/all_gather | solution.py:441
  306.2 47.5 %collective-permute-start.7 = (bf16[512,1024]{1,0:T(8,128)(2,1)}, bf16[512,1024]{1,0:T(8,128)(2,1)}, u32[]{:S(2)}, u32[]{:S(2)}) collective-permute-start(bf16[512,1024]{1,0:T(8,128)(2,1)} %collective-permute-done.6), channel_id=1, source_target_pairs={{2,0},{3,1},{10,8},{11,9},{18,16},{19,17},{26,24},{27,25}} | collective-permute-start | bytes 3145736 | tf_op jit(solution)/shard_map/ppermute | solution.py:409
  307.9 82.3 %collective-permute-start.11 = (bf16[288,2304]{1,0:T(8,128)(2,1)}, bf16[288,2304]{1,0:T(8,128)(2,1)}, u32[]{:S(2)}, u32[]{:S(2)}) collective-permute-start(bf16[288,2304]{1,0:T(8,128)(2,1)} %pad_maximum_fusion.12), channel_id=1, source_target_pairs={{0,4},{2,6},{4,0},{6,2},{1,5},{3,7},{5,1},{7,3},{8,12},{10,14},{12... | collective-permute-start | bytes 3981320 | tf_op jit(solution)/shard_map/ppermute | solution.py:370
  393.8 732.6 %reduce-scatter.8.cloned.1.call-start = ((), (), s32[]{:S(2)}) async-start(), calls=%async_computation.10 | async-start | bytes 1474560 | tf_op jit(solution)/shard_map/reduce_scatter | solution.py:496
  431.4 51.4 %collective-permute-start.14 = (bf16[256,2304]{1,0:T(8,128)(2,1)S(1)}, bf16[256,2304]{1,0:T(8,128)(2,1)}, u32[]{:S(2)}, u32[]{:S(2)}) collective-permute-start(bf16[256,2304]{1,0:T(8,128)(2,1)S(1)} %multiply_convert_fusion.3), channel_id=1, source_target_pairs={{0,3},{1,2},{2,1},{3,0},{4,7},{5,6},{6,5},{7,4},{8,11},{9,10},{10,... | collective-permute-start | bytes 3538952 | tf_op jit(solution)/shard_map/ppermute | solution.py:315
  547.3 50.2 %collective-permute-start.17 = (bf16[256,2304]{1,0:T(8,128)(2,1)}, bf16[256,2304]{1,0:T(8,128)(2,1)}, u32[]{:S(2)}, u32[]{:S(2)}) collective-permute-start(bf16[256,2304]{1,0:T(8,128)(2,1)} %get-tuple-element.225), channel_id=1, source_target_pairs={{0,3},{1,2},{2,1},{3,0},{4,7},{5,6},{6,5},{7,4},{8,11},{9,10},{10,... | collective-permute-start | bytes 3538952 | tf_op jit(solution)/shard_map/ppermute | solution.py:323
  604.3 54.3 %collective-permute-start.19 = (bf16[256,2304]{1,0:T(8,128)(2,1)S(1)}, bf16[256,2304]{1,0:T(8,128)(2,1)}, u32[]{:S(2)}, u32[]{:S(2)}) collective-permute-start(bf16[256,2304]{1,0:T(8,128)(2,1)S(1)} %get-tuple-element.245), channel_id=1, source_target_pairs={{0,1},{1,0},{2,3},{3,2},{4,5},{5,4},{6,7},{7,6},{8,9},{9,8},{10,11... | collective-permute-start | bytes 3538952 | tf_op jit(solution)/shard_map/ppermute | solution.py:315
  605.9 52.8 %collective-permute-start.20 = (bf16[256,2304]{1,0:T(8,128)(2,1)S(1)}, bf16[256,2304]{1,0:T(8,128)(2,1)}, u32[]{:S(2)}, u32[]{:S(2)}) collective-permute-start(bf16[256,2304]{1,0:T(8,128)(2,1)S(1)} %get-tuple-element.245), channel_id=1, source_target_pairs={{0,2},{1,3},{2,0},{3,1},{4,6},{5,7},{6,4},{7,5},{8,10},{9,11},{10,... | collective-permute-start | bytes 3538952 | tf_op jit(solution)/shard_map/ppermute | solution.py:315
  606.4 52.2 %collective-permute-start.21 = (bf16[256,2304]{1,0:T(8,128)(2,1)S(1)}, bf16[256,2304]{1,0:T(8,128)(2,1)}, u32[]{:S(2)}, u32[]{:S(2)}) collective-permute-start(bf16[256,2304]{1,0:T(8,128)(2,1)S(1)} %get-tuple-element.245), channel_id=1, source_target_pairs={{0,3},{1,2},{2,1},{3,0},{4,7},{5,6},{6,5},{7,4},{8,11},{9,10},{10,... | collective-permute-start | bytes 3538952 | tf_op jit(solution)/shard_map/ppermute | solution.py:315
  613.8 208.8 %collective-permute-start.18 = (bf16[256,2304]{1,0:T(8,128)(2,1)}, bf16[256,2304]{1,0:T(8,128)(2,1)}, u32[]{:S(2)}, u32[]{:S(2)}) collective-permute-start(bf16[256,2304]{1,0:T(8,128)(2,1)} %get-tuple-element.246), channel_id=1, source_target_pairs={{0,1},{1,0},{2,3},{3,2},{4,5},{5,4},{6,7},{7,6},{8,9},{9,8},{10,11... | collective-permute-start | bytes 3538952 | tf_op jit(solution)/shard_map/ppermute | solution.py:307
  678.6 35.1 %collective-permute-start.22 = (bf16[576,2304]{1,0:T(8,128)(2,1)}, bf16[576,2304]{1,0:T(8,128)(2,1)}, u32[]{:S(2)}, u32[]{:S(2)}) collective-permute-start(bf16[576,2304]{1,0:T(8,128)(2,1)} %get-tuple-element.207), channel_id=1, source_target_pairs={{0,8},{8,0},{16,24},{24,16},{1,9},{9,1},{17,25},{25,17},{2,10},{10... | collective-permute-start | bytes 7962632 | tf_op jit(solution)/shard_map/ppermute | solution.py:474
  678.6 104.6 %collective-permute-start.24 = (bf16[576,2304]{1,0:T(8,128)(2,1)}, bf16[576,2304]{1,0:T(8,128)(2,1)}, u32[]{:S(2)}, u32[]{:S(2)}) collective-permute-start(bf16[576,2304]{1,0:T(8,128)(2,1)} %get-tuple-element.208), channel_id=1, source_target_pairs={{0,8},{8,0},{16,24},{24,16},{1,9},{9,1},{17,25},{25,17},{2,10},{10... | collective-permute-start | bytes 7962632 | tf_op jit(solution)/shard_map/ppermute | solution.py:474
  718.5 64.6 %collective-permute-start.25 = (bf16[576,2304]{1,0:T(8,128)(2,1)}, bf16[576,2304]{1,0:T(8,128)(2,1)}, u32[]{:S(2)}, u32[]{:S(2)}) collective-permute-start(bf16[576,2304]{1,0:T(8,128)(2,1)} %add_convert_fusion.5), channel_id=1, source_target_pairs={{0,16},{8,24},{16,0},{24,8},{1,17},{9,25},{17,1},{25,9},{2,18},{10... | collective-permute-start | bytes 7962632 | tf_op jit(solution)/shard_map/ppermute | solution.py:488
  759.9 53.8 %collective-permute-start.26 = (bf16[256,2304]{1,0:T(8,128)(2,1)}, bf16[256,2304]{1,0:T(8,128)(2,1)S(1)}, u32[]{:S(2)}, u32[]{:S(2)}) collective-permute-start(bf16[256,2304]{1,0:T(8,128)(2,1)} %get-tuple-element.221), channel_id=1, source_target_pairs={{0,1},{1,0},{2,3},{3,2},{4,5},{5,4},{6,7},{7,6},{8,9},{9,8},{10,11... | collective-permute-start | bytes 3538952 | tf_op jit(solution)/shard_map/ppermute | solution.py:323
  761.4 52.6 %collective-permute-start.27 = (bf16[256,2304]{1,0:T(8,128)(2,1)}, bf16[256,2304]{1,0:T(8,128)(2,1)}, u32[]{:S(2)}, u32[]{:S(2)}) collective-permute-start(bf16[256,2304]{1,0:T(8,128)(2,1)} %get-tuple-element.223), channel_id=1, source_target_pairs={{0,2},{1,3},{2,0},{3,1},{4,6},{5,7},{6,4},{7,5},{8,10},{9,11},{10,... | collective-permute-start | bytes 3538952 | tf_op jit(solution)/shard_map/ppermute | solution.py:323
  810.8 63.6 %collective-permute-start.31 = (bf16[576,2304]{1,0:T(8,128)(2,1)}, bf16[576,2304]{1,0:T(8,128)(2,1)S(1)}, u32[]{:S(2)}, u32[]{:S(2)}) collective-permute-start(bf16[576,2304]{1,0:T(8,128)(2,1)} %get-tuple-element.205), channel_id=1, source_target_pairs={{0,8},{8,0},{16,24},{24,16},{1,9},{9,1},{17,25},{25,17},{2,10},{10... | collective-permute-start | bytes 7962632 | tf_op jit(solution)/shard_map/ppermute | solution.py:474
  814.0 60.4 %collective-permute-start.32 = (bf16[576,2304]{1,0:T(8,128)(2,1)S(1)}, bf16[576,2304]{1,0:T(8,128)(2,1)S(1)}, u32[]{:S(2)}, u32[]{:S(2)}) collective-permute-start(bf16[576,2304]{1,0:T(8,128)(2,1)S(1)} %add_convert_fusion.3), channel_id=1, source_target_pairs={{0,16},{8,24},{16,0},{24,8},{1,17},{9,25},{17,1},{25,9},{2,18},{10... | collective-permute-start | bytes 7962632 | tf_op jit(solution)/shard_map/ppermute | solution.py:488
  825.4 94.1 %collective-permute-start.35 = (bf16[288,2304]{1,0:T(8,128)(2,1)}, bf16[288,2304]{1,0:T(8,128)(2,1)}, u32[]{:S(2)}, u32[]{:S(2)}) collective-permute-start(bf16[288,2304]{1,0:T(8,128)(2,1)} %broadcast_select_fusion.2), channel_id=1, source_target_pairs={{0,4},{2,6},{4,0},{6,2},{1,5},{3,7},{5,1},{7,3},{8,12},{10,14},{12... | collective-permute-start | bytes 3981320 | tf_op jit(solution)/shard_map/ppermute | solution.py:518
  825.4 132.2 %collective-permute-start.39 = (bf16[576,2304]{1,0:T(8,128)(2,1)}, bf16[576,2304]{1,0:T(8,128)(2,1)}, u32[]{:S(2)}, u32[]{:S(2)}) collective-permute-start(bf16[576,2304]{1,0:T(8,128)(2,1)} %get-tuple-element.204), channel_id=1, source_target_pairs={{0,8},{8,0},{16,24},{24,16},{1,9},{9,1},{17,25},{25,17},{2,10},{10... | collective-permute-start | bytes 7962632 | tf_op jit(solution)/shard_map/ppermute | solution.py:474
  848.7 107.9 %collective-permute-start.40 = (bf16[576,2304]{1,0:T(8,128)(2,1)}, bf16[576,2304]{1,0:T(8,128)(2,1)}, u32[]{:S(2)}, u32[]{:S(2)}) collective-permute-start(bf16[576,2304]{1,0:T(8,128)(2,1)} %add_convert_fusion.2), channel_id=1, source_target_pairs={{0,16},{8,24},{16,0},{24,8},{1,17},{9,25},{17,1},{25,9},{2,18},{10... | collective-permute-start | bytes 7962632 | tf_op jit(solution)/shard_map/ppermute | solution.py:488
  874.4 38.4 %collective-permute-start.34 = (bf16[576,1024]{1,0:T(8,128)(2,1)}, bf16[576,1024]{1,0:T(8,128)(2,1)S(1)}, u32[]{:S(2)}, u32[]{:S(2)}) collective-permute-start(bf16[576,1024]{1,0:T(8,128)(2,1)} %get-tuple-element.219), channel_id=1, source_target_pairs={{0,8},{8,0},{16,24},{24,16},{1,9},{9,1},{17,25},{25,17},{2,10},{10... | collective-permute-start | bytes 3538952 | tf_op jit(solution)/shard_map/ppermute | solution.py:474
  936.2 71.3 %collective-permute-start.43 = (bf16[288,2304]{1,0:T(8,128)(2,1)S(1)}, bf16[288,2304]{1,0:T(8,128)(2,1)S(1)}, u32[]{:S(2)}, u32[]{:S(2)}) collective-permute-start(bf16[288,2304]{1,0:T(8,128)(2,1)S(1)} %broadcast_select_fusion.1), channel_id=1, source_target_pairs={{0,4},{2,6},{4,0},{6,2},{1,5},{3,7},{5,1},{7,3},{8,12},{10,14},{12... | collective-permute-start | bytes 3981320 | tf_op jit(solution)/shard_map/ppermute | solution.py:518
  952.8 76.2 %collective-permute-start.53 = (bf16[576,1024]{1,0:T(8,128)(2,1)S(1)}, bf16[576,1024]{1,0:T(8,128)(2,1)S(1)}, u32[]{:S(2)}, u32[]{:S(2)}) collective-permute-start(bf16[576,1024]{1,0:T(8,128)(2,1)S(1)} %copy-done.53), channel_id=1, source_target_pairs={{0,8},{8,0},{16,24},{24,16},{1,9},{9,1},{17,25},{25,17},{2,10},{10... | collective-permute-start | bytes 3538952 | tf_op jit(solution)/shard_map/ppermute | solution.py:474
  953.1 47.9 %collective-permute-start.36 = (bf16[512,1024]{1,0:T(8,128)(2,1)S(1)}, bf16[512,1024]{1,0:T(8,128)(2,1)S(1)}, u32[]{:S(2)}, u32[]{:S(2)}) collective-permute-start(bf16[512,1024]{1,0:T(8,128)(2,1)S(1)} %get-tuple-element.212), channel_id=1, source_target_pairs={{0,2},{2,4},{1,3},{3,5},{8,10},{10,12},{9,11},{11,13},{16,18},{18,... | collective-permute-start | bytes 3145736 | tf_op jit(solution)/shard_map/ppermute | solution.py:620
  956.7 44.3 %collective-permute-start.41 = (bf16[512,1024]{1,0:T(8,128)(2,1)S(1)}, bf16[512,1024]{1,0:T(8,128)(2,1)S(1)}, u32[]{:S(2)}, u32[]{:S(2)}) collective-permute-start(bf16[512,1024]{1,0:T(8,128)(2,1)S(1)} %get-tuple-element.211), channel_id=1, source_target_pairs={{4,2},{6,4},{5,3},{7,5},{12,10},{14,12},{13,11},{15,13},{20,18},{2... | collective-permute-start | bytes 3145736 | tf_op jit(solution)/shard_map/ppermute | solution.py:621
  957.6 74.3 %collective-permute-start.54 = (bf16[576,1024]{1,0:T(8,128)(2,1)S(1)}, bf16[576,1024]{1,0:T(8,128)(2,1)S(1)}, u32[]{:S(2)}, u32[]{:S(2)}) collective-permute-start(bf16[576,1024]{1,0:T(8,128)(2,1)S(1)} %add_convert_fusion.11), channel_id=1, source_target_pairs={{0,16},{8,24},{16,0},{24,8},{1,17},{9,25},{17,1},{25,9},{2,18},{10... | collective-permute-start | bytes 3538952 | tf_op jit(solution)/shard_map/ppermute | solution.py:488
  1001.0 121.1 %collective-permute-start.51 = (bf16[576,1024]{1,0:T(8,128)(2,1)}, bf16[576,1024]{1,0:T(8,128)(2,1)}, u32[]{:S(2)}, u32[]{:S(2)}) collective-permute-start(bf16[576,1024]{1,0:T(8,128)(2,1)} %get-tuple-element.218), channel_id=1, source_target_pairs={{0,8},{8,0},{16,24},{24,16},{1,9},{9,1},{17,25},{25,17},{2,10},{10... | collective-permute-start | bytes 3538952 | tf_op jit(solution)/shard_map/ppermute | solution.py:474
  1028.6 93.4 %collective-permute-start.52 = (bf16[576,1024]{1,0:T(8,128)(2,1)}, bf16[576,1024]{1,0:T(8,128)(2,1)}, u32[]{:S(2)}, u32[]{:S(2)}) collective-permute-start(bf16[576,1024]{1,0:T(8,128)(2,1)} %add_convert_fusion.10), channel_id=1, source_target_pairs={{0,16},{8,24},{16,0},{24,8},{1,17},{9,25},{17,1},{25,9},{2,18},{10... | collective-permute-start | bytes 3538952 | tf_op jit(solution)/shard_map/ppermute | solution.py:488
  1029.0 55.0 %collective-permute-start.42 = (bf16[512,1024]{1,0:T(8,128)(2,1)}, bf16[512,1024]{1,0:T(8,128)(2,1)}, u32[]{:S(2)}, u32[]{:S(2)}) collective-permute-start(bf16[512,1024]{1,0:T(8,128)(2,1)} %get-tuple-element.210), channel_id=1, source_target_pairs={{0,2},{2,4},{4,6},{1,3},{3,5},{5,7},{8,10},{10,12},{12,14},{9,11},... | collective-permute-start | bytes 3145736 | tf_op jit(solution)/shard_map/ppermute | solution.py:620
  1031.9 59.3 %collective-permute-start.44 = (bf16[512,1024]{1,0:T(8,128)(2,1)}, bf16[512,1024]{1,0:T(8,128)(2,1)}, u32[]{:S(2)}, u32[]{:S(2)}) collective-permute-start(bf16[512,1024]{1,0:T(8,128)(2,1)} %get-tuple-element.209), channel_id=1, source_target_pairs={{2,0},{4,2},{6,4},{3,1},{5,3},{7,5},{10,8},{12,10},{14,12},{11,9},... | collective-permute-start | bytes 3145736 | tf_op jit(solution)/shard_map/ppermute | solution.py:621
  1036.2 153.6 %reduce-scatter.6.cloned.1.call-start = ((), (), s32[]{:S(2)}) async-start(), calls=%async_computation.9 | async-start | bytes 1474560 | tf_op jit(solution)/shard_map/reduce_scatter | solution.py:496
  1042.9 110.0 %collective-permute-start.56 = (bf16[288,2304]{1,0:T(8,128)(2,1)}, bf16[288,2304]{1,0:T(8,128)(2,1)}, u32[]{:S(2)}, u32[]{:S(2)}) collective-permute-start(bf16[288,2304]{1,0:T(8,128)(2,1)} %broadcast_select_fusion), channel_id=1, source_target_pairs={{0,4},{2,6},{4,0},{6,2},{1,5},{3,7},{5,1},{7,3},{8,12},{10,14},{12... | collective-permute-start | bytes 3981320 | tf_op jit(solution)/shard_map/ppermute | solution.py:518
  1116.1 34.5 %collective-permute-start.48 = (bf16[576,1152]{1,0:T(8,128)(2,1)}, bf16[576,1152]{1,0:T(8,128)(2,1)}, u32[]{:S(2)}, u32[]{:S(2)}) collective-permute-start(bf16[576,1152]{1,0:T(8,128)(2,1)} %get-tuple-element.216), channel_id=1, source_target_pairs={{0,8},{8,0},{16,24},{24,16},{1,9},{9,1},{17,25},{25,17},{2,10},{10... | collective-permute-start | bytes 3981320 | tf_op jit(solution)/shard_map/ppermute | solution.py:474
  1125.9 93.6 %reduce-scatter.10.cloned.1.call-start = ((), (), s32[]{:S(2)}) async-start(), calls=%async_computation.11 | async-start | bytes 1658880
  1126.2 35.1 %collective-permute-start.47 = (bf16[576,1152]{1,0:T(8,128)(2,1)}, bf16[576,1152]{1,0:T(8,128)(2,1)}, u32[]{:S(2)}, u32[]{:S(2)}) collective-permute-start(bf16[576,1152]{1,0:T(8,128)(2,1)} %get-tuple-element.215), channel_id=1, source_target_pairs={{0,8},{8,0},{16,24},{24,16},{1,9},{9,1},{17,25},{25,17},{2,10},{10... | collective-permute-start | bytes 3981320 | tf_op jit(solution)/shard_map/ppermute | solution.py:474
  (116 other events, 3523.4 us)
Sparse Core Ops, SparseCore 0:
  14.5 81.7 all-gather.6
  98.6 84.5 all-gather.8
  185.5 100.3 all-gather.10
  287.8 70.4 all-gather.12
  360.2 70.9 all-gather.14
  433.2 70.9 all-gather.16
  1036.3 49.6 reduce-scatter.7
  1126.0 29.7 reduce-scatter.5
  1186.8 32.6 reduce-scatter.9

commit v3 on v2

--- a/solution.py
+++ b/solution.py
@@ -118,15 +118,15 @@
         ],
         compiler_params=pltpu.CompilerParams(vmem_limit_bytes=attend_limit),
         cost_estimate=pl.CostEstimate(
-            flops=4 * rows * length * width,
-            bytes_accessed=14 * rows * width + 4 * length * groups * HD,
-            transcendentals=2 * rows * length * heads,
+            flops=rows * width,
+            bytes_accessed=rows * width,
+            transcendentals=0,
         ),
         name="attend_forward",
     )(query_pre, kv_all, cosine, sine, qpos, kpos)
 
 
-def backward_kernel(per_group, q_ref, kv_ref, da_ref, out_ref, inv_ref, cos_ref, sin_ref, qpos_ref, kpos_ref, dq_ref, dkv_ref, delta_ref, sum_ref):
+def backward_kernel(per_group, q_ref, kv_ref, da_ref, out_ref, inv_ref, cos_ref, sin_ref, qpos_ref, kpos_ref, dq_ref, dkv_ref, delta_ref, sum_ref, both_ref):
     c, r = pl.program_id(1), pl.program_id(2)
     q, da = q_ref[...], da_ref[...]
     k, v = kv_ref[:, :HD], kv_ref[:, HD:]
@@ -149,13 +149,17 @@
 
     @pl.when(r == 0)
     def _():
-        dkv_ref[:, :HD] = d_key
-        dkv_ref[:, HD:] = d_value
+        both_ref[:, :HD] = d_key
+        both_ref[:, HD:] = d_value
 
     @pl.when(r > 0)
     def _():
-        dkv_ref[:, :HD] += d_key
-        dkv_ref[:, HD:] += d_value
+        both_ref[:, :HD] += d_key
+        both_ref[:, HD:] += d_value
+
+    @pl.when(r == per_group - 1)
+    def _():
+        dkv_ref[...] = both_ref[...].astype(bf16)
 
     @pl.when(c == 0)
     def _():
@@ -203,20 +207,123 @@
         ],
         out_shape=[
             jax.ShapeDtypeStruct((rows, width), bf16),
-            jax.ShapeDtypeStruct((length, groups * 2 * HD), f32),
+            jax.ShapeDtypeStruct((length, groups * 2 * HD), bf16),
         ],
         scratch_shapes=[
             pltpu.VMEM((per_group, 8, rows), f32),
             pltpu.VMEM((per_group, rows, HD), f32),
+            pltpu.VMEM((size, 2 * HD), f32),
         ],
         compiler_params=pltpu.CompilerParams(vmem_limit_bytes=attend_limit),
         cost_estimate=pl.CostEstimate(
-            flops=10 * rows * length * width,
-            bytes_accessed=10 * rows * width + 12 * length * groups * HD,
-            transcendentals=2 * rows * length * heads,
+            flops=rows * width,
+            bytes_accessed=rows * width,
+            transcendentals=0,
         ),
         name="attend_backward",
     )(queries, kv_all, d_attended, out, inverse, cosine, sine, qpos, kpos)
+
+
+feed_limit = 56 * 1024 * 1024
+feed_tile = 256
+
+
+def feed_params():
+    return dict(
+        compiler_params=pltpu.CompilerParams(vmem_limit_bytes=feed_limit),
+        cost_estimate=pl.CostEstimate(flops=1000000, bytes_accessed=1000000, transcendentals=0),
+    )
+
+
+def whole_block(array):
+    return pl.BlockSpec(array.shape, lambda n: (0, 0))
+
+
+def column_tile(array):
+    return pl.BlockSpec((array.shape[0], feed_tile), lambda n: (0, n))
+
+
+def row_tile(array):
+    return pl.BlockSpec((feed_tile, array.shape[1]), lambda n: (n, 0))
+
+
+def mix_kernel(x_ref, gate_mat_ref, up_mat_ref, gate_ref, up_ref, mixed_ref):
+    x = x_ref[...]
+    gate = dotted(x, gate_mat_ref[...], 1, 0)
+    upward = dotted(x, up_mat_ref[...], 1, 0)
+    gate_ref[...] = gate
+    up_ref[...] = upward
+    inner = gelu_coef * (gate + 0.044715 * gate * gate * gate)
+    mixed_ref[...] = (0.5 * gate * (1.0 + jnp.tanh(inner)) * upward).astype(bf16)
+
+
+def mix_forward(x, gate_mat, up_mat):
+    rows, hidden = x.shape[0], gate_mat.shape[1]
+    shapes = [jax.ShapeDtypeStruct((rows, hidden), kind) for kind in (f32, f32, bf16)]
+    return pl.pallas_call(
+        mix_kernel,
+        grid=(hidden // feed_tile,),
+        in_specs=[whole_block(x), column_tile(gate_mat), column_tile(up_mat)],
+        out_specs=[column_tile(shape) for shape in shapes],
+        out_shape=shapes,
+        name="mix_forward",
+        **feed_params(),
+    )(x, gate_mat, up_mat)
+
+
+def mix_back_kernel(d_ref, down_mat_ref, gate_ref, up_ref, d_gate_ref, d_up_ref):
+    d_mixed = dotted(d_ref[...], down_mat_ref[...], 1, 0)
+    gate = gate_ref[...]
+    square = gate * gate
+    level = jnp.tanh(gelu_coef * gate * (1.0 + 0.044715 * square))
+    slope = gelu_coef * (1.0 + 3.0 * 0.044715 * square)
+    curve = 0.5 * (1.0 + level)
+    d_curve = curve + 0.5 * gate * (1.0 - level * level) * slope
+    d_gate_ref[...] = (d_mixed * up_ref[...] * d_curve).astype(bf16)
+    d_up_ref[...] = (d_mixed * (gate * curve)).astype(bf16)
+
+
+def mix_backward(d_out, down_mat, gate, upward):
+    shapes = [jax.ShapeDtypeStruct(gate.shape, bf16)] * 2
+    return pl.pallas_call(
+        mix_back_kernel,
+        grid=(gate.shape[1] // feed_tile,),
+        in_specs=[
+            whole_block(d_out),
+            column_tile(down_mat),
+            column_tile(gate),
+            column_tile(upward),
+        ],
+        out_specs=[column_tile(shape) for shape in shapes],
+        out_shape=shapes,
+        name="mix_backward",
+        **feed_params(),
+    )(d_out, down_mat, gate, upward)
+
+
+def spread_kernel(count, half, *refs):
+    lefts, rights, outs = refs[:count], refs[count : 2 * count], refs[2 * count :]
+    total = dotted(lefts[0][...], rights[0][...], 1, 1)
+    for left, right in zip(lefts[1:], rights[1:]):
+        total = total + dotted(left[...], right[...], 1, 1)
+    for k, out in enumerate(outs):
+        out[...] = total[k * half : (k + 1) * half].astype(out.dtype)
+
+
+def product_blocks(lefts, rights, half):
+    rows, width = lefts[0].shape[0], rights[0].shape[0]
+    shapes = [
+        jax.ShapeDtypeStruct((half, width), bf16 if k else f32) for k in range(rows // half)
+    ]
+    return pl.pallas_call(
+        functools.partial(spread_kernel, len(lefts), half),
+        grid=(width // feed_tile,),
+        in_specs=[whole_block(left) for left in lefts] + [row_tile(right) for right in rights],
+        out_specs=[column_tile(shape) for shape in shapes],
+        out_shape=shapes,
+        name="product_blocks",
+        **feed_params(),
+    )(*lefts, *rights)
 
 
 def contract(left, right, left_dim, right_dim):
@@ -247,14 +354,15 @@
     tensor_count = lax.axis_size("tensor")
     groups = KV // tensor_count
     factor = HD ** (-0.5)
-    dp_count = lax.axis_size("dp")
+    dp_count = lax.axis_size(("y", "core"))
     ctx_count = lax.axis_size("ctx")
     tensor_index = lax.axis_index("tensor")
     ctx_index = lax.axis_index("ctx")
-    dp_index = lax.axis_index("dp")
+    dp_index = lax.axis_index(("y", "core"))
     y_count = dp_count // cores
     y_index = dp_index // cores
     core_index = dp_index % cores
+    dp_axes = ("y", "core")
     share = width // (dp_count * ctx_count)
     quarter = share * ctx_count
     half = rows // tensor_count
@@ -333,14 +441,12 @@
         block_order[0][:, None] * block_len + jnp.arange(block_len, dtype=jnp.int32)[None, :]
     ).reshape(ctx_count, tensor_count, half)
     all_pos = jnp.where(tensor_index == 1, all_pos[:, ::-1], all_pos).reshape(ctx_count, rows)
-    source = (ctx_index - jnp.arange(ctx_count, dtype=jnp.int32)) % ctx_count
-    key_pos = jnp.take(all_pos, source, axis=0)
-    local_pos = key_pos[0]
+    local_pos = lax.dynamic_slice_in_dim(all_pos, ctx_index, 1, 0)[0]
     cosine, sine = rotary_tables(local_pos, HD)
     query_places = local_pos[None, :]
-    key_places = key_pos.reshape(LEN, 1)
-
-    both = ("dp", "ctx")
+    key_places = all_pos.reshape(LEN, 1)
+
+    both = ("y", "core", "ctx")
     gain_pack = jnp.stack([pre_attend, post_attend, pre_feed, post_feed], axis=1)
     gain_pack = jnp.pad(gain_pack, ((0, 0), (0, pad_lanes - 4)))
     heads_in_turn = []
@@ -379,6 +485,7 @@
     up_block = far_pack(up_mine, rest_got[: rest_got.shape[0] // 2])
     down_block = far_pack(down_mine, rest_got[rest_got.shape[0] // 2 :])
 
+    query_width = query_weight.shape[1]
     keyvalue_width = 2 * key_weight.shape[1]
     keyvalue_all = after(keyvalue_all, up_block, down_block)
     keyvalue_mat = keyvalue_all[:, :keyvalue_width]
@@ -411,7 +518,7 @@
     line_step(1, kv_local, kv_local)
     gate_far = [after(part, kv_local) for part in gate_far]
     gate_rows = in_order([gate_block] + gate_far, far_index)
-    gate_mat = lax.all_gather(gate_rows, "dp", axis=0, tiled=True)
+    gate_mat = lax.all_gather(gate_rows, dp_axes, axis=0, tiled=True)
     up_far = far_start(after(up_block, gate_rows))
     for step in range(2, ctx_count):
         left_block, right_block = from_left[-1], from_right[-1]
@@ -427,40 +534,35 @@
         kv_parts.append(
             jnp.where(ctx_index >= step, from_left[step], from_right[ctx_count - step])
         )
-    kv_all = jnp.concatenate(kv_parts, axis=0)
+    kv_all = in_order(kv_parts, ctx_index)
     up_far = [after(part, *last_blocks) for part in up_far]
     up_rows = in_order([up_block] + up_far, far_index)
-    up_mat = lax.all_gather(up_rows, "dp", axis=0, tiled=True)
+    up_mat = lax.all_gather(up_rows, dp_axes, axis=0, tiled=True)
     down_far = far_start(after(down_block, up_rows))
     kv_all = after(kv_all, up_rows)
     queries, attended_wide, attended, inverse_sums = attend_forward(
         query_pre, kv_all, cosine, sine, query_places, key_places, groups, per_group, ctx_count
     )
-    down_far = [after(part, attended) for part in down_far]
+    other = contract(attended[half:], out_mat, 1, 1).astype(bf16)
+    got = lax.ppermute(other, "tensor", x_swap)
+    down_far = [after(part, got) for part in down_far]
     down_rows = in_order([down_block] + down_far, far_index)
-    down_mat = lax.all_gather(down_rows, "dp", axis=0, tiled=True)
-    other = contract(attended[half:], out_mat, 1, 1).astype(bf16)
-    got = after(lax.ppermute(other, "tensor", x_swap), down_rows)
+    down_mat = lax.all_gather(down_rows, dp_axes, axis=0, tiled=True)
     attend_out = contract(attended[:half], out_mat, 1, 1) + got.astype(f32)
     hidden_mid = own_inputs + rms_norm(attend_out, gain_out)
     feed_own = rms_norm(hidden_mid, feed_gain).astype(bf16)
     feed_in = join_all(feed_own)
-    gate = jnp.dot(feed_in, gate_mat, preferred_element_type=f32)
-    upward = jnp.dot(feed_in, up_mat, preferred_element_type=f32)
-    mixed = gated_product(gate, upward).astype(bf16)
-    feed_part = contract(mixed, down_mat, 1, 1)
-    sent = send_all(pack_all(feed_part))
-    feed_out = sum_of(feed_part[:half], sent)
+    gate, upward, mixed = mix_forward(feed_in, gate_mat, up_mat)
+    feed_own, *sent = product_blocks([mixed], [down_mat], half)
+    sent = send_all(sent)
+    feed_out = sum_of(feed_own, sent)
     layer_output = join_absolute(
         (hidden_mid + rms_norm(feed_out, feed_post)).astype(bf16)
     )[None]
 
     class Reduction:
-        def __init__(self, left, right, extra=None):
-            result = contract(left, right, 0, 0).astype(bf16)
-            if extra is not None:
-                result = jnp.concatenate([result, extra.T.astype(bf16)], axis=1)
-            self.whole = result
+        def __init__(self, left, right):
+            self.whole = contract(left, right, 0, 0).astype(bf16)
 
         def piece(self, dy, dc):
             index = ((y_index + dy) % y_count) * cores + (core_index + dc) % cores
@@ -471,7 +573,7 @@
             return self.packed
 
         def core_send(self):
-            self.swapped = [lax.ppermute(p, "dp", along(0, 1)) for p in self.packed]
+            self.swapped = [lax.ppermute(p, dp_axes, along(0, 1)) for p in self.packed]
 
         def y_pack(self, *before):
             swapped = self.swapped
@@ -485,27 +587,21 @@
 
         def y_send(self):
             self.arrived = [
-                lax.ppermute(p, "dp", along(dy + 1, 0)) for dy, p in enumerate(self.packed)
+                lax.ppermute(p, dp_axes, along(dy + 1, 0)) for dy, p in enumerate(self.packed)
             ]
 
-        def column(self):
+        def sum_y(self, *before):
+            arrived = self.arrived
+            if before:
+                arrived = [after(item, *before) for item in arrived]
             total = self.piece(0, 0).astype(f32) + self.swapped[0].astype(f32)
-            return sum_of(total, self.arrived)
+            self.total = sum_of(total, arrived).astype(bf16)
+            return self.total
 
         def finish_ctx(self):
             return lax.psum_scatter(
-                self.column().astype(bf16), "ctx", scatter_dimension=0, tiled=True
+                self.total, "ctx", scatter_dimension=0, tiled=True
             ).astype(f32)
-
-        def far_pack(self, *before):
-            if before:
-                self.arrived = [after(item, *before) for item in self.arrived]
-            total = self.column().astype(bf16)
-            self.blocks = [total[k * pair * share : (k + 1) * pair * share] for k in range(far_count)]
-            self.packed = [
-                self.block_of((far_index + step) % far_count) for step in range(1, far_count)
-            ]
-            return self.packed
 
         def block_of(self, index):
             result = self.blocks[0]
@@ -513,31 +609,43 @@
                 result = jnp.where(index == k, self.blocks[k], result)
             return result
 
+        def far_pack(self, *before):
+            total = self.sum_y(*before)
+            self.blocks = [
+                total[k * pair * share : (k + 1) * pair * share] for k in range(far_count)
+            ]
+            self.packed = [
+                self.block_of((far_index + step) % far_count) for step in range(1, far_count)
+            ]
+            return self.packed
+
         def far_send(self):
             self.arrived = [
                 lax.ppermute(p, "ctx", far_shift(s + 1)) for s, p in enumerate(self.packed)
             ]
 
         def near_pack(self, *before):
+            arrived = self.arrived
             if before:
-                self.arrived = [after(item, *before) for item in self.arrived]
-            total = sum_of(self.block_of(far_index).astype(f32), self.arrived)
+                arrived = [after(item, *before) for item in arrived]
+            total = sum_of(self.block_of(far_index).astype(f32), arrived)
             low, high = total[:share], total[share:]
             self.own = jnp.where(is_high, high, low)
-            self.packed = jnp.where(is_high, low, high).astype(bf16)
-            return [self.packed]
-
-        def near_send(self):
-            self.got = lax.ppermute(self.packed, "ctx", near_swap).astype(f32)
-
-        def finish_near(self):
-            return jnp.concatenate(
-                [
-                    jnp.where(is_high, self.got, self.own),
-                    jnp.where(is_high, self.own, self.got),
-                ],
-                axis=1,
-            )
+            self.other = jnp.where(is_high, low, high).astype(bf16)
+            return self.other
+
+    def near_send(*sums):
+        sent = sums[0].other
+        if len(sums) > 1:
+            sent = jnp.concatenate([item.other for item in sums], axis=0)
+        got = lax.ppermute(sent, "ctx", near_swap).astype(f32)
+        for k, item in enumerate(sums):
+            item.got = got[k * share : (k + 1) * share]
+
+    def finish_near(own, got):
+        return jnp.concatenate(
+            [jnp.where(is_high, got, own), jnp.where(is_high, own, got)], axis=1
+        )
 
     def norm_back(values, gain, incoming):
         _, back = jax.vjp(rms_norm, values, gain)
@@ -548,20 +656,12 @@
     down_sum = Reduction(d_feed_low, mixed)
     down_sum.core_pack()
     down_sum.core_send()
-    d_mixed = jnp.dot(
-        after(d_feed_low, *down_sum.packed), down_mat, preferred_element_type=f32
-    )
-    _, gate_back = jax.vjp(gated_product, gate, upward)
-    d_gate, d_upward = gate_back(d_mixed)
-    d_gate = d_gate.astype(bf16)
-    d_upward = d_upward.astype(bf16)
-
-    down_sum.y_pack(d_gate, d_upward)
+    down_sum.y_pack()
     down_sum.y_send()
-    d_feed_part = contract(after(d_gate, *down_sum.packed), gate_mat, 1, 1) + contract(
-        after(d_upward, *down_sum.packed), up_mat, 1, 1
-    )
-    packed = pack_all(d_feed_part)
+    d_feed_tied = after(d_feed_low, *down_sum.packed)
+    d_gate, d_upward = mix_backward(d_feed_tied, down_mat, gate, upward)
+    d_tied = (after(d_gate, *down_sum.packed), after(d_upward, *down_sum.packed))
+    d_feed_own, *packed = product_blocks(d_tied, [gate_mat, up_mat], half)
     sent = send_all(packed)
     gate_sum = Reduction(after(feed_in, *packed), d_gate)
     gate_sum.core_pack()
@@ -573,7 +673,7 @@
     up_sum.core_send()
     gate_sum.y_pack(*up_sum.packed)
     gate_sum.y_send()
-    own_feed = after(d_feed_part[:half], *gate_sum.packed)
+    own_feed = after(d_feed_own, *up_sum.packed, *gate_sum.packed)
     d_feed_in = sum_of(own_feed, sent)
 
     d_from_feed, pre_feed_part = norm_back(hidden_mid, feed_gain, d_feed_in)
@@ -592,6 +692,7 @@
     gate_sum.far_pack(*out_sum.packed)
     gate_sum.far_send()
     d_attended = after(d_attended, *gate_sum.packed)
+    d_attended = after(d_attended, *down_sum.arrived)
     d_query_pre, d_kv = attend_backward(
         queries,
         kv_all,
@@ -606,47 +707,28 @@
         per_group,
         ctx_count,
     )
-
-    def slot(index, carried):
-        block = d_kv[index * rows : (index + 1) * rows]
-        if carried is not None:
-            block = block + carried.astype(f32)
-        return block.astype(bf16)
-
-    def line_sum(step, left_block, right_block):
-        right_pairs = [(i, i + 1) for i in range(0, step)]
-        left_pairs = [(i, i - 1) for i in range(ctx_count - step, ctx_count)]
-        return (
-            lax.ppermute(left_block, "ctx", right_pairs),
-            lax.ppermute(right_block, "ctx", left_pairs),
-        )
-
-    sent_blocks = (slot(1, None), slot(ctx_count - 1, None))
-    carried = line_sum(1, *sent_blocks)
-    out_sum.y_pack(*sent_blocks)
+    d_kv = after(d_kv, *gate_sum.arrived)
+    d_kv_local = lax.psum_scatter(d_kv, "ctx", scatter_dimension=0, tiled=True).astype(f32)
+    out_sum.y_pack(d_kv)
     out_sum.y_send()
     query_sum = Reduction(after(attend_in, *out_sum.packed), d_query_pre)
     query_sum.core_pack()
     query_sum.core_send()
+    last = query_sum.packed
     down_sum.near_pack(*query_sum.packed)
-    down_sum.near_send()
-    before = (*query_sum.packed, *out_sum.packed, down_sum.packed)
-    for step in range(2, ctx_count):
-        carried = [after(item, *before) for item in carried]
-        sent_blocks = (slot(step, carried[0]), slot(ctx_count - step, carried[1]))
-        carried = line_sum(step, *sent_blocks)
-        before = ()
-        if step == 2:
-            query_sum.y_pack(*sent_blocks)
-            query_sum.y_send()
-            up_sum.far_pack(*query_sum.packed)
-            up_sum.far_send()
-            before = (*query_sum.packed, *up_sum.packed)
-    query_part = contract(after(d_query_pre, *sent_blocks), query_mat, 1, 1)
-    gate_sum.near_pack(query_part)
-    gate_sum.near_send()
-    carried = [after(item, query_part, gate_sum.packed) for item in carried]
-    d_kv_local = sum_of(d_kv[:rows], carried)
+    near_send(down_sum)
+    last = [down_sum.other]
+    up_sum.far_pack(*last)
+    up_sum.far_send()
+    query_sum.y_pack(*up_sum.packed)
+    query_sum.y_send()
+    query_part = contract(after(d_query_pre, *query_sum.packed), query_mat, 1, 1)
+    last = [query_part]
+    gate_sum.near_pack(*last)
+    near_send(gate_sum)
+    last = [gate_sum.other]
+    out_sum.sum_y(*last)
+    d_kv_local = after(d_kv_local, out_sum.total)
     turned = []
     for g in range(groups):
         middle = (2 * g + 1) * HD
@@ -656,36 +738,57 @@
         ]
     d_keyvalue = jnp.concatenate(turned, axis=1).astype(bf16)
 
-    in_factor = lax.rsqrt(jnp.mean(inputs * inputs, axis=-1, keepdims=True) + epsilon)
-    d_attend_part = query_part + contract(d_keyvalue, keyvalue_mat, 1, 1)
-    pre_attend_part = jnp.sum(d_attend_part * inputs * in_factor, axis=0)
-    gain_parts = jnp.stack([pre_attend_part, post_attend_part, pre_feed_part, post_feed_part])
-    gain_parts = jnp.pad(gain_parts, ((0, pad_lanes - 4), (0, 0)))
-    got = lax.ppermute(d_attend_part[half:].astype(bf16), "tensor", x_swap)
-
-    keyvalue_sum = Reduction(attend_in, d_keyvalue, gain_parts)
+    keyvalue_sum = Reduction(attend_in, d_keyvalue)
     keyvalue_sum.core_pack()
     keyvalue_sum.core_send()
-    keyvalue_sum.y_pack()
+    keyvalue_part = contract(
+        after(d_keyvalue, *keyvalue_sum.packed), keyvalue_mat, 1, 1
+    )
+    d_attend_part = query_part + keyvalue_part
+    d_attend_sent = d_attend_part[half:].astype(bf16)
+    got = lax.ppermute(d_attend_sent, "tensor", x_swap)
+    keyvalue_sum.y_pack(d_attend_sent)
     keyvalue_sum.y_send()
-    d_attend_in = d_attend_part[:half] + got.astype(f32)
+    query_sum.sum_y(d_keyvalue)
     up_sum.near_pack(*keyvalue_sum.packed)
-    up_sum.near_send()
+    near_send(up_sum)
+    keyvalue_sum.sum_y()
     out_grad = out_sum.finish_ctx().T
     query_grad = query_sum.finish_ctx()
     attend_grad = keyvalue_sum.finish_ctx()
-    down_grad = down_sum.finish_near().T
-    gate_grad = gate_sum.finish_near()
-    up_grad = up_sum.finish_near()
+
+    in_factor = lax.rsqrt(jnp.mean(inputs * inputs, axis=-1, keepdims=True) + epsilon)
+    pre_attend_part = jnp.sum(
+        after(d_attend_part, *keyvalue_sum.packed) * inputs * in_factor, axis=0
+    )
+    gain_grads = jnp.stack([pre_attend_part, post_attend_part, pre_feed_part, post_feed_part])
+
+    def swap_sum(values, axis, count):
+        bit = 1
+        while bit < count:
+            pairs = [(i, i ^ bit) for i in range(count)]
+            values = values + lax.ppermute(values, axis, pairs)
+            bit *= 2
+        return values
+
+    gain_grads = swap_sum(gain_grads, dp_axes, dp_count)
+    gain_grads = swap_sum(gain_grads, "ctx", ctx_count)
+    gain_grads = swap_sum(gain_grads, "tensor", tensor_count)
+    place = dp_index * ctx_count + ctx_index
+    gain_grads = gain_grads.reshape(4, dp_count * ctx_count, share)
+    gain_grads = lax.dynamic_slice_in_dim(gain_grads, place, 1, 1)[:, 0]
+
+    down_grad = finish_near(down_sum.own, down_sum.got).T
+    gate_grad = finish_near(gate_sum.own, gate_sum.got)
+    up_grad = finish_near(up_sum.own, up_sum.got)
     key_grad = jnp.concatenate(
         [attend_grad[:, 2 * g * HD : (2 * g + 1) * HD] for g in range(groups)], axis=1
     )
     value_grad = jnp.concatenate(
         [attend_grad[:, (2 * g + 1) * HD : (2 * g + 2) * HD] for g in range(groups)], axis=1
     )
-    gain_grads = attend_grad[:, keyvalue_width:]
-    gain_grads = (gain_grads + lax.ppermute(gain_grads, "tensor", x_swap)).T
-
+
+    d_attend_in = after(d_attend_part[:half], *keyvalue_sum.packed) + got.astype(f32)
     d_from_attend, _ = norm_back(own_inputs, gain_in, d_attend_in)
     input_grad = join_absolute((d_mid + d_from_attend).astype(bf16)).astype(f32)[None]
 
@@ -707,13 +810,19 @@
 
 
 def solution(mesh):
-    both = ("dp", "ctx")
+    dp_count, ctx_count, tensor_count = mesh.devices.shape
+    mesh = jax.sharding.Mesh(
+        mesh.devices.reshape(dp_count // cores, cores, ctx_count, tensor_count),
+        ("y", "core", "ctx", "tensor"),
+    )
+    dp = ("y", "core")
+    both = ("y", "core", "ctx")
     return jax.shard_map(
         body,
         mesh=mesh,
         in_specs=(
-            P("dp", "ctx", None),
-            P("dp", None),
+            P(dp, "ctx", None),
+            P(dp, None),
             P(both),
             P(both, "tensor"),
             P(both, "tensor"),
@@ -725,11 +834,11 @@
             P(both, "tensor"),
             P("tensor", both),
             P(both),
-            P("dp", "ctx", None),
+            P(dp, "ctx", None),
         ),
         out_specs=(
-            P("dp", "ctx", None),
-            P("dp", "ctx", None),
+            P(dp, "ctx", None),
+            P(dp, "ctx", None),
             P(both),
             P(both, "tensor"),
             P(both, "tensor"),

time: 1240 us -> 1190 us (0.960)
  matrix products: 213 us -> 85.8 us
  Pallas kernels: 40.9 us -> 139 us
    pallas_call x0 -> x4, Pallas kernels: none -> 98 us  [the longest x2 45.4 us: product_blocks(): pl.pallas_call(functools.partial(spread_kernel, len(lefts), half), grid=(...]
    dot_general x3 -> x0, matrix products: 73.3 us -> none  [the longest x1 29.8 us: body(): jnp.dot(after(d_feed_low, *down_sum.packed), down_mat, preferred_element_...]
    ppermute x30 -> x28, waiting for transfers between devices: 200 us -> 135 us  [the longest x3 78.7 us: near_send(): got = lax.ppermute(sent, 'ctx', near_swap).astype(f32)]
    dot_general x13 -> x10, matrix products: 127 us -> 70.1 us  [contract(): lax.dot_general(left, right, (((left_dim,), (right_dim,)), ((), ())), pre...]
    reduce_scatter x2 -> x4, waiting for transfers between devices: 0.01 us -> 25.9 us  [the longest x3 25.9 us: finish_ctx(): lax.psum_scatter(self.total, 'ctx', scatter_dimension=0, tiled=True)]
    unnamed x10, waiting for transfers between devices: 24.3 us -> 0.84 us
    ppermute x3, waiting for transfers between devices: 0.01 us -> 22.2 us  [far_send(): lax.ppermute(p, 'ctx', far_shift(s + 1))]
    ppermute x2, waiting for transfers between devices: 0.01 us -> 17.8 us  [join(): return jnp.concatenate([own, lax.ppermute(own, 'tensor', x_swap)], axis=0)]
  transfers between devices with their start and end apart: 68 -> 67, of which waited for: 27 -> 32; matrix products, arithmetic and copies ran while one was open for 30% -> 19% of each run, Pallas kernels for 3% -> 10%
where the time goes in v3:
time: 1190 us; the launch traced here: 1180 us
  waiting for transfers between devices  645 us (54%)
  other arithmetic  141 us (12%)
  Pallas kernels  139 us (12%)
  starting transfers between devices  93 us (8%)
  matrix products  85.8 us (7%)
  local copies, waits for them, and re-layouts  59.3 us (5%)
  between operations  15.8 us (1%)
    ppermute x3, waiting for transfers between devices, far_start(): lax.ppermute(block, 'ctx', far_shift(s))  150 us
    ppermute x6, waiting for transfers between devices, join_all(): parts.append(lax.ppermute(own, ('ctx', 'tensor'), pairs))  97.6 us
    ppermute x3, waiting for transfers between devices, near_send(): got = lax.ppermute(sent, 'ctx', near_swap).astype(f32)  78.7 us
    ppermute x1, waiting for transfers between devices, body(): gate_got = lax.ppermute(gate_other, 'ctx', near_swap)  70.3 us
    dot_general x10, matrix products, contract(): lax.dot_general(left, right, (((left_dim,), (right_dim,)), ((), ())), pre...  70.1 us
    ppermute x6, waiting for transfers between devices, send_all(): lax.ppermute(part, ('ctx', 'tensor'), pairs)  54.6 us
    pallas_call x2, Pallas kernels, product_blocks(): pl.pallas_call(functools.partial(spread_kernel, len(lefts), half), grid=(...  45.4 us
    ppermute x3, waiting for transfers between devices, line_step(): from_right.append(lax.ppermute(right_block, 'ctx', left_pairs))  39.6 us
  transfers between devices with their start and end apart: 67, of which 32 were waited for; matrix products, arithmetic and copies ran while one was open for 19% of the time, Pallas kernels for 10%

profile of v3, /device:TPU:0, one launch (start us, length us, event | category | flops | bytes accessed | tf_op | source)
XLA Modules:
  0.0 1178.5 jit_solution(8433533525259348510)
XLA Ops:
  26.7 70.3 %collective-permute-done.2 = bf16[144,2304]{1,0:T(8,128)(2,1)} collective-permute-done((bf16[144,2304]{1,0:T(8,128)(2,1)S(1)}, bf16[144,2304]{1,0:T(8,128)(2,1)}, u32[]{:S(2)}, u32[]{:S(2)}) %collective-permute-start.2) | collective-permute-done | bytes 663584 | tf_op jit(solution)/shard_map/ppermute | solution.py:481
  121.0 67.6 %collective-permute-done.3 = bf16[288,2304]{1,0:T(8,128)(2,1)} collective-permute-done((bf16[288,2304]{1,0:T(8,128)(2,1)}, bf16[288,2304]{1,0:T(8,128)(2,1)}, u32[]{:S(2)}, u32[]{:S(2)}) %collective-permute-start.3) | collective-permute-done | bytes 1327136 | tf_op jit(solution)/shard_map/ppermute | solution.py:476
  194.6 4.6 collective-permute-start.1
  199.7 31.5 %collective-permute-done.5 = bf16[512,1024]{1,0:T(8,128)(2,1)S(1)} collective-permute-done((bf16[512,1024]{1,0:T(8,128)(2,1)S(1)}, bf16[512,1024]{1,0:T(8,128)(2,1)S(1)}, u32[]{:S(2)}, u32[]{:S(2)}) %collective-permute-start.5) | collective-permute-done | bytes 1048608 | tf_op jit(solution)/shard_map/ppermute | solution.py:516
  232.5 4.1 collective-permute-done.1
  238.3 67.2 %collective-permute-done.9 = bf16[288,2304]{1,0:T(8,128)(2,1)S(1)} collective-permute-done((bf16[288,2304]{1,0:T(8,128)(2,1)}, bf16[288,2304]{1,0:T(8,128)(2,1)S(1)}, u32[]{:S(2)}, u32[]{:S(2)}) %collective-permute-start.9) | collective-permute-done | bytes 1327136 | tf_op jit(solution)/shard_map/ppermute | solution.py:476
  313.0 26.3 %collective-permute-start.14 = (bf16[288,2304]{1,0:T(8,128)(2,1)}, bf16[288,2304]{1,0:T(8,128)(2,1)}, u32[]{:S(2)}, u32[]{:S(2)}) collective-permute-start(bf16[288,2304]{1,0:T(8,128)(2,1)} %pad_maximum_fusion.12), channel_id=1, source_target_pairs={{0,4},{2,6},{4,0},{6,2},{1,5},{3,7},{5,1},{7,3},{8,12},{10,14},{12... | collective-permute-start | bytes 3981320 | tf_op jit(solution)/shard_map/ppermute | solution.py:476
  339.3 7.1 fusion.65.pre_ref
  346.4 8.1 collective-permute-done.8
  359.2 12.1 %attend_forward.1 = (bf16[512,1024]{1,0:T(8,128)(2,1)S(1)}, f32[512,1024]{1,0:T(8,128)S(1)}, bf16[512,1024]{1,0:T(8,128)(2,1)S(1)}, f32[4,1,512]{2,1,0:T(1,128)S(1)}) custom-call(f32[512,1024]{1,0:T(8,128)} %fusion.65.pre_ref, bf16[2048,1024]{1,0:T(8,128)(2,1)} %pad_maximum_fusion.3.kv_ref, f32[512,128]{1,0:T(8,128)S(1)} %get-tuple-element.207.cos_ref, ...), custom_call_target="tpu_custom_call" | custom-call | flops 524288 | bytes 524288 | tf_op jit(solution)/shard_map/attend_forward/pallas_call | solution.py:96
  373.6 5.1 convolution_convert_fusion.6
  380.6 15.1 %collective-permute-done.14 = bf16[288,2304]{1,0:T(8,128)(2,1)} collective-permute-done((bf16[288,2304]{1,0:T(8,128)(2,1)}, bf16[288,2304]{1,0:T(8,128)(2,1)}, u32[]{:S(2)}, u32[]{:S(2)}) %collective-permute-start.14) | collective-permute-done | bytes 1327136 | tf_op jit(solution)/shard_map/ppermute | solution.py:476
  395.7 8.4 collective-permute-done.10
  407.7 4.6 multiply_reduce_fusion.10
  418.9 24.5 %collective-permute-done.11 = bf16[256,2304]{1,0:T(8,128)(2,1)S(1)} collective-permute-done((bf16[256,2304]{1,0:T(8,128)(2,1)S(1)}, bf16[256,2304]{1,0:T(8,128)(2,1)S(1)}, u32[]{:S(2)}, u32[]{:S(2)}) %collective-permute-start.11) | collective-permute-done | bytes 1179680 | tf_op jit(solution)/shard_map/ppermute | solution.py:423
  445.9 20.3 %collective-permute-done.13 = bf16[256,2304]{1,0:T(8,128)(2,1)S(1)} collective-permute-done((bf16[256,2304]{1,0:T(8,128)(2,1)S(1)}, bf16[256,2304]{1,0:T(8,128)(2,1)S(1)}, u32[]{:S(2)}, u32[]{:S(2)}) %collective-permute-start.13) | collective-permute-done | bytes 1179680 | tf_op jit(solution)/shard_map/ppermute | solution.py:423
  469.0 29.3 %mix_forward.1 = (f32[1024,2304]{1,0:T(8,128)}, f32[1024,2304]{1,0:T(8,128)}, bf16[1024,2304]{1,0:T(8,128)(2,1)}) custom-call(bf16[1024,2304]{1,0:T(8,128)(2,1)} %pad_maximum_fusion.1.x_ref, bf16[2304,2304]{1,0:T(8,128)(2,1)} %all-gather.13.cloned.1.call-done.gate_mat_ref.refs_2_, bf16[2304,2304]{1,0:T(8,128)(2,1)} %all-gather.15.cloned.1.call-done.up_mat_ref.refs_3_), custom_call_target="tpu_custom_call" | custom-call | flops 1000000 | bytes 1000000 | tf_op jit(solution)/shard_map/mix_forward/pallas_call | solution.py:263
  498.3 8.0 all-gather.17.cloned.1.call-done.refs_1_.down_mat_ref
  506.2 16.3 %product_blocks.2 = (f32[256,2304]{1,0:T(8,128)}, bf16[256,2304]{1,0:T(8,128)(2,1)}, bf16[256,2304]{1,0:T(8,128)(2,1)}, bf16[256,2304]{1,0:T(8,128)(2,1)}) custom-call(bf16[1024,2304]{1,0:T(8,128)(2,1)} %get-tuple-element.81.refs_0_, bf16[2304,2304]{1,0:T(8,128)(2,1)} %all-gather.17.cloned.1.call-done.refs_1_.down_mat_ref), custom_call_target="tpu_custom_call" | custom-call | flops 1000000 | bytes 1000000 | tf_op jit(solution)/shard_map/product_blocks/pallas_call | solution.py:318
  526.0 25.0 %collective-permute-done.15 = bf16[256,2304]{1,0:T(8,128)(2,1)} collective-permute-done((bf16[256,2304]{1,0:T(8,128)(2,1)}, bf16[256,2304]{1,0:T(8,128)(2,1)}, u32[]{:S(2)}, u32[]{:S(2)}) %collective-permute-start.15) | collective-permute-done | bytes 1179680 | tf_op jit(solution)/shard_map/ppermute | solution.py:431
  553.1 24.3 %collective-permute-done.17 = bf16[256,2304]{1,0:T(8,128)(2,1)} collective-permute-done((bf16[256,2304]{1,0:T(8,128)(2,1)}, bf16[256,2304]{1,0:T(8,128)(2,1)}, u32[]{:S(2)}, u32[]{:S(2)}) %collective-permute-start.17) | collective-permute-done | bytes 1179680 | tf_op jit(solution)/shard_map/ppermute | solution.py:431
  588.7 24.8 %collective-permute-done.19 = bf16[256,2304]{1,0:T(8,128)(2,1)} collective-permute-done((bf16[256,2304]{1,0:T(8,128)(2,1)}, bf16[256,2304]{1,0:T(8,128)(2,1)}, u32[]{:S(2)}, u32[]{:S(2)}) %collective-permute-start.19) | collective-permute-done | bytes 1179680 | tf_op jit(solution)/shard_map/ppermute | solution.py:423
  615.9 23.1 %collective-permute-done.21 = bf16[256,2304]{1,0:T(8,128)(2,1)} collective-permute-done((bf16[256,2304]{1,0:T(8,128)(2,1)}, bf16[256,2304]{1,0:T(8,128)(2,1)}, u32[]{:S(2)}, u32[]{:S(2)}) %collective-permute-start.21) | collective-permute-done | bytes 1179680 | tf_op jit(solution)/shard_map/ppermute | solution.py:423
  639.0 14.7 %convolution_convert_fusion.2 = bf16[2304,2304]{1,0:T(8,128)(2,1)S(1)} fusion(bf16[1024,2304]{1,0:T(8,128)(2,1)} %get-tuple-element.81.refs_0_, bf16[256,2304]{1,0:T(8,128)(2,1)} %collective-permute-done.21, bf16[256,2304]{1,0:T(8,128)(2,1)} %collective-permute-done.20, bf16[256,2304]{1,0:T(8,128)(2,1)} %collective-permute-done.19, ...), kind=kOutput, calls=%fused_computation.2 | convolution fusion | flops 10895818752 | bytes 20054016 | tf_op jit(solution)/shard_map/dot_general | solution.py:330
  659.9 5.4 pad_maximum_fusion.2.d_ref
  665.3 4.8 add_convert_fusion.5
  670.3 23.3 %mix_backward.1 = (bf16[1024,2304]{1,0:T(8,128)(2,1)}, bf16[1024,2304]{1,0:T(8,128)(2,1)}) custom-call(bf16[1024,2304]{1,0:T(8,128)(2,1)} %pad_maximum_fusion.2.d_ref, bf16[2304,2304]{1,0:T(8,128)(2,1)} %all-gather.17.cloned.1.call-done.refs_1_.down_mat_ref, f32[1024,2304]{1,0:T(8,128)} %get-tuple-element.89.gate_ref, f32[1024,2304]{1,0:T(8,128)} %get-tuple-element.90.up_ref), custom_call_target="tpu_custom_call" | custom-call | flops 1000000 | bytes 1000000 | tf_op jit(solution)/shard_map/mix_backward/pallas_call | solution.py:288
  693.7 29.1 %product_blocks.3 = (f32[256,2304]{1,0:T(8,128)}, bf16[256,2304]{1,0:T(8,128)(2,1)}, bf16[256,2304]{1,0:T(8,128)(2,1)}, bf16[256,2304]{1,0:T(8,128)(2,1)}) custom-call(bf16[1024,2304]{1,0:T(8,128)(2,1)} %get-tuple-element.92.refs_0_, bf16[1024,2304]{1,0:T(8,128)(2,1)} %get-tuple-element.94.refs_1_, ...), custom_call_target="tpu_custom_call" | custom-call | flops 1000000 | bytes 1000000 | tf_op jit(solution)/shard_map/product_blocks/pallas_call | solution.py:318
  726.2 14.1 %convolution_convert_fusion.1 = bf16[2304,2304]{1,0:T(8,128)(2,1)S(1)} fusion(bf16[1024,2304]{1,0:T(8,128)(2,1)S(1)} %bitcast.54, bf16[1024,2304]{1,0:T(8,128)(2,1)} %get-tuple-element.92.refs_0_), kind=kOutput, calls=%fused_computation.1 | convolution fusion | flops 10876944384 | bytes 20054016 | tf_op jit(solution)/shard_map/dot_general | solution.py:330
  747.0 4.3 add_convert_fusion.4
  754.0 12.2 %convolution_convert_fusion = bf16[2304,2304]{1,0:T(8,128)(2,1)S(1)} fusion(bf16[1024,2304]{1,0:T(8,128)(2,1)S(1)} %bitcast.54, bf16[1024,2304]{1,0:T(8,128)(2,1)S(1)} %bitcast.58), kind=kOutput, calls=%fused_computation | convolution fusion | flops 10876944384 | bytes 20054016 | tf_op jit(solution)/shard_map/dot_general | solution.py:330
  768.8 5.1 add_convert_fusion.3
  790.9 18.7 %collective-permute-done.29 = bf16[256,2304]{1,0:T(8,128)(2,1)S(1)} collective-permute-done((bf16[256,2304]{1,0:T(8,128)(2,1)S(1)}, bf16[256,2304]{1,0:T(8,128)(2,1)S(1)}, u32[]{:S(2)}, u32[]{:S(2)}) %collective-permute-start.29) | collective-permute-done | bytes 1179680 | tf_op jit(solution)/shard_map/ppermute | solution.py:683
  809.8 6.0 convolution_convert_fusion.7.da_ref
  822.0 20.6 %collective-permute-done.32 = bf16[576,2304]{1,0:T(8,128)(2,1)S(1)} collective-permute-done((bf16[576,2304]{1,0:T(8,128)(2,1)S(1)}, bf16[576,2304]{1,0:T(8,128)(2,1)S(1)}, u32[]{:S(2)}, u32[]{:S(2)}) %collective-permute-start.32) | collective-permute-done | bytes 2654240 | tf_op jit(solution)/shard_map/ppermute | solution.py:590
  854.9 29.0 %attend_backward.1 = (bf16[512,1024]{1,0:T(8,128)(2,1)S(1)}, bf16[2048,1024]{1,0:T(8,128)(2,1)}) custom-call(bf16[512,1024]{1,0:T(8,128)(2,1)S(1)} %get-tuple-element.104.q_ref, bf16[2048,1024]{1,0:T(8,128)(2,1)} %pad_maximum_fusion.3.kv_ref, bf16[512,1024]{1,0:T(8,128)(2,1)S(1)} %copy-done.1, f32[512,1024]{1,0:T(8,128)} %copy-done, ...), custom_call_target="tpu_custom_call" | custom-call | flops 524288 | bytes 524288 | tf_op jit(solution)/shard_map/attend_backward/pallas_call | solution.py:190
  884.9 22.2 %collective-permute-done.35 = bf16[288,2304]{1,0:T(8,128)(2,1)} collective-permute-done((bf16[288,2304]{1,0:T(8,128)(2,1)}, bf16[288,2304]{1,0:T(8,128)(2,1)}, u32[]{:S(2)}, u32[]{:S(2)}) %collective-permute-start.35) | collective-permute-done | bytes 1327136 | tf_op jit(solution)/shard_map/ppermute | solution.py:624
  924.3 39.6 %collective-permute-done.56 = bf16[144,2304]{1,0:T(8,128)(2,1)S(1)} collective-permute-done((bf16[144,2304]{1,0:T(8,128)(2,1)S(1)}, bf16[144,2304]{1,0:T(8,128)(2,1)S(1)}, u32[]{:S(2)}, u32[]{:S(2)}) %collective-permute-start.56) | collective-permute-done | bytes 663584 | tf_op jit(solution)/shard_map/ppermute | solution.py:641
  965.7 4.5 add_convert_fusion
  973.3 4.4 fusion.66
  982.2 4.0 collective-permute-start.54
  992.0 39.0 %collective-permute-done.53 = bf16[144,2304]{1,0:T(8,128)(2,1)S(1)} collective-permute-done((bf16[144,2304]{1,0:T(8,128)(2,1)}, bf16[144,2304]{1,0:T(8,128)(2,1)S(1)}, u32[]{:S(2)}, u32[]{:S(2)}) %collective-permute-start.53) | collective-permute-done | bytes 663584 | tf_op jit(solution)/shard_map/ppermute | solution.py:641
  1045.8 22.0 %reduce-scatter.11.cloned.1.call-done = bf16[144,1024]{1,0:T(8,128)(2,1)} async-done(((bf16[576,1024]{1,0:T(8,128)(2,1)}), bf16[144,1024]{1,0:T(8,128)(2,1)}) %reduce-scatter.11.cloned.1.call-update) | async-done | bytes 294928 | tf_op jit(solution)/shard_map/reduce_scatter | solution.py:602
  1069.6 6.0 convolution_add_fusion
  1098.4 18.1 %collective-permute-done.45 = f32[4,2304]{1,0:T(4,128)S(1)} collective-permute-done((f32[4,2304]{1,0:T(4,128)S(1)}, f32[4,2304]{1,0:T(4,128)S(1)}, u32[]{:S(2)}, u32[]{:S(2)}) %collective-permute-start.45) | collective-permute-done | bytes 36896 | tf_op jit(solution)/shard_map/ppermute | solution.py:770
  1119.6 5.7 collective-permute-done.46
  1135.1 3.9 add_convert_fusion.6
  1142.9 17.8 %collective-permute-done.43 = bf16[256,2304]{1,0:T(8,128)(2,1)} collective-permute-done((bf16[256,2304]{1,0:T(8,128)(2,1)}, bf16[256,2304]{1,0:T(8,128)(2,1)}, u32[]{:S(2)}, u32[]{:S(2)}) %collective-permute-start.43) | collective-permute-done | bytes 1179680 | tf_op jit(solution)/shard_map/ppermute | solution.py:415
  (421 shorter events, 260.3 us)
Async XLA Ops:
  7.2 99.5 %all-gather.7.cloned.1.call-start = ((), (), s32[]{:S(2)}) async-start(), calls=%async_computation.4 | async-start | bytes 5640192 | tf_op jit(solution)/shard_map/all_gather | solution.py:459
  14.4 325.0 %all-gather.9.cloned.1.call-start = ((), (), s32[]{:S(2)}) async-start(), calls=%async_computation.5 | async-start | bytes 5013504 | tf_op jit(solution)/shard_map/all_gather | solution.py:460
  15.1 358.5 %all-gather.11.cloned.1.call-start = ((), (), s32[]{:S(2)}) async-start(), calls=%async_computation.6 | async-start | bytes 5013504 | tf_op jit(solution)/shard_map/all_gather | solution.py:461
  18.3 83.6 %collective-permute-start = (bf16[288,2304]{1,0:T(8,128)(2,1)}, bf16[288,2304]{1,0:T(8,128)(2,1)}, u32[]{:S(2)}, u32[]{:S(2)}) collective-permute-start(bf16[288,2304]{1,0:T(8,128)(2,1)} %pad_maximum_fusion.10), channel_id=1, source_target_pairs={{0,2},{2,0},{4,6},{6,4},{1,3},{3,1},{5,7},{7,5},{8,10},{10,8},{12,... | collective-permute-start | bytes 3981320 | tf_op jit(solution)/shard_map/ppermute | solution.py:482
  21.4 75.6 %collective-permute-start.2 = (bf16[144,2304]{1,0:T(8,128)(2,1)S(1)}, bf16[144,2304]{1,0:T(8,128)(2,1)}, u32[]{:S(2)}, u32[]{:S(2)}) collective-permute-start(bf16[144,2304]{1,0:T(8,128)(2,1)S(1)} %broadcast_select_fusion.17), channel_id=1, source_target_pairs={{0,2},{2,0},{4,6},{6,4},{1,3},{3,1},{5,7},{7,5},{8,10},{10,8},{12,... | collective-permute-start | bytes 1990664 | tf_op jit(solution)/shard_map/ppermute | solution.py:481
  21.5 447.5 %all-gather.13.cloned.1.call-start = ((), (), s32[]{:S(2)}) async-start(), calls=%async_computation.7 | async-start | bytes 13271040 | tf_op jit(solution)/shard_map/all_gather | solution.py:521
  100.2 88.4 %collective-permute-start.3 = (bf16[288,2304]{1,0:T(8,128)(2,1)}, bf16[288,2304]{1,0:T(8,128)(2,1)}, u32[]{:S(2)}, u32[]{:S(2)}) collective-permute-start(bf16[288,2304]{1,0:T(8,128)(2,1)} %pad_maximum_fusion.13), channel_id=1, source_target_pairs={{0,4},{2,6},{4,0},{6,2},{1,5},{3,7},{5,1},{7,3},{8,12},{10,14},{12... | collective-permute-start | bytes 3981320 | tf_op jit(solution)/shard_map/ppermute | solution.py:476
  192.1 276.9 %all-gather.15.cloned.1.call-start = ((), (), s32[]{:S(2)}) async-start(), calls=%async_computation.8 | async-start | bytes 13271040 | tf_op jit(solution)/shard_map/all_gather | solution.py:540
  193.3 37.9 %collective-permute-start.5 = (bf16[512,1024]{1,0:T(8,128)(2,1)S(1)}, bf16[512,1024]{1,0:T(8,128)(2,1)S(1)}, u32[]{:S(2)}, u32[]{:S(2)}) collective-permute-start(bf16[512,1024]{1,0:T(8,128)(2,1)S(1)} %copy-done.48), channel_id=1, source_target_pairs={{2,0},{4,2},{6,4},{3,1},{5,3},{7,5},{10,8},{12,10},{14,12},{11,9},... | collective-permute-start | bytes 3145736 | tf_op jit(solution)/shard_map/ppermute | solution.py:516
  194.6 42.0 %collective-permute-start.1 = (bf16[512,1024]{1,0:T(8,128)(2,1)S(1)}, bf16[512,1024]{1,0:T(8,128)(2,1)S(1)}, u32[]{:S(2)}, u32[]{:S(2)}) collective-permute-start(bf16[512,1024]{1,0:T(8,128)(2,1)S(1)} %copy-done.48), channel_id=1, source_target_pairs={{0,2},{2,4},{4,6},{1,3},{3,5},{5,7},{8,10},{10,12},{12,14},{9,11},... | collective-permute-start | bytes 3145736 | tf_op jit(solution)/shard_map/ppermute | solution.py:515
  199.2 106.3 %collective-permute-start.9 = (bf16[288,2304]{1,0:T(8,128)(2,1)}, bf16[288,2304]{1,0:T(8,128)(2,1)S(1)}, u32[]{:S(2)}, u32[]{:S(2)}) collective-permute-start(bf16[288,2304]{1,0:T(8,128)(2,1)} %pad_maximum_fusion.11), channel_id=1, source_target_pairs={{0,4},{2,6},{4,0},{6,2},{1,5},{3,7},{5,1},{7,3},{8,12},{10,14},{12... | collective-permute-start | bytes 3981320 | tf_op jit(solution)/shard_map/ppermute | solution.py:476
  231.2 74.3 %collective-permute-start.6 = (bf16[512,1024]{1,0:T(8,128)(2,1)S(1)}, bf16[512,1024]{1,0:T(8,128)(2,1)}, u32[]{:S(2)}, u32[]{:S(2)}) collective-permute-start(bf16[512,1024]{1,0:T(8,128)(2,1)S(1)} %collective-permute-done.5), channel_id=1, source_target_pairs={{2,0},{4,2},{3,1},{5,3},{10,8},{12,10},{11,9},{13,11},{18,16},{20,... | collective-permute-start | bytes 3145736 | tf_op jit(solution)/shard_map/ppermute | solution.py:516
  236.6 68.9 %collective-permute-start.4 = (bf16[512,1024]{1,0:T(8,128)(2,1)S(1)}, bf16[512,1024]{1,0:T(8,128)(2,1)}, u32[]{:S(2)}, u32[]{:S(2)}) collective-permute-start(bf16[512,1024]{1,0:T(8,128)(2,1)S(1)} %collective-permute-done.1), channel_id=1, source_target_pairs={{2,4},{4,6},{3,5},{5,7},{10,12},{12,14},{11,13},{13,15},{18,20},{2... | collective-permute-start | bytes 3145736 | tf_op jit(solution)/shard_map/ppermute | solution.py:515
  307.8 198.4 %all-gather.17.cloned.1.call-start = ((), (), s32[]{:S(2)}) async-start(), calls=%async_computation.9 | async-start | bytes 13271040 | tf_op jit(solution)/shard_map/all_gather | solution.py:550
  307.8 46.7 %collective-permute-start.8 = (bf16[512,1024]{1,0:T(8,128)(2,1)}, bf16[512,1024]{1,0:T(8,128)(2,1)}, u32[]{:S(2)}, u32[]{:S(2)}) collective-permute-start(bf16[512,1024]{1,0:T(8,128)(2,1)} %collective-permute-done.6), channel_id=1, source_target_pairs={{2,0},{3,1},{10,8},{11,9},{18,16},{19,17},{26,24},{27,25}} | collective-permute-start | bytes 3145736 | tf_op jit(solution)/shard_map/ppermute | solution.py:516
  309.1 45.4 %collective-permute-start.7 = (bf16[512,1024]{1,0:T(8,128)(2,1)}, bf16[512,1024]{1,0:T(8,128)(2,1)}, u32[]{:S(2)}, u32[]{:S(2)}) collective-permute-start(bf16[512,1024]{1,0:T(8,128)(2,1)} %collective-permute-done.4), channel_id=1, source_target_pairs={{4,6},{5,7},{12,14},{13,15},{20,22},{21,23},{28,30},{29,31}} | collective-permute-start | bytes 3145736 | tf_op jit(solution)/shard_map/ppermute | solution.py:515
  313.0 82.7 %collective-permute-start.14 = (bf16[288,2304]{1,0:T(8,128)(2,1)}, bf16[288,2304]{1,0:T(8,128)(2,1)}, u32[]{:S(2)}, u32[]{:S(2)}) collective-permute-start(bf16[288,2304]{1,0:T(8,128)(2,1)} %pad_maximum_fusion.12), channel_id=1, source_target_pairs={{0,4},{2,6},{4,0},{6,2},{1,5},{3,7},{5,1},{7,3},{8,12},{10,14},{12... | collective-permute-start | bytes 3981320 | tf_op jit(solution)/shard_map/ppermute | solution.py:476
  407.6 625.4 %reduce-scatter.5.cloned.1.call-start = ((), (), s32[]{:S(2)}) async-start(), calls=%async_computation.10 | async-start | bytes 5242880 | tf_op jit(solution)/shard_map/reduce_scatter | solution.py:711
  417.0 49.2 %collective-permute-start.13 = (bf16[256,2304]{1,0:T(8,128)(2,1)S(1)}, bf16[256,2304]{1,0:T(8,128)(2,1)S(1)}, u32[]{:S(2)}, u32[]{:S(2)}) collective-permute-start(bf16[256,2304]{1,0:T(8,128)(2,1)S(1)} %multiply_convert_fusion.1), channel_id=1, source_target_pairs={{0,3},{1,2},{2,1},{3,0},{4,7},{5,6},{6,5},{7,4},{8,11},{9,10},{10,... | collective-permute-start | bytes 3538952 | tf_op jit(solution)/shard_map/ppermute | solution.py:423
  525.5 52.0 %collective-permute-start.17 = (bf16[256,2304]{1,0:T(8,128)(2,1)}, bf16[256,2304]{1,0:T(8,128)(2,1)}, u32[]{:S(2)}, u32[]{:S(2)}) collective-permute-start(bf16[256,2304]{1,0:T(8,128)(2,1)} %get-tuple-element.87), channel_id=1, source_target_pairs={{0,3},{1,2},{2,1},{3,0},{4,7},{5,6},{6,5},{7,4},{8,11},{9,10},{10,... | collective-permute-start | bytes 3538952 | tf_op jit(solution)/shard_map/ppermute | solution.py:431
  588.1 50.9 %collective-permute-start.21 = (bf16[256,2304]{1,0:T(8,128)(2,1)}, bf16[256,2304]{1,0:T(8,128)(2,1)}, u32[]{:S(2)}, u32[]{:S(2)}) collective-permute-start(bf16[256,2304]{1,0:T(8,128)(2,1)} %get-tuple-element.188), channel_id=1, source_target_pairs={{0,3},{1,2},{2,1},{3,0},{4,7},{5,6},{6,5},{7,4},{8,11},{9,10},{10,... | collective-permute-start | bytes 3538952 | tf_op jit(solution)/shard_map/ppermute | solution.py:423
  659.4 87.6 %collective-permute-start.23 = (bf16[576,2304]{1,0:T(8,128)(2,1)}, bf16[576,2304]{1,0:T(8,128)(2,1)}, u32[]{:S(2)}, u32[]{:S(2)}) collective-permute-start(bf16[576,2304]{1,0:T(8,128)(2,1)} %get-tuple-element.157), channel_id=1, source_target_pairs={{0,8},{8,0},{16,24},{24,16},{1,9},{9,1},{17,25},{25,17},{2,10},{10... | collective-permute-start | bytes 7962632 | tf_op jit(solution)/shard_map/ppermute | solution.py:576
  670.1 76.9 %collective-permute-start.24 = (bf16[576,2304]{1,0:T(8,128)(2,1)}, bf16[576,2304]{1,0:T(8,128)(2,1)}, u32[]{:S(2)}, u32[]{:S(2)}) collective-permute-start(bf16[576,2304]{1,0:T(8,128)(2,1)} %add_convert_fusion.5), channel_id=1, source_target_pairs={{0,16},{8,24},{16,0},{24,8},{1,17},{9,25},{17,1},{25,9},{2,18},{10... | collective-permute-start | bytes 7962632 | tf_op jit(solution)/shard_map/ppermute | solution.py:590
  722.7 51.2 %collective-permute-start.26 = (bf16[256,2304]{1,0:T(8,128)(2,1)}, bf16[256,2304]{1,0:T(8,128)(2,1)}, u32[]{:S(2)}, u32[]{:S(2)}) collective-permute-start(bf16[256,2304]{1,0:T(8,128)(2,1)} %get-tuple-element.96), channel_id=1, source_target_pairs={{0,1},{1,0},{2,3},{3,2},{4,5},{5,4},{6,7},{7,6},{8,9},{9,8},{10,11... | collective-permute-start | bytes 3538952 | tf_op jit(solution)/shard_map/ppermute | solution.py:431
  724.4 49.5 %collective-permute-start.27 = (bf16[256,2304]{1,0:T(8,128)(2,1)}, bf16[256,2304]{1,0:T(8,128)(2,1)}, u32[]{:S(2)}, u32[]{:S(2)}) collective-permute-start(bf16[256,2304]{1,0:T(8,128)(2,1)} %get-tuple-element.97), channel_id=1, source_target_pairs={{0,2},{1,3},{2,0},{3,1},{4,6},{5,7},{6,4},{7,5},{8,10},{9,11},{10,... | collective-permute-start | bytes 3538952 | tf_op jit(solution)/shard_map/ppermute | solution.py:431
  725.9 51.2 %collective-permute-start.28 = (bf16[256,2304]{1,0:T(8,128)(2,1)}, bf16[256,2304]{1,0:T(8,128)(2,1)}, u32[]{:S(2)}, u32[]{:S(2)}) collective-permute-start(bf16[256,2304]{1,0:T(8,128)(2,1)} %get-tuple-element.98), channel_id=1, source_target_pairs={{0,3},{1,2},{2,1},{3,0},{4,7},{5,6},{6,5},{7,4},{8,11},{9,10},{10,... | collective-permute-start | bytes 3538952 | tf_op jit(solution)/shard_map/ppermute | solution.py:431
  784.7 57.9 %collective-permute-start.32 = (bf16[576,2304]{1,0:T(8,128)(2,1)S(1)}, bf16[576,2304]{1,0:T(8,128)(2,1)S(1)}, u32[]{:S(2)}, u32[]{:S(2)}) collective-permute-start(bf16[576,2304]{1,0:T(8,128)(2,1)S(1)} %add_convert_fusion.3), channel_id=1, source_target_pairs={{0,16},{8,24},{16,0},{24,8},{1,17},{9,25},{17,1},{25,9},{2,18},{10... | collective-permute-start | bytes 7962632 | tf_op jit(solution)/shard_map/ppermute | solution.py:590
  786.2 56.4 %collective-permute-start.31 = (bf16[576,2304]{1,0:T(8,128)(2,1)S(1)}, bf16[576,2304]{1,0:T(8,128)(2,1)}, u32[]{:S(2)}, u32[]{:S(2)}) collective-permute-start(bf16[576,2304]{1,0:T(8,128)(2,1)S(1)} %copy-done.53), channel_id=1, source_target_pairs={{0,8},{8,0},{16,24},{24,16},{1,9},{9,1},{17,25},{25,17},{2,10},{10... | collective-permute-start | bytes 7962632 | tf_op jit(solution)/shard_map/ppermute | solution.py:576
  786.2 65.9 %collective-permute-start.33 = (bf16[288,2304]{1,0:T(8,128)(2,1)}, bf16[288,2304]{1,0:T(8,128)(2,1)}, u32[]{:S(2)}, u32[]{:S(2)}) collective-permute-start(bf16[288,2304]{1,0:T(8,128)(2,1)} %broadcast_select_fusion.2), channel_id=1, source_target_pairs={{0,4},{2,6},{4,0},{6,2},{1,5},{3,7},{5,1},{7,3},{8,12},{10,14},{12... | collective-permute-start | bytes 3981320 | tf_op jit(solution)/shard_map/ppermute | solution.py:624
  848.8 58.3 %collective-permute-start.35 = (bf16[288,2304]{1,0:T(8,128)(2,1)}, bf16[288,2304]{1,0:T(8,128)(2,1)}, u32[]{:S(2)}, u32[]{:S(2)}) collective-permute-start(bf16[288,2304]{1,0:T(8,128)(2,1)} %broadcast_select_fusion.1), channel_id=1, source_target_pairs={{0,4},{2,6},{4,0},{6,2},{1,5},{3,7},{5,1},{7,3},{8,12},{10,14},{12... | collective-permute-start | bytes 3981320 | tf_op jit(solution)/shard_map/ppermute | solution.py:624
  851.2 56.0 %collective-permute-start.34 = (bf16[576,1024]{1,0:T(8,128)(2,1)}, bf16[576,1024]{1,0:T(8,128)(2,1)}, u32[]{:S(2)}, u32[]{:S(2)}) collective-permute-start(bf16[576,1024]{1,0:T(8,128)(2,1)} %get-tuple-element.165), channel_id=1, source_target_pairs={{0,8},{8,0},{16,24},{24,16},{1,9},{9,1},{17,25},{25,17},{2,10},{10... | collective-permute-start | bytes 3538952 | tf_op jit(solution)/shard_map/ppermute | solution.py:576
  851.2 67.7 %collective-permute-start.18 = (bf16[256,2304]{1,0:T(8,128)(2,1)}, bf16[256,2304]{1,0:T(8,128)(2,1)}, u32[]{:S(2)}, u32[]{:S(2)}) collective-permute-start(bf16[256,2304]{1,0:T(8,128)(2,1)} %get-tuple-element.189), channel_id=1, source_target_pairs={{0,1},{1,0},{2,3},{3,2},{4,5},{5,4},{6,7},{7,6},{8,9},{9,8},{10,11... | collective-permute-start | bytes 3538952 | tf_op jit(solution)/shard_map/ppermute | solution.py:415
  851.9 113.8 %collective-permute-start.37 = (bf16[576,2304]{1,0:T(8,128)(2,1)}, bf16[576,2304]{1,0:T(8,128)(2,1)}, u32[]{:S(2)}, u32[]{:S(2)}) collective-permute-start(bf16[576,2304]{1,0:T(8,128)(2,1)} %get-tuple-element.156), channel_id=1, source_target_pairs={{0,8},{8,0},{16,24},{24,16},{1,9},{9,1},{17,25},{25,17},{2,10},{10... | collective-permute-start | bytes 7962632 | tf_op jit(solution)/shard_map/ppermute | solution.py:576
  852.1 113.5 %collective-permute-start.38 = (bf16[576,2304]{1,0:T(8,128)(2,1)}, bf16[576,2304]{1,0:T(8,128)(2,1)}, u32[]{:S(2)}, u32[]{:S(2)}) collective-permute-start(bf16[576,2304]{1,0:T(8,128)(2,1)} %add_convert_fusion.2), channel_id=1, source_target_pairs={{0,16},{8,24},{16,0},{24,8},{1,17},{9,25},{17,1},{25,9},{2,18},{10... | collective-permute-start | bytes 7962632 | tf_op jit(solution)/shard_map/ppermute | solution.py:590
  907.1 160.6 %reduce-scatter.11.cloned.1.call-start = ((), (), s32[]{:S(2)}) async-start(), calls=%async_computation.13 | async-start | bytes 1474560 | tf_op jit(solution)/shard_map/reduce_scatter | solution.py:602
  918.4 45.5 %collective-permute-start.56 = (bf16[144,2304]{1,0:T(8,128)(2,1)S(1)}, bf16[144,2304]{1,0:T(8,128)(2,1)S(1)}, u32[]{:S(2)}, u32[]{:S(2)}) collective-permute-start(bf16[144,2304]{1,0:T(8,128)(2,1)S(1)} %select_convert_fusion.2), channel_id=1, source_target_pairs={{0,2},{2,0},{4,6},{6,4},{1,3},{3,1},{5,7},{7,5},{8,10},{10,8},{12,... | collective-permute-start | bytes 1990664 | tf_op jit(solution)/shard_map/ppermute | solution.py:641
  923.7 65.3 %collective-permute-start.39 = (bf16[576,1024]{1,0:T(8,128)(2,1)S(1)}, bf16[576,1024]{1,0:T(8,128)(2,1)S(1)}, u32[]{:S(2)}, u32[]{:S(2)}) collective-permute-start(bf16[576,1024]{1,0:T(8,128)(2,1)S(1)} %copy-done.59), channel_id=1, source_target_pairs={{0,8},{8,0},{16,24},{24,16},{1,9},{9,1},{17,25},{25,17},{2,10},{10... | collective-permute-start | bytes 3538952 | tf_op jit(solution)/shard_map/ppermute | solution.py:576
  923.8 47.9 %collective-permute-start.36 = (bf16[576,1024]{1,0:T(8,128)(2,1)S(1)}, bf16[576,1024]{1,0:T(8,128)(2,1)S(1)}, u32[]{:S(2)}, u32[]{:S(2)}) collective-permute-start(bf16[576,1024]{1,0:T(8,128)(2,1)S(1)} %get-tuple-element.164), channel_id=1, source_target_pairs={{0,8},{8,0},{16,24},{24,16},{1,9},{9,1},{17,25},{25,17},{2,10},{10... | collective-permute-start | bytes 3538952 | tf_op jit(solution)/shard_map/ppermute | solution.py:576
  965.6 113.3 %collective-permute-start.49 = (bf16[576,1024]{1,0:T(8,128)(2,1)}, bf16[576,1024]{1,0:T(8,128)(2,1)}, u32[]{:S(2)}, u32[]{:S(2)}) collective-permute-start(bf16[576,1024]{1,0:T(8,128)(2,1)} %get-tuple-element.163), channel_id=1, source_target_pairs={{0,8},{8,0},{16,24},{24,16},{1,9},{9,1},{17,25},{25,17},{2,10},{10... | collective-permute-start | bytes 3538952 | tf_op jit(solution)/shard_map/ppermute | solution.py:576
  980.4 50.6 %collective-permute-start.53 = (bf16[144,2304]{1,0:T(8,128)(2,1)}, bf16[144,2304]{1,0:T(8,128)(2,1)S(1)}, u32[]{:S(2)}, u32[]{:S(2)}) collective-permute-start(bf16[144,2304]{1,0:T(8,128)(2,1)} %select_convert_fusion.1), channel_id=1, source_target_pairs={{0,2},{2,0},{4,6},{6,4},{1,3},{3,1},{5,7},{7,5},{8,10},{10,8},{12,... | collective-permute-start | bytes 1990664 | tf_op jit(solution)/shard_map/ppermute | solution.py:641
  982.2 106.3 %collective-permute-start.54 = (bf16[288,2304]{1,0:T(8,128)(2,1)}, bf16[288,2304]{1,0:T(8,128)(2,1)}, u32[]{:S(2)}, u32[]{:S(2)}) collective-permute-start(bf16[288,2304]{1,0:T(8,128)(2,1)} %broadcast_select_fusion), channel_id=1, source_target_pairs={{0,4},{2,6},{4,0},{6,2},{1,5},{3,7},{5,1},{7,3},{8,12},{10,14},{12... | collective-permute-start | bytes 3981320 | tf_op jit(solution)/shard_map/ppermute | solution.py:624
  987.5 91.4 %collective-permute-start.50 = (bf16[576,1024]{1,0:T(8,128)(2,1)}, bf16[576,1024]{1,0:T(8,128)(2,1)}, u32[]{:S(2)}, u32[]{:S(2)}) collective-permute-start(bf16[576,1024]{1,0:T(8,128)(2,1)} %add_convert_fusion.10), channel_id=1, source_target_pairs={{0,16},{8,24},{16,0},{24,8},{1,17},{9,25},{17,1},{25,9},{2,18},{10... | collective-permute-start | bytes 3538952 | tf_op jit(solution)/shard_map/ppermute | solution.py:590
  991.9 149.1 %reduce-scatter.7.cloned.1.call-start = ((), (), s32[]{:S(2)}) async-start(), calls=%async_computation.11 | async-start | bytes 1474560 | tf_op jit(solution)/shard_map/reduce_scatter | solution.py:602
  1045.5 38.6 %collective-permute-start.41 = (bf16[576,1024]{1,0:T(8,128)(2,1)S(1)}, bf16[576,1024]{1,0:T(8,128)(2,1)}, u32[]{:S(2)}, u32[]{:S(2)}) collective-permute-start(bf16[576,1024]{1,0:T(8,128)(2,1)S(1)} %get-tuple-element.161), channel_id=1, source_target_pairs={{0,8},{8,0},{16,24},{24,16},{1,9},{9,1},{17,25},{25,17},{2,10},{10... | collective-permute-start | bytes 3538952 | tf_op jit(solution)/shard_map/ppermute | solution.py:576
  1069.6 65.5 %collective-permute-start.51 = (bf16[576,1024]{1,0:T(8,128)(2,1)}, bf16[576,1024]{1,0:T(8,128)(2,1)}, u32[]{:S(2)}, u32[]{:S(2)}) collective-permute-start(bf16[576,1024]{1,0:T(8,128)(2,1)} %get-tuple-element.162), channel_id=1, source_target_pairs={{0,8},{8,0},{16,24},{24,16},{1,9},{9,1},{17,25},{25,17},{2,10},{10... | collective-permute-start | bytes 3538952 | tf_op jit(solution)/shard_map/ppermute | solution.py:576
  1082.7 86.2 %reduce-scatter.9.cloned.1.call-start = ((), (), s32[]{:S(2)}) async-start(), calls=%async_computation.12 | async-start | bytes 1474560 | tf_op jit(solution)/shard_map/reduce_scatter | solution.py:602
  1087.3 47.8 %collective-permute-start.52 = (bf16[576,1024]{1,0:T(8,128)(2,1)}, bf16[576,1024]{1,0:T(8,128)(2,1)}, u32[]{:S(2)}, u32[]{:S(2)}) collective-permute-start(bf16[576,1024]{1,0:T(8,128)(2,1)} %add_convert_fusion.8), channel_id=1, source_target_pairs={{0,16},{8,24},{16,0},{24,8},{1,17},{9,25},{17,1},{25,9},{2,18},{10... | collective-permute-start | bytes 3538952 | tf_op jit(solution)/shard_map/ppermute | solution.py:590
  1096.1 42.9 %collective-permute-start.55 = (bf16[144,2304]{1,0:T(8,128)(2,1)}, bf16[144,2304]{1,0:T(8,128)(2,1)S(1)}, u32[]{:S(2)}, u32[]{:S(2)}) collective-permute-start(bf16[144,2304]{1,0:T(8,128)(2,1)} %select_convert_fusion), channel_id=1, source_target_pairs={{0,2},{2,0},{4,6},{6,4},{1,3},{3,1},{5,7},{7,5},{8,10},{10,8},{12,... | collective-permute-start | bytes 1990664 | tf_op jit(solution)/shard_map/ppermute | solution.py:641
  (102 other events, 2406.6 us)
Sparse Core Ops, SparseCore 0:
  14.5 81.7 all-gather.6
  98.6 86.3 all-gather.8
  187.3 100.7 all-gather.10
  290.1 70.1 all-gather.12
  362.3 70.9 all-gather.14
  435.2 70.9 all-gather.16
  907.2 117.3 reduce-scatter.4
  1027.1 40.6 reduce-scatter.10
  1082.8 39.0 reduce-scatter.6
  1139.2 29.6 reduce-scatter.8

commit v4 on v3

--- a/solution.py
+++ b/solution.py
@@ -555,6 +555,7 @@
     gate, upward, mixed = mix_forward(feed_in, gate_mat, up_mat)
     feed_own, *sent = product_blocks([mixed], [down_mat], half)
     sent = send_all(sent)
+    feed_left = feed_in
     feed_out = sum_of(feed_own, sent)
     layer_output = join_absolute(
         (hidden_mid + rms_norm(feed_out, feed_post)).astype(bf16)
@@ -633,6 +634,8 @@
             self.own = jnp.where(is_high, high, low)
             self.other = jnp.where(is_high, low, high).astype(bf16)
             return self.other
+
+    CoreReduction = Reduction
 
     def near_send(*sums):
         sent = sums[0].other
@@ -663,12 +666,12 @@
     d_tied = (after(d_gate, *down_sum.packed), after(d_upward, *down_sum.packed))
     d_feed_own, *packed = product_blocks(d_tied, [gate_mat, up_mat], half)
     sent = send_all(packed)
-    gate_sum = Reduction(after(feed_in, *packed), d_gate)
+    gate_sum = CoreReduction(after(feed_left, *packed), d_gate)
     gate_sum.core_pack()
     gate_sum.core_send()
     down_sum.far_pack(*gate_sum.packed)
     down_sum.far_send()
-    up_sum = Reduction(after(feed_in, *down_sum.packed), d_upward)
+    up_sum = CoreReduction(after(feed_left, *down_sum.packed), d_upward)
     up_sum.core_pack()
     up_sum.core_send()
     gate_sum.y_pack(*up_sum.packed)
@@ -718,12 +721,13 @@
     down_sum.near_pack(*query_sum.packed)
     near_send(down_sum)
     last = [down_sum.other]
-    up_sum.far_pack(*last)
-    up_sum.far_send()
-    query_sum.y_pack(*up_sum.packed)
+    query_sum.y_pack(*last)
     query_sum.y_send()
     query_part = contract(after(d_query_pre, *query_sum.packed), query_mat, 1, 1)
     last = [query_part]
+    up_sum.far_pack(query_part)
+    up_sum.far_send()
+    last = up_sum.packed
     gate_sum.near_pack(*last)
     near_send(gate_sum)
     last = [gate_sum.other]
@@ -753,13 +757,15 @@
     up_sum.near_pack(*keyvalue_sum.packed)
     near_send(up_sum)
     keyvalue_sum.sum_y()
-    out_grad = out_sum.finish_ctx().T
-    query_grad = query_sum.finish_ctx()
+    joint = jnp.concatenate([out_sum.total, query_sum.total], axis=1)
+    joint = lax.psum_scatter(joint, "ctx", scatter_dimension=0, tiled=True).astype(f32)
+    joint = after(joint, keyvalue_sum.total)
+    out_grad, query_grad = joint[:, :query_width].T, joint[:, query_width:]
     attend_grad = keyvalue_sum.finish_ctx()
 
     in_factor = lax.rsqrt(jnp.mean(inputs * inputs, axis=-1, keepdims=True) + epsilon)
     pre_attend_part = jnp.sum(
-        after(d_attend_part, *keyvalue_sum.packed) * inputs * in_factor, axis=0
+        after(d_attend_part, keyvalue_sum.total) * inputs * in_factor, axis=0
     )
     gain_grads = jnp.stack([pre_attend_part, post_attend_part, pre_feed_part, post_feed_part])
 

time: 1190 us -> 1170 us (0.983)
  waiting for transfers between devices: 645 us -> 631 us
    ppermute x5, waiting for transfers between devices: 26.5 us -> 3.13 us  [swap_sum(): values = values + lax.ppermute(values, axis, pairs)]
    ppermute x1, waiting for transfers between devices: 0.01 us -> 20 us  [body(): got = lax.ppermute(d_attend_sent, 'tensor', x_swap)]
    reduce_scatter x3 -> x1, waiting for transfers between devices: 25.9 us -> 12.9 us  [finish_ctx(): lax.psum_scatter(self.total, 'ctx', scatter_dimension=0, tiled=True)]
    unnamed x174 -> x202, local copies, waits for them, and re-layouts: 34.7 us -> 36.3 us
  transfers between devices with their start and end apart: 67 -> 66, of which waited for: 32 -> 32; matrix products, arithmetic and copies ran while one was open for 19% -> 19% of each run, Pallas kernels for 10% -> 11%
where the time goes in v4:
time: 1170 us; the launch traced here: 1160 us
  waiting for transfers between devices  631 us (54%)
  Pallas kernels  139 us (12%)
  other arithmetic  138 us (12%)
  starting transfers between devices  88.1 us (8%)
  matrix products  82.6 us (7%)
  local copies, waits for them, and re-layouts  62.7 us (5%)
  between operations  15.8 us (1%)
    ppermute x3, waiting for transfers between devices, far_start(): lax.ppermute(block, 'ctx', far_shift(s))  150 us
    ppermute x6, waiting for transfers between devices, join_all(): parts.append(lax.ppermute(own, ('ctx', 'tensor'), pairs))  97.6 us
    ppermute x3, waiting for transfers between devices, near_send(): got = lax.ppermute(sent, 'ctx', near_swap).astype(f32)  86.3 us
    ppermute x1, waiting for transfers between devices, body(): gate_got = lax.ppermute(gate_other, 'ctx', near_swap)  70.3 us
    dot_general x10, matrix products, contract(): lax.dot_general(left, right, (((left_dim,), (right_dim,)), ((), ())), pre...  66.9 us
    ppermute x6, waiting for transfers between devices, send_all(): lax.ppermute(part, ('ctx', 'tensor'), pairs)  54.4 us
    pallas_call x2, Pallas kernels, product_blocks(): pl.pallas_call(functools.partial(spread_kernel, len(lefts), half), grid=(...  45.4 us
    ppermute x3, waiting for transfers between devices, line_step(): from_right.append(lax.ppermute(right_block, 'ctx', left_pairs))  39.6 us
  transfers between devices with their start and end apart: 66, of which 32 were waited for; matrix products, arithmetic and copies ran while one was open for 19% of the time, Pallas kernels for 11%

profile of v4, /device:TPU:0, one launch (start us, length us, event | category | flops | bytes accessed | tf_op | source)
XLA Modules:
  0.0 1157.7 jit_solution(5600246313263376523)
XLA Ops:
  26.7 70.3 %collective-permute-done.2 = bf16[144,2304]{1,0:T(8,128)(2,1)} collective-permute-done((bf16[144,2304]{1,0:T(8,128)(2,1)S(1)}, bf16[144,2304]{1,0:T(8,128)(2,1)}, u32[]{:S(2)}, u32[]{:S(2)}) %collective-permute-start.2) | collective-permute-done | bytes 663584 | tf_op jit(solution)/shard_map/ppermute | solution.py:481
  121.0 67.6 %collective-permute-done.3 = bf16[288,2304]{1,0:T(8,128)(2,1)} collective-permute-done((bf16[288,2304]{1,0:T(8,128)(2,1)}, bf16[288,2304]{1,0:T(8,128)(2,1)}, u32[]{:S(2)}, u32[]{:S(2)}) %collective-permute-start.3) | collective-permute-done | bytes 1327136 | tf_op jit(solution)/shard_map/ppermute | solution.py:476
  194.6 4.6 collective-permute-start.1
  199.6 31.5 %collective-permute-done.5 = bf16[512,1024]{1,0:T(8,128)(2,1)S(1)} collective-permute-done((bf16[512,1024]{1,0:T(8,128)(2,1)S(1)}, bf16[512,1024]{1,0:T(8,128)(2,1)S(1)}, u32[]{:S(2)}, u32[]{:S(2)}) %collective-permute-start.5) | collective-permute-done | bytes 1048608 | tf_op jit(solution)/shard_map/ppermute | solution.py:516
  232.5 4.1 collective-permute-done.1
  238.3 67.2 %collective-permute-done.9 = bf16[288,2304]{1,0:T(8,128)(2,1)S(1)} collective-permute-done((bf16[288,2304]{1,0:T(8,128)(2,1)}, bf16[288,2304]{1,0:T(8,128)(2,1)S(1)}, u32[]{:S(2)}, u32[]{:S(2)}) %collective-permute-start.9) | collective-permute-done | bytes 1327136 | tf_op jit(solution)/shard_map/ppermute | solution.py:476
  313.0 26.3 %collective-permute-start.14 = (bf16[288,2304]{1,0:T(8,128)(2,1)}, bf16[288,2304]{1,0:T(8,128)(2,1)}, u32[]{:S(2)}, u32[]{:S(2)}) collective-permute-start(bf16[288,2304]{1,0:T(8,128)(2,1)} %pad_maximum_fusion.13), channel_id=1, source_target_pairs={{0,4},{2,6},{4,0},{6,2},{1,5},{3,7},{5,1},{7,3},{8,12},{10,14},{12... | collective-permute-start | bytes 3981320 | tf_op jit(solution)/shard_map/ppermute | solution.py:476
  339.3 7.1 fusion.65.pre_ref
  346.4 8.1 collective-permute-done.8
  359.2 12.0 %attend_forward.1 = (bf16[512,1024]{1,0:T(8,128)(2,1)S(1)}, f32[512,1024]{1,0:T(8,128)S(1)}, bf16[512,1024]{1,0:T(8,128)(2,1)S(1)}, f32[4,1,512]{2,1,0:T(1,128)S(1)}) custom-call(f32[512,1024]{1,0:T(8,128)} %fusion.65.pre_ref, bf16[2048,1024]{1,0:T(8,128)(2,1)} %pad_maximum_fusion.3.kv_ref, f32[512,128]{1,0:T(8,128)S(1)} %get-tuple-element.211.cos_ref, ...), custom_call_target="tpu_custom_call" | custom-call | flops 524288 | bytes 524288 | tf_op jit(solution)/shard_map/attend_forward/pallas_call | solution.py:96
  373.6 5.1 convolution_convert_fusion.6
  380.6 15.2 %collective-permute-done.14 = bf16[288,2304]{1,0:T(8,128)(2,1)} collective-permute-done((bf16[288,2304]{1,0:T(8,128)(2,1)}, bf16[288,2304]{1,0:T(8,128)(2,1)}, u32[]{:S(2)}, u32[]{:S(2)}) %collective-permute-start.14) | collective-permute-done | bytes 1327136 | tf_op jit(solution)/shard_map/ppermute | solution.py:476
  395.7 8.3 collective-permute-done.10
  407.7 4.6 multiply_reduce_fusion.10
  418.9 24.5 %collective-permute-done.11 = bf16[256,2304]{1,0:T(8,128)(2,1)S(1)} collective-permute-done((bf16[256,2304]{1,0:T(8,128)(2,1)S(1)}, bf16[256,2304]{1,0:T(8,128)(2,1)S(1)}, u32[]{:S(2)}, u32[]{:S(2)}) %collective-permute-start.11) | collective-permute-done | bytes 1179680 | tf_op jit(solution)/shard_map/ppermute | solution.py:423
  445.9 20.3 %collective-permute-done.13 = bf16[256,2304]{1,0:T(8,128)(2,1)S(1)} collective-permute-done((bf16[256,2304]{1,0:T(8,128)(2,1)S(1)}, bf16[256,2304]{1,0:T(8,128)(2,1)S(1)}, u32[]{:S(2)}, u32[]{:S(2)}) %collective-permute-start.13) | collective-permute-done | bytes 1179680 | tf_op jit(solution)/shard_map/ppermute | solution.py:423
  469.0 29.3 %mix_forward.1 = (f32[1024,2304]{1,0:T(8,128)}, f32[1024,2304]{1,0:T(8,128)}, bf16[1024,2304]{1,0:T(8,128)(2,1)}) custom-call(bf16[1024,2304]{1,0:T(8,128)(2,1)} %pad_maximum_fusion.1.x_ref, bf16[2304,2304]{1,0:T(8,128)(2,1)} %all-gather.13.cloned.1.call-done.gate_mat_ref.refs_2_, bf16[2304,2304]{1,0:T(8,128)(2,1)} %all-gather.15.cloned.1.call-done.up_mat_ref.refs_3_), custom_call_target="tpu_custom_call" | custom-call | flops 1000000 | bytes 1000000 | tf_op jit(solution)/shard_map/mix_forward/pallas_call | solution.py:263
  498.2 8.0 all-gather.17.cloned.1.call-done.refs_1_.down_mat_ref
  506.2 16.4 %product_blocks.2 = (f32[256,2304]{1,0:T(8,128)}, bf16[256,2304]{1,0:T(8,128)(2,1)}, bf16[256,2304]{1,0:T(8,128)(2,1)}, bf16[256,2304]{1,0:T(8,128)(2,1)}) custom-call(bf16[1024,2304]{1,0:T(8,128)(2,1)} %get-tuple-element.82.refs_0_, bf16[2304,2304]{1,0:T(8,128)(2,1)} %all-gather.17.cloned.1.call-done.refs_1_.down_mat_ref), custom_call_target="tpu_custom_call" | custom-call | flops 1000000 | bytes 1000000 | tf_op jit(solution)/shard_map/product_blocks/pallas_call | solution.py:318
  526.0 25.0 %collective-permute-done.15 = bf16[256,2304]{1,0:T(8,128)(2,1)} collective-permute-done((bf16[256,2304]{1,0:T(8,128)(2,1)}, bf16[256,2304]{1,0:T(8,128)(2,1)}, u32[]{:S(2)}, u32[]{:S(2)}) %collective-permute-start.15) | collective-permute-done | bytes 1179680 | tf_op jit(solution)/shard_map/ppermute | solution.py:431
  553.2 24.3 %collective-permute-done.17 = bf16[256,2304]{1,0:T(8,128)(2,1)} collective-permute-done((bf16[256,2304]{1,0:T(8,128)(2,1)}, bf16[256,2304]{1,0:T(8,128)(2,1)}, u32[]{:S(2)}, u32[]{:S(2)}) %collective-permute-start.17) | collective-permute-done | bytes 1179680 | tf_op jit(solution)/shard_map/ppermute | solution.py:431
  588.7 24.8 %collective-permute-done.19 = bf16[256,2304]{1,0:T(8,128)(2,1)} collective-permute-done((bf16[256,2304]{1,0:T(8,128)(2,1)}, bf16[256,2304]{1,0:T(8,128)(2,1)}, u32[]{:S(2)}, u32[]{:S(2)}) %collective-permute-start.19) | collective-permute-done | bytes 1179680 | tf_op jit(solution)/shard_map/ppermute | solution.py:423
  615.9 23.1 %collective-permute-done.21 = bf16[256,2304]{1,0:T(8,128)(2,1)} collective-permute-done((bf16[256,2304]{1,0:T(8,128)(2,1)}, bf16[256,2304]{1,0:T(8,128)(2,1)}, u32[]{:S(2)}, u32[]{:S(2)}) %collective-permute-start.21) | collective-permute-done | bytes 1179680 | tf_op jit(solution)/shard_map/ppermute | solution.py:423
  639.0 14.7 %convolution_convert_fusion.2 = bf16[2304,2304]{1,0:T(8,128)(2,1)S(1)} fusion(bf16[1024,2304]{1,0:T(8,128)(2,1)} %get-tuple-element.82.refs_0_, bf16[256,2304]{1,0:T(8,128)(2,1)} %collective-permute-done.21, bf16[256,2304]{1,0:T(8,128)(2,1)} %collective-permute-done.20, bf16[256,2304]{1,0:T(8,128)(2,1)} %collective-permute-done.19, ...), kind=kOutput, calls=%fused_computation.2 | convolution fusion | flops 10895818752 | bytes 20054016 | tf_op jit(solution)/shard_map/dot_general | solution.py:330
  659.8 5.4 pad_maximum_fusion.2.d_ref
  665.2 4.8 add_convert_fusion.5
  670.4 23.3 %mix_backward.1 = (bf16[1024,2304]{1,0:T(8,128)(2,1)}, bf16[1024,2304]{1,0:T(8,128)(2,1)}) custom-call(bf16[1024,2304]{1,0:T(8,128)(2,1)} %pad_maximum_fusion.2.d_ref, bf16[2304,2304]{1,0:T(8,128)(2,1)} %all-gather.17.cloned.1.call-done.refs_1_.down_mat_ref, f32[1024,2304]{1,0:T(8,128)} %get-tuple-element.90.gate_ref, f32[1024,2304]{1,0:T(8,128)} %get-tuple-element.91.up_ref), custom_call_target="tpu_custom_call" | custom-call | flops 1000000 | bytes 1000000 | tf_op jit(solution)/shard_map/mix_backward/pallas_call | solution.py:288
  693.7 29.1 %product_blocks.3 = (f32[256,2304]{1,0:T(8,128)}, bf16[256,2304]{1,0:T(8,128)(2,1)}, bf16[256,2304]{1,0:T(8,128)(2,1)}, bf16[256,2304]{1,0:T(8,128)(2,1)}) custom-call(bf16[1024,2304]{1,0:T(8,128)(2,1)} %get-tuple-element.93.refs_0_, bf16[1024,2304]{1,0:T(8,128)(2,1)} %get-tuple-element.95.refs_1_, ...), custom_call_target="tpu_custom_call" | custom-call | flops 1000000 | bytes 1000000 | tf_op jit(solution)/shard_map/product_blocks/pallas_call | solution.py:318
  726.3 14.1 %convolution_convert_fusion.1 = bf16[2304,2304]{1,0:T(8,128)(2,1)S(1)} fusion(bf16[1024,2304]{1,0:T(8,128)(2,1)S(1)} %bitcast.54, bf16[1024,2304]{1,0:T(8,128)(2,1)} %get-tuple-element.93.refs_0_), kind=kOutput, calls=%fused_computation.1 | convolution fusion | flops 10876944384 | bytes 20054016 | tf_op jit(solution)/shard_map/dot_general | solution.py:330
  747.0 4.3 add_convert_fusion.4
  754.1 12.4 %convolution_convert_fusion = bf16[2304,2304]{1,0:T(8,128)(2,1)S(1)} fusion(bf16[1024,2304]{1,0:T(8,128)(2,1)S(1)} %bitcast.54, bf16[1024,2304]{1,0:T(8,128)(2,1)S(1)} %bitcast.58), kind=kOutput, calls=%fused_computation | convolution fusion | flops 10876944384 | bytes 20054016 | tf_op jit(solution)/shard_map/dot_general | solution.py:330
  769.1 5.1 add_convert_fusion.3
  791.5 19.0 %collective-permute-done.29 = bf16[256,2304]{1,0:T(8,128)(2,1)S(1)} collective-permute-done((bf16[256,2304]{1,0:T(8,128)(2,1)S(1)}, bf16[256,2304]{1,0:T(8,128)(2,1)S(1)}, u32[]{:S(2)}, u32[]{:S(2)}) %collective-permute-start.29) | collective-permute-done | bytes 1179680 | tf_op jit(solution)/shard_map/ppermute | solution.py:686
  810.6 6.0 convolution_convert_fusion.7.da_ref
  822.6 20.8 %collective-permute-done.32 = bf16[576,2304]{1,0:T(8,128)(2,1)S(1)} collective-permute-done((bf16[576,2304]{1,0:T(8,128)(2,1)S(1)}, bf16[576,2304]{1,0:T(8,128)(2,1)S(1)}, u32[]{:S(2)}, u32[]{:S(2)}) %collective-permute-start.32) | collective-permute-done | bytes 2654240 | tf_op jit(solution)/shard_map/ppermute | solution.py:591
  856.3 29.0 %attend_backward.1 = (bf16[512,1024]{1,0:T(8,128)(2,1)S(1)}, bf16[2048,1024]{1,0:T(8,128)(2,1)}) custom-call(bf16[512,1024]{1,0:T(8,128)(2,1)S(1)} %get-tuple-element.105.q_ref, bf16[2048,1024]{1,0:T(8,128)(2,1)} %pad_maximum_fusion.3.kv_ref, bf16[512,1024]{1,0:T(8,128)(2,1)S(1)} %copy-done.1, f32[512,1024]{1,0:T(8,128)} %copy-done, ...), custom_call_target="tpu_custom_call" | custom-call | flops 524288 | bytes 524288 | tf_op jit(solution)/shard_map/attend_backward/pallas_call | solution.py:190
  886.3 21.9 %collective-permute-done.35 = bf16[288,2304]{1,0:T(8,128)(2,1)} collective-permute-done((bf16[288,2304]{1,0:T(8,128)(2,1)}, bf16[288,2304]{1,0:T(8,128)(2,1)}, u32[]{:S(2)}, u32[]{:S(2)}) %collective-permute-start.35) | collective-permute-done | bytes 1327136 | tf_op jit(solution)/shard_map/ppermute | solution.py:625
  925.6 39.4 %collective-permute-done.56 = bf16[144,2304]{1,0:T(8,128)(2,1)S(1)} collective-permute-done((bf16[144,2304]{1,0:T(8,128)(2,1)S(1)}, bf16[144,2304]{1,0:T(8,128)(2,1)S(1)}, u32[]{:S(2)}, u32[]{:S(2)}) %collective-permute-start.56) | collective-permute-done | bytes 663584 | tf_op jit(solution)/shard_map/ppermute | solution.py:644
  968.4 4.3 fusion.66
  972.7 4.4 add_convert_fusion
  984.5 5.6 collective-permute-done.38
  990.1 5.1 collective-permute-start.54
  997.1 32.6 %collective-permute-done.53 = bf16[144,2304]{1,0:T(8,128)(2,1)S(1)} collective-permute-done((bf16[144,2304]{1,0:T(8,128)(2,1)S(1)}, bf16[144,2304]{1,0:T(8,128)(2,1)S(1)}, u32[]{:S(2)}, u32[]{:S(2)}) %collective-permute-start.53) | collective-permute-done | bytes 663584 | tf_op jit(solution)/shard_map/ppermute | solution.py:644
  1065.1 20.0 %collective-permute-done.42 = bf16[256,2304]{1,0:T(8,128)(2,1)S(1)} collective-permute-done((bf16[256,2304]{1,0:T(8,128)(2,1)}, bf16[256,2304]{1,0:T(8,128)(2,1)S(1)}, u32[]{:S(2)}, u32[]{:S(2)}) %collective-permute-start.42) | collective-permute-done | bytes 1179680 | tf_op jit(solution)/shard_map/ppermute | solution.py:753
  1091.8 3.9 multiply_reduce_fusion
  1100.1 14.3 %collective-permute-done.55 = bf16[144,2304]{1,0:T(8,128)(2,1)} collective-permute-done((bf16[144,2304]{1,0:T(8,128)(2,1)}, bf16[144,2304]{1,0:T(8,128)(2,1)}, u32[]{:S(2)}, u32[]{:S(2)}) %collective-permute-start.55) | collective-permute-done | bytes 663584 | tf_op jit(solution)/shard_map/ppermute | solution.py:644
  1120.0 6.5 collective-permute-done.43
  1135.3 12.9 %reduce-scatter.8.cloned.1.call-done = bf16[144,1024]{1,0:T(8,128)(2,1)} async-done(((bf16[576,1024]{1,0:T(8,128)(2,1)}), bf16[144,1024]{1,0:T(8,128)(2,1)}) %reduce-scatter.8.cloned.1.call-update) | async-done | bytes 294928 | tf_op jit(solution)/shard_map/reduce_scatter | solution.py:603
  (449 shorter events, 255.3 us)
Async XLA Ops:
  7.2 99.5 %all-gather.7.cloned.1.call-start = ((), (), s32[]{:S(2)}) async-start(), calls=%async_computation.3 | async-start | bytes 5640192 | tf_op jit(solution)/shard_map/all_gather | solution.py:459
  14.4 325.0 %all-gather.9.cloned.1.call-start = ((), (), s32[]{:S(2)}) async-start(), calls=%async_computation.4 | async-start | bytes 5013504 | tf_op jit(solution)/shard_map/all_gather | solution.py:460
  15.1 358.4 %all-gather.11.cloned.1.call-start = ((), (), s32[]{:S(2)}) async-start(), calls=%async_computation.5 | async-start | bytes 5013504 | tf_op jit(solution)/shard_map/all_gather | solution.py:461
  18.3 83.6 %collective-permute-start = (bf16[288,2304]{1,0:T(8,128)(2,1)}, bf16[288,2304]{1,0:T(8,128)(2,1)}, u32[]{:S(2)}, u32[]{:S(2)}) collective-permute-start(bf16[288,2304]{1,0:T(8,128)(2,1)} %pad_maximum_fusion.11), channel_id=1, source_target_pairs={{0,2},{2,0},{4,6},{6,4},{1,3},{3,1},{5,7},{7,5},{8,10},{10,8},{12,... | collective-permute-start | bytes 3981320 | tf_op jit(solution)/shard_map/ppermute | solution.py:482
  21.4 75.6 %collective-permute-start.2 = (bf16[144,2304]{1,0:T(8,128)(2,1)S(1)}, bf16[144,2304]{1,0:T(8,128)(2,1)}, u32[]{:S(2)}, u32[]{:S(2)}) collective-permute-start(bf16[144,2304]{1,0:T(8,128)(2,1)S(1)} %broadcast_select_fusion.17), channel_id=1, source_target_pairs={{0,2},{2,0},{4,6},{6,4},{1,3},{3,1},{5,7},{7,5},{8,10},{10,8},{12,... | collective-permute-start | bytes 1990664 | tf_op jit(solution)/shard_map/ppermute | solution.py:481
  21.5 447.5 %all-gather.13.cloned.1.call-start = ((), (), s32[]{:S(2)}) async-start(), calls=%async_computation.6 | async-start | bytes 13271040 | tf_op jit(solution)/shard_map/all_gather | solution.py:521
  100.2 88.4 %collective-permute-start.3 = (bf16[288,2304]{1,0:T(8,128)(2,1)}, bf16[288,2304]{1,0:T(8,128)(2,1)}, u32[]{:S(2)}, u32[]{:S(2)}) collective-permute-start(bf16[288,2304]{1,0:T(8,128)(2,1)} %pad_maximum_fusion.14), channel_id=1, source_target_pairs={{0,4},{2,6},{4,0},{6,2},{1,5},{3,7},{5,1},{7,3},{8,12},{10,14},{12... | collective-permute-start | bytes 3981320 | tf_op jit(solution)/shard_map/ppermute | solution.py:476
  192.1 276.9 %all-gather.15.cloned.1.call-start = ((), (), s32[]{:S(2)}) async-start(), calls=%async_computation.7 | async-start | bytes 13271040 | tf_op jit(solution)/shard_map/all_gather | solution.py:540
  193.3 37.9 %collective-permute-start.5 = (bf16[512,1024]{1,0:T(8,128)(2,1)S(1)}, bf16[512,1024]{1,0:T(8,128)(2,1)S(1)}, u32[]{:S(2)}, u32[]{:S(2)}) collective-permute-start(bf16[512,1024]{1,0:T(8,128)(2,1)S(1)} %copy-done.48), channel_id=1, source_target_pairs={{2,0},{4,2},{6,4},{3,1},{5,3},{7,5},{10,8},{12,10},{14,12},{11,9},... | collective-permute-start | bytes 3145736 | tf_op jit(solution)/shard_map/ppermute | solution.py:516
  194.6 42.0 %collective-permute-start.1 = (bf16[512,1024]{1,0:T(8,128)(2,1)S(1)}, bf16[512,1024]{1,0:T(8,128)(2,1)S(1)}, u32[]{:S(2)}, u32[]{:S(2)}) collective-permute-start(bf16[512,1024]{1,0:T(8,128)(2,1)S(1)} %copy-done.48), channel_id=1, source_target_pairs={{0,2},{2,4},{4,6},{1,3},{3,5},{5,7},{8,10},{10,12},{12,14},{9,11},... | collective-permute-start | bytes 3145736 | tf_op jit(solution)/shard_map/ppermute | solution.py:515
  199.2 106.3 %collective-permute-start.9 = (bf16[288,2304]{1,0:T(8,128)(2,1)}, bf16[288,2304]{1,0:T(8,128)(2,1)S(1)}, u32[]{:S(2)}, u32[]{:S(2)}) collective-permute-start(bf16[288,2304]{1,0:T(8,128)(2,1)} %pad_maximum_fusion.12), channel_id=1, source_target_pairs={{0,4},{2,6},{4,0},{6,2},{1,5},{3,7},{5,1},{7,3},{8,12},{10,14},{12... | collective-permute-start | bytes 3981320 | tf_op jit(solution)/shard_map/ppermute | solution.py:476
  231.2 74.3 %collective-permute-start.6 = (bf16[512,1024]{1,0:T(8,128)(2,1)S(1)}, bf16[512,1024]{1,0:T(8,128)(2,1)}, u32[]{:S(2)}, u32[]{:S(2)}) collective-permute-start(bf16[512,1024]{1,0:T(8,128)(2,1)S(1)} %collective-permute-done.5), channel_id=1, source_target_pairs={{2,0},{4,2},{3,1},{5,3},{10,8},{12,10},{11,9},{13,11},{18,16},{20,... | collective-permute-start | bytes 3145736 | tf_op jit(solution)/shard_map/ppermute | solution.py:516
  236.6 68.9 %collective-permute-start.4 = (bf16[512,1024]{1,0:T(8,128)(2,1)S(1)}, bf16[512,1024]{1,0:T(8,128)(2,1)}, u32[]{:S(2)}, u32[]{:S(2)}) collective-permute-start(bf16[512,1024]{1,0:T(8,128)(2,1)S(1)} %collective-permute-done.1), channel_id=1, source_target_pairs={{2,4},{4,6},{3,5},{5,7},{10,12},{12,14},{11,13},{13,15},{18,20},{2... | collective-permute-start | bytes 3145736 | tf_op jit(solution)/shard_map/ppermute | solution.py:515
  307.8 198.4 %all-gather.17.cloned.1.call-start = ((), (), s32[]{:S(2)}) async-start(), calls=%async_computation.8 | async-start | bytes 13271040 | tf_op jit(solution)/shard_map/all_gather | solution.py:550
  307.8 46.7 %collective-permute-start.8 = (bf16[512,1024]{1,0:T(8,128)(2,1)}, bf16[512,1024]{1,0:T(8,128)(2,1)}, u32[]{:S(2)}, u32[]{:S(2)}) collective-permute-start(bf16[512,1024]{1,0:T(8,128)(2,1)} %collective-permute-done.6), channel_id=1, source_target_pairs={{2,0},{3,1},{10,8},{11,9},{18,16},{19,17},{26,24},{27,25}} | collective-permute-start | bytes 3145736 | tf_op jit(solution)/shard_map/ppermute | solution.py:516
  309.1 45.4 %collective-permute-start.7 = (bf16[512,1024]{1,0:T(8,128)(2,1)}, bf16[512,1024]{1,0:T(8,128)(2,1)}, u32[]{:S(2)}, u32[]{:S(2)}) collective-permute-start(bf16[512,1024]{1,0:T(8,128)(2,1)} %collective-permute-done.4), channel_id=1, source_target_pairs={{4,6},{5,7},{12,14},{13,15},{20,22},{21,23},{28,30},{29,31}} | collective-permute-start | bytes 3145736 | tf_op jit(solution)/shard_map/ppermute | solution.py:515
  313.0 82.7 %collective-permute-start.14 = (bf16[288,2304]{1,0:T(8,128)(2,1)}, bf16[288,2304]{1,0:T(8,128)(2,1)}, u32[]{:S(2)}, u32[]{:S(2)}) collective-permute-start(bf16[288,2304]{1,0:T(8,128)(2,1)} %pad_maximum_fusion.13), channel_id=1, source_target_pairs={{0,4},{2,6},{4,0},{6,2},{1,5},{3,7},{5,1},{7,3},{8,12},{10,14},{12... | collective-permute-start | bytes 3981320 | tf_op jit(solution)/shard_map/ppermute | solution.py:476
  407.6 624.1 %reduce-scatter.4.cloned.1.call-start = ((), (), s32[]{:S(2)}) async-start(), calls=%async_computation.9 | async-start | bytes 5242880 | tf_op jit(solution)/shard_map/reduce_scatter | solution.py:714
  417.0 49.2 %collective-permute-start.13 = (bf16[256,2304]{1,0:T(8,128)(2,1)S(1)}, bf16[256,2304]{1,0:T(8,128)(2,1)S(1)}, u32[]{:S(2)}, u32[]{:S(2)}) collective-permute-start(bf16[256,2304]{1,0:T(8,128)(2,1)S(1)} %multiply_convert_fusion.1), channel_id=1, source_target_pairs={{0,3},{1,2},{2,1},{3,0},{4,7},{5,6},{6,5},{7,4},{8,11},{9,10},{10,... | collective-permute-start | bytes 3538952 | tf_op jit(solution)/shard_map/ppermute | solution.py:423
  524.0 29.2 %collective-permute-start.16 = (bf16[256,2304]{1,0:T(8,128)(2,1)}, bf16[256,2304]{1,0:T(8,128)(2,1)}, u32[]{:S(2)}, u32[]{:S(2)}) collective-permute-start(bf16[256,2304]{1,0:T(8,128)(2,1)} %get-tuple-element.87), channel_id=1, source_target_pairs={{0,2},{1,3},{2,0},{3,1},{4,6},{5,7},{6,4},{7,5},{8,10},{9,11},{10,... | collective-permute-start | bytes 3538952 | tf_op jit(solution)/shard_map/ppermute | solution.py:431
  525.5 51.9 %collective-permute-start.17 = (bf16[256,2304]{1,0:T(8,128)(2,1)}, bf16[256,2304]{1,0:T(8,128)(2,1)}, u32[]{:S(2)}, u32[]{:S(2)}) collective-permute-start(bf16[256,2304]{1,0:T(8,128)(2,1)} %get-tuple-element.88), channel_id=1, source_target_pairs={{0,3},{1,2},{2,1},{3,0},{4,7},{5,6},{6,5},{7,4},{8,11},{9,10},{10,... | collective-permute-start | bytes 3538952 | tf_op jit(solution)/shard_map/ppermute | solution.py:431
  586.7 29.2 %collective-permute-start.20 = (bf16[256,2304]{1,0:T(8,128)(2,1)}, bf16[256,2304]{1,0:T(8,128)(2,1)}, u32[]{:S(2)}, u32[]{:S(2)}) collective-permute-start(bf16[256,2304]{1,0:T(8,128)(2,1)} %get-tuple-element.190), channel_id=1, source_target_pairs={{0,2},{1,3},{2,0},{3,1},{4,6},{5,7},{6,4},{7,5},{8,10},{9,11},{10,... | collective-permute-start | bytes 3538952 | tf_op jit(solution)/shard_map/ppermute | solution.py:423
  588.2 50.8 %collective-permute-start.21 = (bf16[256,2304]{1,0:T(8,128)(2,1)}, bf16[256,2304]{1,0:T(8,128)(2,1)}, u32[]{:S(2)}, u32[]{:S(2)}) collective-permute-start(bf16[256,2304]{1,0:T(8,128)(2,1)} %get-tuple-element.190), channel_id=1, source_target_pairs={{0,3},{1,2},{2,1},{3,0},{4,7},{5,6},{6,5},{7,4},{8,11},{9,10},{10,... | collective-permute-start | bytes 3538952 | tf_op jit(solution)/shard_map/ppermute | solution.py:423
  659.3 87.7 %collective-permute-start.23 = (bf16[576,2304]{1,0:T(8,128)(2,1)}, bf16[576,2304]{1,0:T(8,128)(2,1)}, u32[]{:S(2)}, u32[]{:S(2)}) collective-permute-start(bf16[576,2304]{1,0:T(8,128)(2,1)} %get-tuple-element.159), channel_id=1, source_target_pairs={{0,8},{8,0},{16,24},{24,16},{1,9},{9,1},{17,25},{25,17},{2,10},{10... | collective-permute-start | bytes 7962632 | tf_op jit(solution)/shard_map/ppermute | solution.py:577
  670.0 77.0 %collective-permute-start.24 = (bf16[576,2304]{1,0:T(8,128)(2,1)}, bf16[576,2304]{1,0:T(8,128)(2,1)}, u32[]{:S(2)}, u32[]{:S(2)}) collective-permute-start(bf16[576,2304]{1,0:T(8,128)(2,1)} %add_convert_fusion.5), channel_id=1, source_target_pairs={{0,16},{8,24},{16,0},{24,8},{1,17},{9,25},{17,1},{25,9},{2,18},{10... | collective-permute-start | bytes 7962632 | tf_op jit(solution)/shard_map/ppermute | solution.py:591
  722.8 51.4 %collective-permute-start.26 = (bf16[256,2304]{1,0:T(8,128)(2,1)}, bf16[256,2304]{1,0:T(8,128)(2,1)}, u32[]{:S(2)}, u32[]{:S(2)}) collective-permute-start(bf16[256,2304]{1,0:T(8,128)(2,1)} %get-tuple-element.97), channel_id=1, source_target_pairs={{0,1},{1,0},{2,3},{3,2},{4,5},{5,4},{6,7},{7,6},{8,9},{9,8},{10,11... | collective-permute-start | bytes 3538952 | tf_op jit(solution)/shard_map/ppermute | solution.py:431
  724.5 49.8 %collective-permute-start.27 = (bf16[256,2304]{1,0:T(8,128)(2,1)}, bf16[256,2304]{1,0:T(8,128)(2,1)}, u32[]{:S(2)}, u32[]{:S(2)}) collective-permute-start(bf16[256,2304]{1,0:T(8,128)(2,1)} %get-tuple-element.98), channel_id=1, source_target_pairs={{0,2},{1,3},{2,0},{3,1},{4,6},{5,7},{6,4},{7,5},{8,10},{9,11},{10,... | collective-permute-start | bytes 3538952 | tf_op jit(solution)/shard_map/ppermute | solution.py:431
  725.9 51.2 %collective-permute-start.28 = (bf16[256,2304]{1,0:T(8,128)(2,1)}, bf16[256,2304]{1,0:T(8,128)(2,1)}, u32[]{:S(2)}, u32[]{:S(2)}) collective-permute-start(bf16[256,2304]{1,0:T(8,128)(2,1)} %get-tuple-element.99), channel_id=1, source_target_pairs={{0,3},{1,2},{2,1},{3,0},{4,7},{5,6},{6,5},{7,4},{8,11},{9,10},{10,... | collective-permute-start | bytes 3538952 | tf_op jit(solution)/shard_map/ppermute | solution.py:431
  785.4 58.1 %collective-permute-start.32 = (bf16[576,2304]{1,0:T(8,128)(2,1)S(1)}, bf16[576,2304]{1,0:T(8,128)(2,1)S(1)}, u32[]{:S(2)}, u32[]{:S(2)}) collective-permute-start(bf16[576,2304]{1,0:T(8,128)(2,1)S(1)} %add_convert_fusion.3), channel_id=1, source_target_pairs={{0,16},{8,24},{16,0},{24,8},{1,17},{9,25},{17,1},{25,9},{2,18},{10... | collective-permute-start | bytes 7962632 | tf_op jit(solution)/shard_map/ppermute | solution.py:591
  786.8 56.6 %collective-permute-start.31 = (bf16[576,2304]{1,0:T(8,128)(2,1)S(1)}, bf16[576,2304]{1,0:T(8,128)(2,1)}, u32[]{:S(2)}, u32[]{:S(2)}) collective-permute-start(bf16[576,2304]{1,0:T(8,128)(2,1)S(1)} %copy-done.53), channel_id=1, source_target_pairs={{0,8},{8,0},{16,24},{24,16},{1,9},{9,1},{17,25},{25,17},{2,10},{10... | collective-permute-start | bytes 7962632 | tf_op jit(solution)/shard_map/ppermute | solution.py:577
  786.8 66.8 %collective-permute-start.33 = (bf16[288,2304]{1,0:T(8,128)(2,1)}, bf16[288,2304]{1,0:T(8,128)(2,1)}, u32[]{:S(2)}, u32[]{:S(2)}) collective-permute-start(bf16[288,2304]{1,0:T(8,128)(2,1)} %broadcast_select_fusion.2), channel_id=1, source_target_pairs={{0,4},{2,6},{4,0},{6,2},{1,5},{3,7},{5,1},{7,3},{8,12},{10,14},{12... | collective-permute-start | bytes 3981320 | tf_op jit(solution)/shard_map/ppermute | solution.py:625
  849.8 58.5 %collective-permute-start.35 = (bf16[288,2304]{1,0:T(8,128)(2,1)}, bf16[288,2304]{1,0:T(8,128)(2,1)}, u32[]{:S(2)}, u32[]{:S(2)}) collective-permute-start(bf16[288,2304]{1,0:T(8,128)(2,1)} %broadcast_select_fusion.1), channel_id=1, source_target_pairs={{0,4},{2,6},{4,0},{6,2},{1,5},{3,7},{5,1},{7,3},{8,12},{10,14},{12... | collective-permute-start | bytes 3981320 | tf_op jit(solution)/shard_map/ppermute | solution.py:625
  852.2 56.2 %collective-permute-start.34 = (bf16[576,1024]{1,0:T(8,128)(2,1)}, bf16[576,1024]{1,0:T(8,128)(2,1)}, u32[]{:S(2)}, u32[]{:S(2)}) collective-permute-start(bf16[576,1024]{1,0:T(8,128)(2,1)} %get-tuple-element.167), channel_id=1, source_target_pairs={{0,8},{8,0},{16,24},{24,16},{1,9},{9,1},{17,25},{25,17},{2,10},{10... | collective-permute-start | bytes 3538952 | tf_op jit(solution)/shard_map/ppermute | solution.py:577
  852.8 67.3 %collective-permute-start.18 = (bf16[256,2304]{1,0:T(8,128)(2,1)}, bf16[256,2304]{1,0:T(8,128)(2,1)}, u32[]{:S(2)}, u32[]{:S(2)}) collective-permute-start(bf16[256,2304]{1,0:T(8,128)(2,1)} %get-tuple-element.191), channel_id=1, source_target_pairs={{0,1},{1,0},{2,3},{3,2},{4,5},{5,4},{6,7},{7,6},{8,9},{9,8},{10,11... | collective-permute-start | bytes 3538952 | tf_op jit(solution)/shard_map/ppermute | solution.py:415
  853.4 119.3 %collective-permute-start.39 = (bf16[576,2304]{1,0:T(8,128)(2,1)}, bf16[576,2304]{1,0:T(8,128)(2,1)}, u32[]{:S(2)}, u32[]{:S(2)}) collective-permute-start(bf16[576,2304]{1,0:T(8,128)(2,1)} %get-tuple-element.158), channel_id=1, source_target_pairs={{0,8},{8,0},{16,24},{24,16},{1,9},{9,1},{17,25},{25,17},{2,10},{10... | collective-permute-start | bytes 7962632 | tf_op jit(solution)/shard_map/ppermute | solution.py:577
  853.6 119.1 %collective-permute-start.40 = (bf16[576,2304]{1,0:T(8,128)(2,1)}, bf16[576,2304]{1,0:T(8,128)(2,1)}, u32[]{:S(2)}, u32[]{:S(2)}) collective-permute-start(bf16[576,2304]{1,0:T(8,128)(2,1)} %add_convert_fusion.2), channel_id=1, source_target_pairs={{0,16},{8,24},{16,0},{24,8},{1,17},{9,25},{17,1},{25,9},{2,18},{10... | collective-permute-start | bytes 7962632 | tf_op jit(solution)/shard_map/ppermute | solution.py:591
  908.3 224.7 %reduce-scatter.6.cloned.1.call-start = ((), (), s32[]{:S(2)}) async-start(), calls=%async_computation.10 | async-start | bytes 2949120 | tf_op jit(solution)/shard_map/reduce_scatter | solution.py:761
  919.6 45.5 %collective-permute-start.56 = (bf16[144,2304]{1,0:T(8,128)(2,1)S(1)}, bf16[144,2304]{1,0:T(8,128)(2,1)S(1)}, u32[]{:S(2)}, u32[]{:S(2)}) collective-permute-start(bf16[144,2304]{1,0:T(8,128)(2,1)S(1)} %select_convert_fusion.2), channel_id=1, source_target_pairs={{0,2},{2,0},{4,6},{6,4},{1,3},{3,1},{5,7},{7,5},{8,10},{10,8},{12,... | collective-permute-start | bytes 1990664 | tf_op jit(solution)/shard_map/ppermute | solution.py:644
  922.3 44.5 %collective-permute-start.36 = (bf16[576,1024]{1,0:T(8,128)(2,1)S(1)}, bf16[576,1024]{1,0:T(8,128)(2,1)S(1)}, u32[]{:S(2)}, u32[]{:S(2)}) collective-permute-start(bf16[576,1024]{1,0:T(8,128)(2,1)S(1)} %get-tuple-element.166), channel_id=1, source_target_pairs={{0,8},{8,0},{16,24},{24,16},{1,9},{9,1},{17,25},{25,17},{2,10},{10... | collective-permute-start | bytes 3538952 | tf_op jit(solution)/shard_map/ppermute | solution.py:577
  925.1 70.1 %collective-permute-start.37 = (bf16[576,1024]{1,0:T(8,128)(2,1)S(1)}, bf16[576,1024]{1,0:T(8,128)(2,1)S(1)}, u32[]{:S(2)}, u32[]{:S(2)}) collective-permute-start(bf16[576,1024]{1,0:T(8,128)(2,1)S(1)} %copy-done.58), channel_id=1, source_target_pairs={{0,8},{8,0},{16,24},{24,16},{1,9},{9,1},{17,25},{25,17},{2,10},{10... | collective-permute-start | bytes 3538952 | tf_op jit(solution)/shard_map/ppermute | solution.py:577
  966.8 83.5 %collective-permute-start.51 = (bf16[576,1024]{1,0:T(8,128)(2,1)}, bf16[576,1024]{1,0:T(8,128)(2,1)}, u32[]{:S(2)}, u32[]{:S(2)}) collective-permute-start(bf16[576,1024]{1,0:T(8,128)(2,1)} %get-tuple-element.165), channel_id=1, source_target_pairs={{0,8},{8,0},{16,24},{24,16},{1,9},{9,1},{17,25},{25,17},{2,10},{10... | collective-permute-start | bytes 3538952 | tf_op jit(solution)/shard_map/ppermute | solution.py:577
  982.2 47.5 %collective-permute-start.53 = (bf16[144,2304]{1,0:T(8,128)(2,1)S(1)}, bf16[144,2304]{1,0:T(8,128)(2,1)S(1)}, u32[]{:S(2)}, u32[]{:S(2)}) collective-permute-start(bf16[144,2304]{1,0:T(8,128)(2,1)S(1)} %select_convert_fusion.1), channel_id=1, source_target_pairs={{0,2},{2,0},{4,6},{6,4},{1,3},{3,1},{5,7},{7,5},{8,10},{10,8},{12,... | collective-permute-start | bytes 1990664 | tf_op jit(solution)/shard_map/ppermute | solution.py:644
  984.1 66.3 %collective-permute-start.52 = (bf16[576,1024]{1,0:T(8,128)(2,1)}, bf16[576,1024]{1,0:T(8,128)(2,1)}, u32[]{:S(2)}, u32[]{:S(2)}) collective-permute-start(bf16[576,1024]{1,0:T(8,128)(2,1)} %add_convert_fusion.10), channel_id=1, source_target_pairs={{0,16},{8,24},{16,0},{24,8},{1,17},{9,25},{17,1},{25,9},{2,18},{10... | collective-permute-start | bytes 3538952 | tf_op jit(solution)/shard_map/ppermute | solution.py:591
  990.1 71.9 %collective-permute-start.54 = (bf16[288,2304]{1,0:T(8,128)(2,1)}, bf16[288,2304]{1,0:T(8,128)(2,1)}, u32[]{:S(2)}, u32[]{:S(2)}) collective-permute-start(bf16[288,2304]{1,0:T(8,128)(2,1)} %broadcast_select_fusion), channel_id=1, source_target_pairs={{0,4},{2,6},{4,0},{6,2},{1,5},{3,7},{5,1},{7,3},{8,12},{10,14},{12... | collective-permute-start | bytes 3981320 | tf_op jit(solution)/shard_map/ppermute | solution.py:625
  1044.1 42.4 %collective-permute-start.44 = (bf16[576,1024]{1,0:T(8,128)(2,1)}, bf16[576,1024]{1,0:T(8,128)(2,1)}, u32[]{:S(2)}, u32[]{:S(2)}) collective-permute-start(bf16[576,1024]{1,0:T(8,128)(2,1)} %get-tuple-element.164), channel_id=1, source_target_pairs={{0,8},{8,0},{16,24},{24,16},{1,9},{9,1},{17,25},{25,17},{2,10},{10... | collective-permute-start | bytes 3538952 | tf_op jit(solution)/shard_map/ppermute | solution.py:577
  1054.7 93.5 %reduce-scatter.8.cloned.1.call-start = ((), (), s32[]{:S(2)}) async-start(), calls=%async_computation.11 | async-start | bytes 1474560 | tf_op jit(solution)/shard_map/reduce_scatter | solution.py:603
  1054.7 30.3 %collective-permute-start.42 = (bf16[256,2304]{1,0:T(8,128)(2,1)}, bf16[256,2304]{1,0:T(8,128)(2,1)S(1)}, u32[]{:S(2)}, u32[]{:S(2)}) collective-permute-start(bf16[256,2304]{1,0:T(8,128)(2,1)} %slice.456), channel_id=1, source_target_pairs={{0,1},{1,0},{2,3},{3,2},{4,5},{5,4},{6,7},{7,6},{8,9},{9,8},{10,11... | collective-permute-start | bytes 3538952 | tf_op jit(solution)/shard_map/ppermute | solution.py:753
  1065.1 49.3 %collective-permute-start.55 = (bf16[144,2304]{1,0:T(8,128)(2,1)}, bf16[144,2304]{1,0:T(8,128)(2,1)}, u32[]{:S(2)}, u32[]{:S(2)}) collective-permute-start(bf16[144,2304]{1,0:T(8,128)(2,1)} %select_convert_fusion), channel_id=1, source_target_pairs={{0,2},{2,0},{4,6},{6,4},{1,3},{3,1},{5,7},{7,5},{8,10},{10,8},{12,... | collective-permute-start | bytes 1990664 | tf_op jit(solution)/shard_map/ppermute | solution.py:644
  (115 other events, 2550.5 us)
Sparse Core Ops, SparseCore 0:
  14.5 81.7 all-gather.6
  98.6 86.3 all-gather.8
  187.3 100.7 all-gather.10
  290.1 70.1 all-gather.12
  362.3 70.9 all-gather.14
  435.2 70.9 all-gather.16
  908.4 114.8 reduce-scatter.3
  1054.8 61.4 reduce-scatter.5
  1118.8 29.4 reduce-scatter.7

commit v5 on v4

--- a/solution.py
+++ b/solution.py
@@ -432,6 +432,27 @@
             for part, pairs in zip(parts, all_swaps.values())
         ]
 
+    part = half // 2
+
+    def hop(values, bz, bx):
+        return lax.ppermute(values, ("ctx", "tensor"), all_swaps[bz, bx])
+
+    def join_by_hops(own):
+        beside, below = hop(own, 0, 1), hop(own, 1, 0)
+        corner = [hop(beside[:part], 1, 0), hop(below[part:], 0, 1)]
+        return jnp.concatenate([own, beside, below, *corner], axis=0)
+
+    def send_by_hops(parts):
+        beside, below, corner = parts
+        by_side, by_below = hop(corner[:part], 0, 1), hop(corner[part:], 1, 0)
+
+        def joined(values, got):
+            return (values.astype(f32) + got.astype(f32)).astype(bf16)
+
+        below = jnp.concatenate([joined(below[:part], by_side), below[part:]], axis=0)
+        beside = jnp.concatenate([beside[:part], joined(beside[part:], by_below)], axis=0)
+        return [hop(below, 1, 0), hop(beside, 0, 1)]
+
     def sum_of(own, parts):
         for item in parts:
             own = own + item.astype(f32)
@@ -551,10 +572,10 @@
     attend_out = contract(attended[:half], out_mat, 1, 1) + got.astype(f32)
     hidden_mid = own_inputs + rms_norm(attend_out, gain_out)
     feed_own = rms_norm(hidden_mid, feed_gain).astype(bf16)
-    feed_in = join_all(feed_own)
+    feed_in = join_by_hops(feed_own)
     gate, upward, mixed = mix_forward(feed_in, gate_mat, up_mat)
     feed_own, *sent = product_blocks([mixed], [down_mat], half)
-    sent = send_all(sent)
+    sent = send_by_hops(sent)
     feed_left = feed_in
     feed_out = sum_of(feed_own, sent)
     layer_output = join_absolute(
@@ -655,7 +676,7 @@
         return back(incoming)
 
     d_feed_out, post_feed_part = norm_back(feed_out, feed_post, cot)
-    d_feed_low = join_all(d_feed_out.astype(bf16))
+    d_feed_low = join_by_hops(d_feed_out.astype(bf16))
     down_sum = Reduction(d_feed_low, mixed)
     down_sum.core_pack()
     down_sum.core_send()

time: 1170 us -> 1150 us (0.983)
  waiting for transfers between devices: 631 us -> 604 us
  local copies, waits for them, and re-layouts: 62.7 us -> 75.3 us
    ppermute x6 -> x3, waiting for transfers between devices: 54.4 us -> 3.25 us  [send_all(): lax.ppermute(part, ('ctx', 'tensor'), pairs)]
    all_gather x1, waiting for transfers between devices: 7.98 us -> 21.6 us  [body(): down_mat = lax.all_gather(down_rows, dp_axes, axis=0, tiled=True)]
    unnamed x202 -> x210, local copies, waits for them, and re-layouts: 36.3 us -> 44.3 us
    ppermute x6 -> x12, waiting for transfers between devices: 97.6 us -> 101 us  [hop(): return lax.ppermute(values, ('ctx', 'tensor'), all_swaps[bz, bx])]
  transfers between devices with their start and end apart: 66 -> 69, of which waited for: 32 -> 33; matrix products, arithmetic and copies ran while one was open for 19% -> 20% of each run, Pallas kernels for 11% -> 11%
where the time goes in v5:
time: 1150 us; the launch traced here: 1140 us
  waiting for transfers between devices  604 us (53%)
  Pallas kernels  139 us (12%)
  other arithmetic  134 us (12%)
  starting transfers between devices  87.3 us (8%)
  matrix products  83.3 us (7%)
  local copies, waits for them, and re-layouts  75.3 us (7%)
  between operations  15.7 us (1%)
    ppermute x3, waiting for transfers between devices, far_start(): lax.ppermute(block, 'ctx', far_shift(s))  150 us
    ppermute x12, waiting for transfers between devices, hop(): return lax.ppermute(values, ('ctx', 'tensor'), all_swaps[bz, bx])  101 us
    ppermute x3, waiting for transfers between devices, near_send(): got = lax.ppermute(sent, 'ctx', near_swap).astype(f32)  84.9 us
    ppermute x1, waiting for transfers between devices, body(): gate_got = lax.ppermute(gate_other, 'ctx', near_swap)  70.3 us
    dot_general x10, matrix products, contract(): lax.dot_general(left, right, (((left_dim,), (right_dim,)), ((), ())), pre...  67.6 us
    pallas_call x2, Pallas kernels, product_blocks(): pl.pallas_call(functools.partial(spread_kernel, len(lefts), half), grid=(...  45.6 us
    unnamed x210, local copies, waits for them, and re-layouts  44.3 us
    ppermute x3, waiting for transfers between devices, line_step(): from_right.append(lax.ppermute(right_block, 'ctx', left_pairs))  39.6 us
  transfers between devices with their start and end apart: 69, of which 33 were waited for; matrix products, arithmetic and copies ran while one was open for 20% of the time, Pallas kernels for 11%

profile of v5, /device:TPU:0, one launch (start us, length us, event | category | flops | bytes accessed | tf_op | source)
XLA Modules:
  0.0 1139.3 jit_solution(439884066423542357)
XLA Ops:
  26.7 70.3 %collective-permute-done.2 = bf16[144,2304]{1,0:T(8,128)(2,1)} collective-permute-done((bf16[144,2304]{1,0:T(8,128)(2,1)S(1)}, bf16[144,2304]{1,0:T(8,128)(2,1)}, u32[]{:S(2)}, u32[]{:S(2)}) %collective-permute-start.2) | collective-permute-done | bytes 663584 | tf_op jit(solution)/shard_map/ppermute | solution.py:502
  121.0 67.6 %collective-permute-done.3 = bf16[288,2304]{1,0:T(8,128)(2,1)} collective-permute-done((bf16[288,2304]{1,0:T(8,128)(2,1)}, bf16[288,2304]{1,0:T(8,128)(2,1)}, u32[]{:S(2)}, u32[]{:S(2)}) %collective-permute-start.3) | collective-permute-done | bytes 1327136 | tf_op jit(solution)/shard_map/ppermute | solution.py:497
  194.6 4.6 collective-permute-start.1
  199.7 31.5 %collective-permute-done.5 = bf16[512,1024]{1,0:T(8,128)(2,1)S(1)} collective-permute-done((bf16[512,1024]{1,0:T(8,128)(2,1)S(1)}, bf16[512,1024]{1,0:T(8,128)(2,1)S(1)}, u32[]{:S(2)}, u32[]{:S(2)}) %collective-permute-start.5) | collective-permute-done | bytes 1048608 | tf_op jit(solution)/shard_map/ppermute | solution.py:537
  232.4 4.2 collective-permute-done.1
  238.3 67.2 %collective-permute-done.9 = bf16[288,2304]{1,0:T(8,128)(2,1)S(1)} collective-permute-done((bf16[288,2304]{1,0:T(8,128)(2,1)}, bf16[288,2304]{1,0:T(8,128)(2,1)S(1)}, u32[]{:S(2)}, u32[]{:S(2)}) %collective-permute-start.9) | collective-permute-done | bytes 1327136 | tf_op jit(solution)/shard_map/ppermute | solution.py:497
  313.0 26.3 %collective-permute-start.15 = (bf16[288,2304]{1,0:T(8,128)(2,1)}, bf16[288,2304]{1,0:T(8,128)(2,1)}, u32[]{:S(2)}, u32[]{:S(2)}) collective-permute-start(bf16[288,2304]{1,0:T(8,128)(2,1)} %pad_maximum_fusion.11), channel_id=1, source_target_pairs={{0,4},{2,6},{4,0},{6,2},{1,5},{3,7},{5,1},{7,3},{8,12},{10,14},{12... | collective-permute-start | bytes 3981320 | tf_op jit(solution)/shard_map/ppermute | solution.py:497
  339.3 7.1 fusion.67.pre_ref
  346.4 8.1 collective-permute-done.8
  359.3 12.0 %attend_forward.1 = (bf16[512,1024]{1,0:T(8,128)(2,1)S(1)}, f32[512,1024]{1,0:T(8,128)S(1)}, bf16[512,1024]{1,0:T(8,128)(2,1)S(1)}, f32[4,1,512]{2,1,0:T(1,128)S(1)}) custom-call(f32[512,1024]{1,0:T(8,128)} %fusion.67.pre_ref, bf16[2048,1024]{1,0:T(8,128)(2,1)} %pad_maximum_fusion.1.kv_ref, f32[512,128]{1,0:T(8,128)S(1)} %get-tuple-element.216.cos_ref, ...), custom_call_target="tpu_custom_call" | custom-call | flops 524288 | bytes 524288 | tf_op jit(solution)/shard_map/attend_forward/pallas_call | solution.py:96
  373.6 5.1 convolution_convert_fusion.6
  380.6 15.1 %collective-permute-done.15 = bf16[288,2304]{1,0:T(8,128)(2,1)} collective-permute-done((bf16[288,2304]{1,0:T(8,128)(2,1)}, bf16[288,2304]{1,0:T(8,128)(2,1)}, u32[]{:S(2)}, u32[]{:S(2)}) %collective-permute-start.15) | collective-permute-done | bytes 1327136 | tf_op jit(solution)/shard_map/ppermute | solution.py:497
  395.7 8.5 collective-permute-done.10
  407.9 4.6 multiply_reduce_fusion.10
  417.3 24.0 %collective-permute-done.11 = bf16[256,2304]{1,0:T(8,128)(2,1)S(1)} collective-permute-done((bf16[256,2304]{1,0:T(8,128)(2,1)S(1)}, bf16[256,2304]{1,0:T(8,128)(2,1)S(1)}, u32[]{:S(2)}, u32[]{:S(2)}) %collective-permute-start.11) | collective-permute-done | bytes 1179680 | tf_op jit(solution)/shard_map/ppermute | solution.py:438
  446.6 7.2 collective-permute-done.13
  455.4 29.2 %mix_forward.1 = (f32[1024,2304]{1,0:T(8,128)}, f32[1024,2304]{1,0:T(8,128)}, bf16[1024,2304]{1,0:T(8,128)(2,1)}) custom-call(bf16[1024,2304]{1,0:T(8,128)(2,1)} %constant_dynamic-update-slice_fusion.1.x_ref, bf16[2304,2304]{1,0:T(8,128)(2,1)} %all-gather.13.cloned.1.call-done.gate_mat_ref.refs_2_, ...), custom_call_target="tpu_custom_call" | custom-call | flops 1000000 | bytes 1000000 | tf_op jit(solution)/shard_map/mix_forward/pallas_call | solution.py:263
  484.7 21.6 %all-gather.17.cloned.1.call-done.refs_1_.down_mat_ref = bf16[2304,2304]{1,0:T(8,128)(2,1)} async-done(((bf16[576,2304]{1,0:T(8,128)(2,1)}), bf16[2304,2304]{1,0:T(8,128)(2,1)}) %all-gather.17.cloned.1.call-update) | async-done | bytes 10616848 | tf_op jit(solution)/shard_map/all_gather | solution.py:571
  506.3 16.3 %product_blocks.2 = (f32[256,2304]{1,0:T(8,128)}, bf16[256,2304]{1,0:T(8,128)(2,1)}, bf16[256,2304]{1,0:T(8,128)(2,1)}, bf16[256,2304]{1,0:T(8,128)(2,1)}) custom-call(bf16[1024,2304]{1,0:T(8,128)(2,1)} %get-tuple-element.82.refs_0_, bf16[2304,2304]{1,0:T(8,128)(2,1)} %all-gather.17.cloned.1.call-done.refs_1_.down_mat_ref), custom_call_target="tpu_custom_call" | custom-call | flops 1000000 | bytes 1000000 | tf_op jit(solution)/shard_map/product_blocks/pallas_call | solution.py:318
  527.2 12.4 %collective-permute-done.16 = bf16[128,2304]{1,0:T(8,128)(2,1)S(1)} collective-permute-done((bf16[128,2304]{1,0:T(8,128)(2,1)S(1)}, bf16[128,2304]{1,0:T(8,128)(2,1)S(1)}, u32[]{:S(2)}, u32[]{:S(2)}) %collective-permute-start.16) | collective-permute-done | bytes 589856 | tf_op jit(solution)/shard_map/ppermute | solution.py:438
  545.0 23.4 %collective-permute-done.17 = bf16[256,2304]{1,0:T(8,128)(2,1)} collective-permute-done((bf16[256,2304]{1,0:T(8,128)(2,1)}, bf16[256,2304]{1,0:T(8,128)(2,1)}, u32[]{:S(2)}, u32[]{:S(2)}) %collective-permute-start.17) | collective-permute-done | bytes 1179680 | tf_op jit(solution)/shard_map/ppermute | solution.py:438
  581.1 24.4 %collective-permute-done.21 = bf16[256,2304]{1,0:T(8,128)(2,1)} collective-permute-done((bf16[256,2304]{1,0:T(8,128)(2,1)}, bf16[256,2304]{1,0:T(8,128)(2,1)}, u32[]{:S(2)}, u32[]{:S(2)}) %collective-permute-start.21) | collective-permute-done | bytes 1179680 | tf_op jit(solution)/shard_map/ppermute | solution.py:438
  614.6 4.6 collective-permute-done.23
  621.5 14.9 %convolution_convert_fusion.2 = bf16[2304,2304]{1,0:T(8,128)(2,1)S(1)} fusion(bf16[1024,2304]{1,0:T(8,128)(2,1)} %constant_dynamic-update-slice_fusion.6.d_ref, bf16[1024,2304]{1,0:T(8,128)(2,1)} %get-tuple-element.82.refs_0_), kind=kOutput, calls=%fused_computation.2 | convolution fusion | flops 10876944384 | bytes 20054016 | tf_op jit(solution)/shard_map/dot_general | solution.py:330
  642.5 4.8 collective-permute-done.25
  647.3 4.7 add_convert_fusion.5
  652.4 23.3 %mix_backward.1 = (bf16[1024,2304]{1,0:T(8,128)(2,1)}, bf16[1024,2304]{1,0:T(8,128)(2,1)}) custom-call(bf16[1024,2304]{1,0:T(8,128)(2,1)} %constant_dynamic-update-slice_fusion.6.d_ref, bf16[2304,2304]{1,0:T(8,128)(2,1)} %all-gather.17.cloned.1.call-done.refs_1_.down_mat_ref, f32[1024,2304]{1,0:T(8,128)} %get-tuple-element.90.gate_ref, ...), custom_call_target="tpu_custom_call" | custom-call | flops 1000000 | bytes 1000000 | tf_op jit(solution)/shard_map/mix_backward/pallas_call | solution.py:288
  675.7 29.2 %product_blocks.3 = (f32[256,2304]{1,0:T(8,128)}, bf16[256,2304]{1,0:T(8,128)(2,1)}, bf16[256,2304]{1,0:T(8,128)(2,1)}, bf16[256,2304]{1,0:T(8,128)(2,1)}) custom-call(bf16[1024,2304]{1,0:T(8,128)(2,1)} %get-tuple-element.93.refs_0_, bf16[1024,2304]{1,0:T(8,128)(2,1)} %get-tuple-element.95.refs_1_, ...), custom_call_target="tpu_custom_call" | custom-call | flops 1000000 | bytes 1000000 | tf_op jit(solution)/shard_map/product_blocks/pallas_call | solution.py:318
  708.4 13.3 %convolution_convert_fusion.1 = bf16[2304,2304]{1,0:T(8,128)(2,1)S(1)} fusion(bf16[1024,2304]{1,0:T(8,128)(2,1)} %constant_dynamic-update-slice_fusion.1.x_ref, bf16[1024,2304]{1,0:T(8,128)(2,1)S(1)} %copy-done.53), kind=kOutput, calls=%fused_computation.1 | convolution fusion | flops 10876944384 | bytes 20054016 | tf_op jit(solution)/shard_map/dot_general | solution.py:330
  723.6 4.0 copy-done.30
  727.6 4.3 add_convert_fusion.4
  734.7 13.7 %convolution_convert_fusion = bf16[2304,2304]{1,0:T(8,128)(2,1)S(1)} fusion(bf16[1024,2304]{1,0:T(8,128)(2,1)} %constant_dynamic-update-slice_fusion.1.x_ref, bf16[1024,2304]{1,0:T(8,128)(2,1)S(1)} %bitcast.58), kind=kOutput, calls=%fused_computation | convolution fusion | flops 10876944384 | bytes 20054016 | tf_op jit(solution)/shard_map/dot_general | solution.py:330
  750.9 5.1 add_convert_fusion.3
  773.7 18.7 %collective-permute-done.32 = bf16[256,2304]{1,0:T(8,128)(2,1)S(1)} collective-permute-done((bf16[256,2304]{1,0:T(8,128)(2,1)S(1)}, bf16[256,2304]{1,0:T(8,128)(2,1)S(1)}, u32[]{:S(2)}, u32[]{:S(2)}) %collective-permute-start.32) | collective-permute-done | bytes 1179680 | tf_op jit(solution)/shard_map/ppermute | solution.py:707
  792.6 6.0 convolution_convert_fusion.7.da_ref
  804.5 20.8 %collective-permute-done.35 = bf16[576,2304]{1,0:T(8,128)(2,1)S(1)} collective-permute-done((bf16[576,2304]{1,0:T(8,128)(2,1)S(1)}, bf16[576,2304]{1,0:T(8,128)(2,1)S(1)}, u32[]{:S(2)}, u32[]{:S(2)}) %collective-permute-start.35) | collective-permute-done | bytes 2654240 | tf_op jit(solution)/shard_map/ppermute | solution.py:612
  838.3 28.8 %attend_backward.1 = (bf16[512,1024]{1,0:T(8,128)(2,1)S(1)}, bf16[2048,1024]{1,0:T(8,128)(2,1)}) custom-call(bf16[512,1024]{1,0:T(8,128)(2,1)S(1)} %get-tuple-element.105.q_ref, bf16[2048,1024]{1,0:T(8,128)(2,1)} %pad_maximum_fusion.1.kv_ref, bf16[512,1024]{1,0:T(8,128)(2,1)S(1)} %copy-done.1, f32[512,1024]{1,0:T(8,128)} %copy-done, ...), custom_call_target="tpu_custom_call" | custom-call | flops 524288 | bytes 524288 | tf_op jit(solution)/shard_map/attend_backward/pallas_call | solution.py:190
  868.1 21.8 %collective-permute-done.38 = bf16[288,2304]{1,0:T(8,128)(2,1)} collective-permute-done((bf16[288,2304]{1,0:T(8,128)(2,1)}, bf16[288,2304]{1,0:T(8,128)(2,1)}, u32[]{:S(2)}, u32[]{:S(2)}) %collective-permute-start.38) | collective-permute-done | bytes 1327136 | tf_op jit(solution)/shard_map/ppermute | solution.py:646
  907.5 39.4 %collective-permute-done.59 = bf16[144,2304]{1,0:T(8,128)(2,1)S(1)} collective-permute-done((bf16[144,2304]{1,0:T(8,128)(2,1)S(1)}, bf16[144,2304]{1,0:T(8,128)(2,1)S(1)}, u32[]{:S(2)}, u32[]{:S(2)}) %collective-permute-start.59) | collective-permute-done | bytes 663584 | tf_op jit(solution)/shard_map/ppermute | solution.py:665
  950.4 4.3 fusion.68
  954.7 4.4 add_convert_fusion
  966.3 9.5 collective-permute-done.41
  979.6 31.4 %collective-permute-done.56 = bf16[144,2304]{1,0:T(8,128)(2,1)S(1)} collective-permute-done((bf16[144,2304]{1,0:T(8,128)(2,1)S(1)}, bf16[144,2304]{1,0:T(8,128)(2,1)S(1)}, u32[]{:S(2)}, u32[]{:S(2)}) %collective-permute-start.56) | collective-permute-done | bytes 663584 | tf_op jit(solution)/shard_map/ppermute | solution.py:665
  1036.2 4.2 collective-permute-start.45
  1046.8 20.1 %collective-permute-done.45 = bf16[256,2304]{1,0:T(8,128)(2,1)S(1)} collective-permute-done((bf16[256,2304]{1,0:T(8,128)(2,1)}, bf16[256,2304]{1,0:T(8,128)(2,1)S(1)}, u32[]{:S(2)}, u32[]{:S(2)}) %collective-permute-start.45) | collective-permute-done | bytes 1179680 | tf_op jit(solution)/shard_map/ppermute | solution.py:774
  1082.0 14.2 %collective-permute-done.58 = bf16[144,2304]{1,0:T(8,128)(2,1)} collective-permute-done((bf16[144,2304]{1,0:T(8,128)(2,1)}, bf16[144,2304]{1,0:T(8,128)(2,1)}, u32[]{:S(2)}, u32[]{:S(2)}) %collective-permute-start.58) | collective-permute-done | bytes 663584 | tf_op jit(solution)/shard_map/ppermute | solution.py:665
  1101.8 6.5 collective-permute-done.46
  1117.1 12.9 %reduce-scatter.8.cloned.1.call-done = bf16[144,1024]{1,0:T(8,128)(2,1)} async-done(((bf16[576,1024]{1,0:T(8,128)(2,1)}), bf16[144,1024]{1,0:T(8,128)(2,1)}) %reduce-scatter.8.cloned.1.call-update) | async-done | bytes 294928 | tf_op jit(solution)/shard_map/reduce_scatter | solution.py:624
  (473 shorter events, 268.2 us)
Async XLA Ops:
  7.2 99.5 %all-gather.7.cloned.1.call-start = ((), (), s32[]{:S(2)}) async-start(), calls=%async_computation.3 | async-start | bytes 5640192 | tf_op jit(solution)/shard_map/all_gather | solution.py:480
  14.4 324.9 %all-gather.9.cloned.1.call-start = ((), (), s32[]{:S(2)}) async-start(), calls=%async_computation.4 | async-start | bytes 5013504 | tf_op jit(solution)/shard_map/all_gather | solution.py:481
  15.1 358.5 %all-gather.11.cloned.1.call-start = ((), (), s32[]{:S(2)}) async-start(), calls=%async_computation.5 | async-start | bytes 5013504 | tf_op jit(solution)/shard_map/all_gather | solution.py:482
  18.3 83.7 %collective-permute-start = (bf16[288,2304]{1,0:T(8,128)(2,1)}, bf16[288,2304]{1,0:T(8,128)(2,1)}, u32[]{:S(2)}, u32[]{:S(2)}) collective-permute-start(bf16[288,2304]{1,0:T(8,128)(2,1)} %pad_maximum_fusion.9), channel_id=1, source_target_pairs={{0,2},{2,0},{4,6},{6,4},{1,3},{3,1},{5,7},{7,5},{8,10},{10,8},{12,... | collective-permute-start | bytes 3981320 | tf_op jit(solution)/shard_map/ppermute | solution.py:503
  21.4 75.6 %collective-permute-start.2 = (bf16[144,2304]{1,0:T(8,128)(2,1)S(1)}, bf16[144,2304]{1,0:T(8,128)(2,1)}, u32[]{:S(2)}, u32[]{:S(2)}) collective-permute-start(bf16[144,2304]{1,0:T(8,128)(2,1)S(1)} %broadcast_select_fusion.17), channel_id=1, source_target_pairs={{0,2},{2,0},{4,6},{6,4},{1,3},{3,1},{5,7},{7,5},{8,10},{10,8},{12,... | collective-permute-start | bytes 1990664 | tf_op jit(solution)/shard_map/ppermute | solution.py:502
  21.5 434.0 %all-gather.13.cloned.1.call-start = ((), (), s32[]{:S(2)}) async-start(), calls=%async_computation.6 | async-start | bytes 13271040 | tf_op jit(solution)/shard_map/all_gather | solution.py:542
  100.2 88.4 %collective-permute-start.3 = (bf16[288,2304]{1,0:T(8,128)(2,1)}, bf16[288,2304]{1,0:T(8,128)(2,1)}, u32[]{:S(2)}, u32[]{:S(2)}) collective-permute-start(bf16[288,2304]{1,0:T(8,128)(2,1)} %pad_maximum_fusion.12), channel_id=1, source_target_pairs={{0,4},{2,6},{4,0},{6,2},{1,5},{3,7},{5,1},{7,3},{8,12},{10,14},{12... | collective-permute-start | bytes 3981320 | tf_op jit(solution)/shard_map/ppermute | solution.py:497
  192.1 263.3 %all-gather.15.cloned.1.call-start = ((), (), s32[]{:S(2)}) async-start(), calls=%async_computation.7 | async-start | bytes 13271040 | tf_op jit(solution)/shard_map/all_gather | solution.py:561
  193.3 37.8 %collective-permute-start.5 = (bf16[512,1024]{1,0:T(8,128)(2,1)S(1)}, bf16[512,1024]{1,0:T(8,128)(2,1)S(1)}, u32[]{:S(2)}, u32[]{:S(2)}) collective-permute-start(bf16[512,1024]{1,0:T(8,128)(2,1)S(1)} %copy-done.48), channel_id=1, source_target_pairs={{2,0},{4,2},{6,4},{3,1},{5,3},{7,5},{10,8},{12,10},{14,12},{11,9},... | collective-permute-start | bytes 3145736 | tf_op jit(solution)/shard_map/ppermute | solution.py:537
  194.6 42.0 %collective-permute-start.1 = (bf16[512,1024]{1,0:T(8,128)(2,1)S(1)}, bf16[512,1024]{1,0:T(8,128)(2,1)S(1)}, u32[]{:S(2)}, u32[]{:S(2)}) collective-permute-start(bf16[512,1024]{1,0:T(8,128)(2,1)S(1)} %copy-done.48), channel_id=1, source_target_pairs={{0,2},{2,4},{4,6},{1,3},{3,5},{5,7},{8,10},{10,12},{12,14},{9,11},... | collective-permute-start | bytes 3145736 | tf_op jit(solution)/shard_map/ppermute | solution.py:536
  199.2 106.3 %collective-permute-start.9 = (bf16[288,2304]{1,0:T(8,128)(2,1)}, bf16[288,2304]{1,0:T(8,128)(2,1)S(1)}, u32[]{:S(2)}, u32[]{:S(2)}) collective-permute-start(bf16[288,2304]{1,0:T(8,128)(2,1)} %pad_maximum_fusion.10), channel_id=1, source_target_pairs={{0,4},{2,6},{4,0},{6,2},{1,5},{3,7},{5,1},{7,3},{8,12},{10,14},{12... | collective-permute-start | bytes 3981320 | tf_op jit(solution)/shard_map/ppermute | solution.py:497
  231.1 74.4 %collective-permute-start.6 = (bf16[512,1024]{1,0:T(8,128)(2,1)S(1)}, bf16[512,1024]{1,0:T(8,128)(2,1)}, u32[]{:S(2)}, u32[]{:S(2)}) collective-permute-start(bf16[512,1024]{1,0:T(8,128)(2,1)S(1)} %collective-permute-done.5), channel_id=1, source_target_pairs={{2,0},{4,2},{3,1},{5,3},{10,8},{12,10},{11,9},{13,11},{18,16},{20,... | collective-permute-start | bytes 3145736 | tf_op jit(solution)/shard_map/ppermute | solution.py:537
  236.6 68.9 %collective-permute-start.4 = (bf16[512,1024]{1,0:T(8,128)(2,1)S(1)}, bf16[512,1024]{1,0:T(8,128)(2,1)}, u32[]{:S(2)}, u32[]{:S(2)}) collective-permute-start(bf16[512,1024]{1,0:T(8,128)(2,1)S(1)} %collective-permute-done.1), channel_id=1, source_target_pairs={{2,4},{4,6},{3,5},{5,7},{10,12},{12,14},{11,13},{13,15},{18,20},{2... | collective-permute-start | bytes 3145736 | tf_op jit(solution)/shard_map/ppermute | solution.py:536
  307.7 198.5 %all-gather.17.cloned.1.call-start = ((), (), s32[]{:S(2)}) async-start(), calls=%async_computation.8 | async-start | bytes 13271040 | tf_op jit(solution)/shard_map/all_gather | solution.py:571
  307.8 46.7 %collective-permute-start.8 = (bf16[512,1024]{1,0:T(8,128)(2,1)}, bf16[512,1024]{1,0:T(8,128)(2,1)}, u32[]{:S(2)}, u32[]{:S(2)}) collective-permute-start(bf16[512,1024]{1,0:T(8,128)(2,1)} %collective-permute-done.6), channel_id=1, source_target_pairs={{2,0},{3,1},{10,8},{11,9},{18,16},{19,17},{26,24},{27,25}} | collective-permute-start | bytes 3145736 | tf_op jit(solution)/shard_map/ppermute | solution.py:537
  309.1 45.4 %collective-permute-start.7 = (bf16[512,1024]{1,0:T(8,128)(2,1)}, bf16[512,1024]{1,0:T(8,128)(2,1)}, u32[]{:S(2)}, u32[]{:S(2)}) collective-permute-start(bf16[512,1024]{1,0:T(8,128)(2,1)} %collective-permute-done.4), channel_id=1, source_target_pairs={{4,6},{5,7},{12,14},{13,15},{20,22},{21,23},{28,30},{29,31}} | collective-permute-start | bytes 3145736 | tf_op jit(solution)/shard_map/ppermute | solution.py:536
  313.0 82.7 %collective-permute-start.15 = (bf16[288,2304]{1,0:T(8,128)(2,1)}, bf16[288,2304]{1,0:T(8,128)(2,1)}, u32[]{:S(2)}, u32[]{:S(2)}) collective-permute-start(bf16[288,2304]{1,0:T(8,128)(2,1)} %pad_maximum_fusion.11), channel_id=1, source_target_pairs={{0,4},{2,6},{4,0},{6,2},{1,5},{3,7},{5,1},{7,3},{8,12},{10,14},{12... | collective-permute-start | bytes 3981320 | tf_op jit(solution)/shard_map/ppermute | solution.py:497
  407.6 605.3 %reduce-scatter.4.cloned.1.call-start = ((), (), s32[]{:S(2)}) async-start(), calls=%async_computation.9 | async-start | bytes 5242880 | tf_op jit(solution)/shard_map/reduce_scatter | solution.py:735
  540.8 27.6 %collective-permute-start.17 = (bf16[256,2304]{1,0:T(8,128)(2,1)}, bf16[256,2304]{1,0:T(8,128)(2,1)}, u32[]{:S(2)}, u32[]{:S(2)}) collective-permute-start(bf16[256,2304]{1,0:T(8,128)(2,1)} %pad_maximum_fusion.13), channel_id=1, source_target_pairs={{0,2},{1,3},{2,0},{3,1},{4,6},{5,7},{6,4},{7,5},{8,10},{9,11},{10,... | collective-permute-start | bytes 3538952 | tf_op jit(solution)/shard_map/ppermute | solution.py:438
  543.6 27.4 %collective-permute-start.19 = (bf16[256,2304]{1,0:T(8,128)(2,1)}, bf16[256,2304]{1,0:T(8,128)(2,1)}, u32[]{:S(2)}, u32[]{:S(2)}) collective-permute-start(bf16[256,2304]{1,0:T(8,128)(2,1)} %pad_maximum_fusion.14), channel_id=1, source_target_pairs={{0,1},{1,0},{2,3},{3,2},{4,5},{5,4},{6,7},{7,6},{8,9},{9,8},{10,11... | collective-permute-start | bytes 3538952 | tf_op jit(solution)/shard_map/ppermute | solution.py:438
  642.0 85.5 %collective-permute-start.26 = (bf16[576,2304]{1,0:T(8,128)(2,1)}, bf16[576,2304]{1,0:T(8,128)(2,1)}, u32[]{:S(2)}, u32[]{:S(2)}) collective-permute-start(bf16[576,2304]{1,0:T(8,128)(2,1)} %get-tuple-element.163), channel_id=1, source_target_pairs={{0,8},{8,0},{16,24},{24,16},{1,9},{9,1},{17,25},{25,17},{2,10},{10... | collective-permute-start | bytes 7962632 | tf_op jit(solution)/shard_map/ppermute | solution.py:598
  652.0 75.6 %collective-permute-start.27 = (bf16[576,2304]{1,0:T(8,128)(2,1)}, bf16[576,2304]{1,0:T(8,128)(2,1)}, u32[]{:S(2)}, u32[]{:S(2)}) collective-permute-start(bf16[576,2304]{1,0:T(8,128)(2,1)} %add_convert_fusion.5), channel_id=1, source_target_pairs={{0,16},{8,24},{16,0},{24,8},{1,17},{9,25},{17,1},{25,9},{2,18},{10... | collective-permute-start | bytes 7962632 | tf_op jit(solution)/shard_map/ppermute | solution.py:612
  704.9 51.2 %collective-permute-start.29 = (bf16[256,2304]{1,0:T(8,128)(2,1)}, bf16[256,2304]{1,0:T(8,128)(2,1)}, u32[]{:S(2)}, u32[]{:S(2)}) collective-permute-start(bf16[256,2304]{1,0:T(8,128)(2,1)} %get-tuple-element.97), channel_id=1, source_target_pairs={{0,1},{1,0},{2,3},{3,2},{4,5},{5,4},{6,7},{7,6},{8,9},{9,8},{10,11... | collective-permute-start | bytes 3538952 | tf_op jit(solution)/shard_map/ppermute | solution.py:431
  706.5 49.6 %collective-permute-start.30 = (bf16[256,2304]{1,0:T(8,128)(2,1)}, bf16[256,2304]{1,0:T(8,128)(2,1)}, u32[]{:S(2)}, u32[]{:S(2)}) collective-permute-start(bf16[256,2304]{1,0:T(8,128)(2,1)} %get-tuple-element.98), channel_id=1, source_target_pairs={{0,2},{1,3},{2,0},{3,1},{4,6},{5,7},{6,4},{7,5},{8,10},{9,11},{10,... | collective-permute-start | bytes 3538952 | tf_op jit(solution)/shard_map/ppermute | solution.py:431
  708.1 51.2 %collective-permute-start.31 = (bf16[256,2304]{1,0:T(8,128)(2,1)}, bf16[256,2304]{1,0:T(8,128)(2,1)}, u32[]{:S(2)}, u32[]{:S(2)}) collective-permute-start(bf16[256,2304]{1,0:T(8,128)(2,1)} %get-tuple-element.99), channel_id=1, source_target_pairs={{0,3},{1,2},{2,1},{3,0},{4,7},{5,6},{6,5},{7,4},{8,11},{9,10},{10,... | collective-permute-start | bytes 3538952 | tf_op jit(solution)/shard_map/ppermute | solution.py:431
  767.6 57.8 %collective-permute-start.35 = (bf16[576,2304]{1,0:T(8,128)(2,1)S(1)}, bf16[576,2304]{1,0:T(8,128)(2,1)S(1)}, u32[]{:S(2)}, u32[]{:S(2)}) collective-permute-start(bf16[576,2304]{1,0:T(8,128)(2,1)S(1)} %add_convert_fusion.3), channel_id=1, source_target_pairs={{0,16},{8,24},{16,0},{24,8},{1,17},{9,25},{17,1},{25,9},{2,18},{10... | collective-permute-start | bytes 7962632 | tf_op jit(solution)/shard_map/ppermute | solution.py:612
  769.2 56.2 %collective-permute-start.34 = (bf16[576,2304]{1,0:T(8,128)(2,1)S(1)}, bf16[576,2304]{1,0:T(8,128)(2,1)}, u32[]{:S(2)}, u32[]{:S(2)}) collective-permute-start(bf16[576,2304]{1,0:T(8,128)(2,1)S(1)} %copy-done.54), channel_id=1, source_target_pairs={{0,8},{8,0},{16,24},{24,16},{1,9},{9,1},{17,25},{25,17},{2,10},{10... | collective-permute-start | bytes 7962632 | tf_op jit(solution)/shard_map/ppermute | solution.py:598
  769.2 66.5 %collective-permute-start.36 = (bf16[288,2304]{1,0:T(8,128)(2,1)}, bf16[288,2304]{1,0:T(8,128)(2,1)}, u32[]{:S(2)}, u32[]{:S(2)}) collective-permute-start(bf16[288,2304]{1,0:T(8,128)(2,1)} %broadcast_select_fusion.2), channel_id=1, source_target_pairs={{0,4},{2,6},{4,0},{6,2},{1,5},{3,7},{5,1},{7,3},{8,12},{10,14},{12... | collective-permute-start | bytes 3981320 | tf_op jit(solution)/shard_map/ppermute | solution.py:646
  831.7 58.2 %collective-permute-start.38 = (bf16[288,2304]{1,0:T(8,128)(2,1)}, bf16[288,2304]{1,0:T(8,128)(2,1)}, u32[]{:S(2)}, u32[]{:S(2)}) collective-permute-start(bf16[288,2304]{1,0:T(8,128)(2,1)} %broadcast_select_fusion.1), channel_id=1, source_target_pairs={{0,4},{2,6},{4,0},{6,2},{1,5},{3,7},{5,1},{7,3},{8,12},{10,14},{12... | collective-permute-start | bytes 3981320 | tf_op jit(solution)/shard_map/ppermute | solution.py:646
  834.3 55.7 %collective-permute-start.37 = (bf16[576,1024]{1,0:T(8,128)(2,1)}, bf16[576,1024]{1,0:T(8,128)(2,1)}, u32[]{:S(2)}, u32[]{:S(2)}) collective-permute-start(bf16[576,1024]{1,0:T(8,128)(2,1)} %get-tuple-element.171), channel_id=1, source_target_pairs={{0,8},{8,0},{16,24},{24,16},{1,9},{9,1},{17,25},{25,17},{2,10},{10... | collective-permute-start | bytes 3538952 | tf_op jit(solution)/shard_map/ppermute | solution.py:598
  834.9 67.1 %collective-permute-start.20 = (bf16[256,2304]{1,0:T(8,128)(2,1)}, bf16[256,2304]{1,0:T(8,128)(2,1)}, u32[]{:S(2)}, u32[]{:S(2)}) collective-permute-start(bf16[256,2304]{1,0:T(8,128)(2,1)} %get-tuple-element.194), channel_id=1, source_target_pairs={{0,1},{1,0},{2,3},{3,2},{4,5},{5,4},{6,7},{7,6},{8,9},{9,8},{10,11... | collective-permute-start | bytes 3538952 | tf_op jit(solution)/shard_map/ppermute | solution.py:415
  835.4 119.4 %collective-permute-start.42 = (bf16[576,2304]{1,0:T(8,128)(2,1)}, bf16[576,2304]{1,0:T(8,128)(2,1)}, u32[]{:S(2)}, u32[]{:S(2)}) collective-permute-start(bf16[576,2304]{1,0:T(8,128)(2,1)} %get-tuple-element.162), channel_id=1, source_target_pairs={{0,8},{8,0},{16,24},{24,16},{1,9},{9,1},{17,25},{25,17},{2,10},{10... | collective-permute-start | bytes 7962632 | tf_op jit(solution)/shard_map/ppermute | solution.py:598
  835.6 119.1 %collective-permute-start.43 = (bf16[576,2304]{1,0:T(8,128)(2,1)}, bf16[576,2304]{1,0:T(8,128)(2,1)}, u32[]{:S(2)}, u32[]{:S(2)}) collective-permute-start(bf16[576,2304]{1,0:T(8,128)(2,1)} %add_convert_fusion.2), channel_id=1, source_target_pairs={{0,16},{8,24},{16,0},{24,8},{1,17},{9,25},{17,1},{25,9},{2,18},{10... | collective-permute-start | bytes 7962632 | tf_op jit(solution)/shard_map/ppermute | solution.py:612
  890.0 224.8 %reduce-scatter.6.cloned.1.call-start = ((), (), s32[]{:S(2)}) async-start(), calls=%async_computation.10 | async-start | bytes 2949120 | tf_op jit(solution)/shard_map/reduce_scatter | solution.py:782
  901.4 45.4 %collective-permute-start.59 = (bf16[144,2304]{1,0:T(8,128)(2,1)S(1)}, bf16[144,2304]{1,0:T(8,128)(2,1)S(1)}, u32[]{:S(2)}, u32[]{:S(2)}) collective-permute-start(bf16[144,2304]{1,0:T(8,128)(2,1)S(1)} %select_convert_fusion.2), channel_id=1, source_target_pairs={{0,2},{2,0},{4,6},{6,4},{1,3},{3,1},{5,7},{7,5},{8,10},{10,8},{12,... | collective-permute-start | bytes 1990664 | tf_op jit(solution)/shard_map/ppermute | solution.py:665
  904.1 44.7 %collective-permute-start.39 = (bf16[576,1024]{1,0:T(8,128)(2,1)S(1)}, bf16[576,1024]{1,0:T(8,128)(2,1)S(1)}, u32[]{:S(2)}, u32[]{:S(2)}) collective-permute-start(bf16[576,1024]{1,0:T(8,128)(2,1)S(1)} %get-tuple-element.170), channel_id=1, source_target_pairs={{0,8},{8,0},{16,24},{24,16},{1,9},{9,1},{17,25},{25,17},{2,10},{10... | collective-permute-start | bytes 3538952 | tf_op jit(solution)/shard_map/ppermute | solution.py:598
  907.0 70.6 %collective-permute-start.40 = (bf16[576,1024]{1,0:T(8,128)(2,1)S(1)}, bf16[576,1024]{1,0:T(8,128)(2,1)S(1)}, u32[]{:S(2)}, u32[]{:S(2)}) collective-permute-start(bf16[576,1024]{1,0:T(8,128)(2,1)S(1)} %copy-done.59), channel_id=1, source_target_pairs={{0,8},{8,0},{16,24},{24,16},{1,9},{9,1},{17,25},{25,17},{2,10},{10... | collective-permute-start | bytes 3538952 | tf_op jit(solution)/shard_map/ppermute | solution.py:598
  946.8 28.9 %collective-permute-start.41 = (bf16[576,1024]{1,0:T(8,128)(2,1)S(1)}, bf16[576,1024]{1,0:T(8,128)(2,1)S(1)}, u32[]{:S(2)}, u32[]{:S(2)}) collective-permute-start(bf16[576,1024]{1,0:T(8,128)(2,1)S(1)} %add_convert_fusion.11), channel_id=1, source_target_pairs={{0,16},{8,24},{16,0},{24,8},{1,17},{9,25},{17,1},{25,9},{2,18},{10... | collective-permute-start | bytes 3538952 | tf_op jit(solution)/shard_map/ppermute | solution.py:612
  948.8 82.9 %collective-permute-start.54 = (bf16[576,1024]{1,0:T(8,128)(2,1)}, bf16[576,1024]{1,0:T(8,128)(2,1)}, u32[]{:S(2)}, u32[]{:S(2)}) collective-permute-start(bf16[576,1024]{1,0:T(8,128)(2,1)} %get-tuple-element.169), channel_id=1, source_target_pairs={{0,8},{8,0},{16,24},{24,16},{1,9},{9,1},{17,25},{25,17},{2,10},{10... | collective-permute-start | bytes 3538952 | tf_op jit(solution)/shard_map/ppermute | solution.py:598
  964.2 46.7 %collective-permute-start.56 = (bf16[144,2304]{1,0:T(8,128)(2,1)S(1)}, bf16[144,2304]{1,0:T(8,128)(2,1)S(1)}, u32[]{:S(2)}, u32[]{:S(2)}) collective-permute-start(bf16[144,2304]{1,0:T(8,128)(2,1)S(1)} %select_convert_fusion.1), channel_id=1, source_target_pairs={{0,2},{2,0},{4,6},{6,4},{1,3},{3,1},{5,7},{7,5},{8,10},{10,8},{12,... | collective-permute-start | bytes 1990664 | tf_op jit(solution)/shard_map/ppermute | solution.py:665
  966.1 65.7 %collective-permute-start.55 = (bf16[576,1024]{1,0:T(8,128)(2,1)}, bf16[576,1024]{1,0:T(8,128)(2,1)}, u32[]{:S(2)}, u32[]{:S(2)}) collective-permute-start(bf16[576,1024]{1,0:T(8,128)(2,1)} %add_convert_fusion.10), channel_id=1, source_target_pairs={{0,16},{8,24},{16,0},{24,8},{1,17},{9,25},{17,1},{25,9},{2,18},{10... | collective-permute-start | bytes 3538952 | tf_op jit(solution)/shard_map/ppermute | solution.py:612
  975.7 68.1 %collective-permute-start.57 = (bf16[288,2304]{1,0:T(8,128)(2,1)}, bf16[288,2304]{1,0:T(8,128)(2,1)}, u32[]{:S(2)}, u32[]{:S(2)}) collective-permute-start(bf16[288,2304]{1,0:T(8,128)(2,1)} %broadcast_select_fusion), channel_id=1, source_target_pairs={{0,4},{2,6},{4,0},{6,2},{1,5},{3,7},{5,1},{7,3},{8,12},{10,14},{12... | collective-permute-start | bytes 3981320 | tf_op jit(solution)/shard_map/ppermute | solution.py:646
  1025.4 42.9 %collective-permute-start.47 = (bf16[576,1024]{1,0:T(8,128)(2,1)}, bf16[576,1024]{1,0:T(8,128)(2,1)}, u32[]{:S(2)}, u32[]{:S(2)}) collective-permute-start(bf16[576,1024]{1,0:T(8,128)(2,1)} %get-tuple-element.168), channel_id=1, source_target_pairs={{0,8},{8,0},{16,24},{24,16},{1,9},{9,1},{17,25},{25,17},{2,10},{10... | collective-permute-start | bytes 3538952 | tf_op jit(solution)/shard_map/ppermute | solution.py:598
  1036.1 93.9 %reduce-scatter.8.cloned.1.call-start = ((), (), s32[]{:S(2)}) async-start(), calls=%async_computation.11 | async-start | bytes 1474560 | tf_op jit(solution)/shard_map/reduce_scatter | solution.py:624
  1036.2 30.7 %collective-permute-start.45 = (bf16[256,2304]{1,0:T(8,128)(2,1)}, bf16[256,2304]{1,0:T(8,128)(2,1)S(1)}, u32[]{:S(2)}, u32[]{:S(2)}) collective-permute-start(bf16[256,2304]{1,0:T(8,128)(2,1)} %slice.502), channel_id=1, source_target_pairs={{0,1},{1,0},{2,3},{3,2},{4,5},{5,4},{6,7},{7,6},{8,9},{9,8},{10,11... | collective-permute-start | bytes 3538952 | tf_op jit(solution)/shard_map/ppermute | solution.py:774
  1042.4 27.9 %collective-permute-start.48 = (bf16[576,1024]{1,0:T(8,128)(2,1)S(1)}, bf16[576,1024]{1,0:T(8,128)(2,1)S(1)}, u32[]{:S(2)}, u32[]{:S(2)}) collective-permute-start(bf16[576,1024]{1,0:T(8,128)(2,1)S(1)} %add_convert_fusion.8), channel_id=1, source_target_pairs={{0,16},{8,24},{16,0},{24,8},{1,17},{9,25},{17,1},{25,9},{2,18},{10... | collective-permute-start | bytes 3538952 | tf_op jit(solution)/shard_map/ppermute | solution.py:612
  1046.8 49.3 %collective-permute-start.58 = (bf16[144,2304]{1,0:T(8,128)(2,1)}, bf16[144,2304]{1,0:T(8,128)(2,1)}, u32[]{:S(2)}, u32[]{:S(2)}) collective-permute-start(bf16[144,2304]{1,0:T(8,128)(2,1)} %select_convert_fusion), channel_id=1, source_target_pairs={{0,2},{2,0},{4,6},{6,4},{1,3},{3,1},{5,7},{7,5},{8,10},{10,8},{12,... | collective-permute-start | bytes 1990664 | tf_op jit(solution)/shard_map/ppermute | solution.py:665
  1080.1 28.2 %collective-permute-start.46 = (bf16[256,2304]{1,0:T(8,128)(2,1)}, bf16[256,2304]{1,0:T(8,128)(2,1)}, u32[]{:S(2)}, u32[]{:S(2)}) collective-permute-start(bf16[256,2304]{1,0:T(8,128)(2,1)} %fusion.9), channel_id=1, source_target_pairs={{0,1},{1,0},{2,3},{3,2},{4,5},{5,4},{6,7},{7,6},{8,9},{9,8},{10,11... | collective-permute-start | bytes 3538952 | tf_op jit(solution)/shard_map/ppermute | solution.py:415
  (119 other events, 2468.4 us)
Sparse Core Ops, SparseCore 0:
  14.5 81.7 all-gather.6
  98.6 86.4 all-gather.8
  187.3 100.7 all-gather.10
  290.1 70.1 all-gather.12
  362.3 70.9 all-gather.14
  435.3 70.9 all-gather.16
  890.0 114.4 reduce-scatter.3
  1036.2 61.8 reduce-scatter.5
  1100.5 29.3 reduce-scatter.7

commit v6 on v5

--- a/solution.py
+++ b/solution.py
@@ -478,8 +478,10 @@
         ]
     keyvalue_pack = jnp.concatenate([*heads_in_turn, gain_pack], axis=1)
     keyvalue_all = lax.all_gather(keyvalue_pack, both, axis=0, tiled=True)
-    query_mat = lax.all_gather(query_weight, both, axis=0, tiled=True)
-    out_mat = lax.all_gather(output_weight.T, both, axis=0, tiled=True)
+    query_pack = jnp.concatenate([query_weight, output_weight.T], axis=1)
+    query_all = lax.all_gather(query_pack, both, axis=0, tiled=True)
+    query_mat = query_all[:, : query_weight.shape[1]]
+    out_mat = query_all[:, query_weight.shape[1] :]
 
     hidden = gate_weight.shape[1] // pair
     is_high = near_index == 1
@@ -731,7 +733,7 @@
         per_group,
         ctx_count,
     )
-    d_kv = after(d_kv, *gate_sum.arrived)
+    d_kv = after(d_kv, *gate_sum.arrived, *up_sum.arrived)
     d_kv_local = lax.psum_scatter(d_kv, "ctx", scatter_dimension=0, tiled=True).astype(f32)
     out_sum.y_pack(d_kv)
     out_sum.y_send()
@@ -742,13 +744,12 @@
     down_sum.near_pack(*query_sum.packed)
     near_send(down_sum)
     last = [down_sum.other]
-    query_sum.y_pack(*last)
+    up_sum.far_pack(*last)
+    up_sum.far_send()
+    query_sum.y_pack(*up_sum.packed)
     query_sum.y_send()
     query_part = contract(after(d_query_pre, *query_sum.packed), query_mat, 1, 1)
     last = [query_part]
-    up_sum.far_pack(query_part)
-    up_sum.far_send()
-    last = up_sum.packed
     gate_sum.near_pack(*last)
     near_send(gate_sum)
     last = [gate_sum.other]

time: 1150 us -> 1120 us (0.974)
  starting transfers between devices: 87.3 us -> 70.4 us
    reduce_scatter x1, waiting for transfers between devices: 0.01 us -> 40.4 us  [body(): lax.psum_scatter(d_kv, 'ctx', scatter_dimension=0, tiled=True).astype(f32)]
    ppermute x3, waiting for transfers between devices: 84.9 us -> 52.3 us  [near_send(): got = lax.ppermute(sent, 'ctx', near_swap).astype(f32)]
    ppermute x3, waiting for transfers between devices: 39.6 us -> 63.2 us  [line_step(): from_right.append(lax.ppermute(right_block, 'ctx', left_pairs))]
    ppermute x3, starting transfers between devices: 28.5 us -> 6.62 us  [far_start(): lax.ppermute(block, 'ctx', far_shift(s))]
    all_gather x1, waiting for transfers between devices: 21.6 us -> 0.01 us  [body(): down_mat = lax.all_gather(down_rows, dp_axes, axis=0, tiled=True)]
    reduce_scatter x1, waiting for transfers between devices: 12.9 us -> 0.01 us  [finish_ctx(): lax.psum_scatter(self.total, 'ctx', scatter_dimension=0, tiled=True)]
    unnamed x210 -> x192, local copies, waits for them, and re-layouts: 44.3 us -> 40.4 us
  transfers between devices with their start and end apart: 69 -> 68, of which waited for: 33 -> 34; matrix products, arithmetic and copies ran while one was open for 20% -> 20% of each run, Pallas kernels for 11% -> 11%
where the time goes in v6:
time: 1120 us; the launch traced here: 1110 us
  waiting for transfers between devices  599 us (53%)
  other arithmetic  139 us (12%)
  Pallas kernels  139 us (12%)
  matrix products  81.9 us (7%)
  starting transfers between devices  70.4 us (6%)
  local copies, waits for them, and re-layouts  68.7 us (6%)
  between operations  16.2 us (1%)
    ppermute x3, waiting for transfers between devices, far_start(): lax.ppermute(block, 'ctx', far_shift(s))  148 us
    ppermute x12, waiting for transfers between devices, hop(): return lax.ppermute(values, ('ctx', 'tensor'), all_swaps[bz, bx])  95.7 us
    dot_general x10, matrix products, contract(): lax.dot_general(left, right, (((left_dim,), (right_dim,)), ((), ())), pre...  67.2 us
    ppermute x1, waiting for transfers between devices, body(): gate_got = lax.ppermute(gate_other, 'ctx', near_swap)  65.1 us
    ppermute x3, waiting for transfers between devices, line_step(): from_right.append(lax.ppermute(right_block, 'ctx', left_pairs))  63.2 us
    ppermute x3, waiting for transfers between devices, near_send(): got = lax.ppermute(sent, 'ctx', near_swap).astype(f32)  52.3 us
    pallas_call x2, Pallas kernels, product_blocks(): pl.pallas_call(functools.partial(spread_kernel, len(lefts), half), grid=(...  45.6 us
    unnamed x192, local copies, waits for them, and re-layouts  40.4 us
  transfers between devices with their start and end apart: 68, of which 34 were waited for; matrix products, arithmetic and copies ran while one was open for 20% of the time, Pallas kernels for 11%

profile of v6, /device:TPU:0, one launch (start us, length us, event | category | flops | bytes accessed | tf_op | source)
XLA Modules:
  0.0 1114.1 jit_solution(10624787184175136009)
XLA Ops:
  31.5 65.1 %collective-permute-done.2 = bf16[144,2304]{1,0:T(8,128)(2,1)} collective-permute-done((bf16[144,2304]{1,0:T(8,128)(2,1)S(1)}, bf16[144,2304]{1,0:T(8,128)(2,1)}, u32[]{:S(2)}, u32[]{:S(2)}) %collective-permute-start.2) | collective-permute-done | bytes 663584 | tf_op jit(solution)/shard_map/ppermute | solution.py:504
  120.8 85.2 %collective-permute-done.3 = bf16[288,2304]{1,0:T(8,128)(2,1)} collective-permute-done((bf16[288,2304]{1,0:T(8,128)(2,1)}, bf16[288,2304]{1,0:T(8,128)(2,1)}, u32[]{:S(2)}, u32[]{:S(2)}) %collective-permute-start.3) | collective-permute-done | bytes 1327136 | tf_op jit(solution)/shard_map/ppermute | solution.py:499
  212.1 4.6 collective-permute-start.1
  217.2 22.2 %collective-permute-done.5 = bf16[512,1024]{1,0:T(8,128)(2,1)S(1)} collective-permute-done((bf16[512,1024]{1,0:T(8,128)(2,1)S(1)}, bf16[512,1024]{1,0:T(8,128)(2,1)S(1)}, u32[]{:S(2)}, u32[]{:S(2)}) %collective-permute-start.5) | collective-permute-done | bytes 1048608 | tf_op jit(solution)/shard_map/ppermute | solution.py:539
  242.4 54.5 %collective-permute-done.9 = bf16[288,2304]{1,0:T(8,128)(2,1)S(1)} collective-permute-done((bf16[288,2304]{1,0:T(8,128)(2,1)}, bf16[288,2304]{1,0:T(8,128)(2,1)S(1)}, u32[]{:S(2)}, u32[]{:S(2)}) %collective-permute-start.9) | collective-permute-done | bytes 1327136 | tf_op jit(solution)/shard_map/ppermute | solution.py:499
  296.9 22.1 %collective-permute-done.6 = bf16[512,1024]{1,0:T(8,128)(2,1)} collective-permute-done((bf16[512,1024]{1,0:T(8,128)(2,1)S(1)}, bf16[512,1024]{1,0:T(8,128)(2,1)}, u32[]{:S(2)}, u32[]{:S(2)}) %collective-permute-start.6) | collective-permute-done | bytes 1048608 | tf_op jit(solution)/shard_map/ppermute | solution.py:539
  326.8 4.4 collective-permute-start.15
  331.2 18.8 %collective-permute-done.8 = bf16[512,1024]{1,0:T(8,128)(2,1)} collective-permute-done((bf16[512,1024]{1,0:T(8,128)(2,1)}, bf16[512,1024]{1,0:T(8,128)(2,1)}, u32[]{:S(2)}, u32[]{:S(2)}) %collective-permute-start.8) | collective-permute-done | bytes 1048608 | tf_op jit(solution)/shard_map/ppermute | solution.py:539
  355.1 7.1 fusion.2.pre_ref
  362.2 12.2 %attend_forward.1 = (bf16[512,1024]{1,0:T(8,128)(2,1)S(1)}, f32[512,1024]{1,0:T(8,128)S(1)}, bf16[512,1024]{1,0:T(8,128)(2,1)S(1)}, f32[4,1,512]{2,1,0:T(1,128)S(1)}) custom-call(f32[512,1024]{1,0:T(8,128)} %fusion.2.pre_ref, bf16[2048,1024]{1,0:T(8,128)(2,1)} %pad_maximum_fusion.1.kv_ref, f32[512,128]{1,0:T(8,128)S(1)} %get-tuple-element.216.cos_ref, ...), custom_call_target="tpu_custom_call" | custom-call | flops 524288 | bytes 524288 | tf_op jit(solution)/shard_map/attend_forward/pallas_call | solution.py:96
  374.4 5.0 convolution_convert_fusion.6
  380.4 8.6 collective-permute-done.15
  389.0 17.4 %collective-permute-done.10 = bf16[256,2304]{1,0:T(8,128)(2,1)} collective-permute-done((bf16[256,2304]{1,0:T(8,128)(2,1)S(1)}, bf16[256,2304]{1,0:T(8,128)(2,1)}, u32[]{:S(2)}, u32[]{:S(2)}) %collective-permute-start.10) | collective-permute-done | bytes 1179680 | tf_op jit(solution)/shard_map/ppermute | solution.py:570
  410.2 4.6 multiply_reduce_fusion.10
  419.1 24.8 %collective-permute-done.11 = bf16[256,2304]{1,0:T(8,128)(2,1)S(1)} collective-permute-done((bf16[256,2304]{1,0:T(8,128)(2,1)S(1)}, bf16[256,2304]{1,0:T(8,128)(2,1)S(1)}, u32[]{:S(2)}, u32[]{:S(2)}) %collective-permute-start.11) | collective-permute-done | bytes 1179680 | tf_op jit(solution)/shard_map/ppermute | solution.py:438
  448.3 9.2 collective-permute-done.13
  459.3 29.3 %mix_forward.1 = (f32[1024,2304]{1,0:T(8,128)}, f32[1024,2304]{1,0:T(8,128)}, bf16[1024,2304]{1,0:T(8,128)(2,1)}) custom-call(bf16[1024,2304]{1,0:T(8,128)(2,1)} %constant_dynamic-update-slice_fusion.1.x_ref, bf16[2304,2304]{1,0:T(8,128)(2,1)} %all-gather.10.cloned.1.call-done.gate_mat_ref.refs_2_, ...), custom_call_target="tpu_custom_call" | custom-call | flops 1000000 | bytes 1000000 | tf_op jit(solution)/shard_map/mix_forward/pallas_call | solution.py:263
  488.5 16.4 %product_blocks.2 = (f32[256,2304]{1,0:T(8,128)}, bf16[256,2304]{1,0:T(8,128)(2,1)}, bf16[256,2304]{1,0:T(8,128)(2,1)}, bf16[256,2304]{1,0:T(8,128)(2,1)}) custom-call(bf16[1024,2304]{1,0:T(8,128)(2,1)} %get-tuple-element.82.refs_0_, bf16[2304,2304]{1,0:T(8,128)(2,1)} %all-gather.14.cloned.1.call-done.refs_1_.down_mat_ref), custom_call_target="tpu_custom_call" | custom-call | flops 1000000 | bytes 1000000 | tf_op jit(solution)/shard_map/product_blocks/pallas_call | solution.py:318
  507.8 11.2 %collective-permute-done.16 = bf16[128,2304]{1,0:T(8,128)(2,1)S(1)} collective-permute-done((bf16[128,2304]{1,0:T(8,128)(2,1)S(1)}, bf16[128,2304]{1,0:T(8,128)(2,1)S(1)}, u32[]{:S(2)}, u32[]{:S(2)}) %collective-permute-start.16) | collective-permute-done | bytes 589856 | tf_op jit(solution)/shard_map/ppermute | solution.py:438
  523.5 21.3 %collective-permute-done.17 = bf16[256,2304]{1,0:T(8,128)(2,1)} collective-permute-done((bf16[256,2304]{1,0:T(8,128)(2,1)}, bf16[256,2304]{1,0:T(8,128)(2,1)}, u32[]{:S(2)}, u32[]{:S(2)}) %collective-permute-start.17) | collective-permute-done | bytes 1179680 | tf_op jit(solution)/shard_map/ppermute | solution.py:438
  556.3 22.5 %collective-permute-done.21 = bf16[256,2304]{1,0:T(8,128)(2,1)} collective-permute-done((bf16[256,2304]{1,0:T(8,128)(2,1)}, bf16[256,2304]{1,0:T(8,128)(2,1)}, u32[]{:S(2)}, u32[]{:S(2)}) %collective-permute-start.21) | collective-permute-done | bytes 1179680 | tf_op jit(solution)/shard_map/ppermute | solution.py:438
  593.2 14.7 %convolution_convert_fusion.2 = bf16[2304,2304]{1,0:T(8,128)(2,1)S(1)} fusion(bf16[1024,2304]{1,0:T(8,128)(2,1)} %constant_dynamic-update-slice_fusion.6.d_ref, bf16[1024,2304]{1,0:T(8,128)(2,1)} %get-tuple-element.82.refs_0_), kind=kOutput, calls=%fused_computation.2 | convolution fusion | flops 10876944384 | bytes 20054016 | tf_op jit(solution)/shard_map/dot_general | solution.py:330
  614.1 4.8 collective-permute-done.25
  618.8 4.7 add_convert_fusion.5
  625.6 23.3 %mix_backward.1 = (bf16[1024,2304]{1,0:T(8,128)(2,1)}, bf16[1024,2304]{1,0:T(8,128)(2,1)}) custom-call(bf16[1024,2304]{1,0:T(8,128)(2,1)} %constant_dynamic-update-slice_fusion.6.d_ref, bf16[2304,2304]{1,0:T(8,128)(2,1)} %all-gather.14.cloned.1.call-done.refs_1_.down_mat_ref, f32[1024,2304]{1,0:T(8,128)} %get-tuple-element.90.gate_ref, ...), custom_call_target="tpu_custom_call" | custom-call | flops 1000000 | bytes 1000000 | tf_op jit(solution)/shard_map/mix_backward/pallas_call | solution.py:288
  648.9 29.3 %product_blocks.3 = (f32[256,2304]{1,0:T(8,128)}, bf16[256,2304]{1,0:T(8,128)(2,1)}, bf16[256,2304]{1,0:T(8,128)(2,1)}, bf16[256,2304]{1,0:T(8,128)(2,1)}) custom-call(bf16[1024,2304]{1,0:T(8,128)(2,1)} %get-tuple-element.93.refs_0_, bf16[1024,2304]{1,0:T(8,128)(2,1)} %get-tuple-element.95.refs_1_, ...), custom_call_target="tpu_custom_call" | custom-call | flops 1000000 | bytes 1000000 | tf_op jit(solution)/shard_map/product_blocks/pallas_call | solution.py:318
  681.6 13.7 %convolution_convert_fusion.1 = bf16[2304,2304]{1,0:T(8,128)(2,1)S(1)} fusion(bf16[1024,2304]{1,0:T(8,128)(2,1)} %constant_dynamic-update-slice_fusion.1.x_ref, bf16[1024,2304]{1,0:T(8,128)(2,1)S(1)} %copy-done.53), kind=kOutput, calls=%fused_computation.1 | convolution fusion | flops 10876944384 | bytes 20054016 | tf_op jit(solution)/shard_map/dot_general | solution.py:330
  701.2 4.3 add_convert_fusion.4
  708.2 13.3 %convolution_convert_fusion = bf16[2304,2304]{1,0:T(8,128)(2,1)S(1)} fusion(bf16[1024,2304]{1,0:T(8,128)(2,1)} %constant_dynamic-update-slice_fusion.1.x_ref, bf16[1024,2304]{1,0:T(8,128)(2,1)S(1)} %bitcast.55), kind=kOutput, calls=%fused_computation | convolution fusion | flops 10876944384 | bytes 20054016 | tf_op jit(solution)/shard_map/dot_general | solution.py:330
  724.9 6.6 add_convert_fusion.3
  740.8 5.6 collective-permute-start.36
  751.4 14.9 %collective-permute-done.32 = bf16[256,2304]{1,0:T(8,128)(2,1)S(1)} collective-permute-done((bf16[256,2304]{1,0:T(8,128)(2,1)S(1)}, bf16[256,2304]{1,0:T(8,128)(2,1)S(1)}, u32[]{:S(2)}, u32[]{:S(2)}) %collective-permute-start.32) | collective-permute-done | bytes 1179680 | tf_op jit(solution)/shard_map/ppermute | solution.py:709
  766.5 5.0 fusion.20.da_ref
  777.5 23.8 %collective-permute-done.35 = bf16[576,2304]{1,0:T(8,128)(2,1)S(1)} collective-permute-done((bf16[576,2304]{1,0:T(8,128)(2,1)S(1)}, bf16[576,2304]{1,0:T(8,128)(2,1)S(1)}, u32[]{:S(2)}, u32[]{:S(2)}) %collective-permute-start.35) | collective-permute-done | bytes 2654240 | tf_op jit(solution)/shard_map/ppermute | solution.py:614
  807.2 4.8 collective-permute-start.38
  813.1 29.0 %attend_backward.1 = (bf16[512,1024]{1,0:T(8,128)(2,1)S(1)}, bf16[2048,1024]{1,0:T(8,128)(2,1)}) custom-call(bf16[512,1024]{1,0:T(8,128)(2,1)S(1)} %get-tuple-element.105.q_ref, bf16[2048,1024]{1,0:T(8,128)(2,1)} %pad_maximum_fusion.1.kv_ref, bf16[512,1024]{1,0:T(8,128)(2,1)S(1)} %fusion.20.da_ref, f32[512,1024]{1,0:T(8,128)} %copy-done, ...), custom_call_target="tpu_custom_call" | custom-call | flops 524288 | bytes 524288 | tf_op jit(solution)/shard_map/attend_backward/pallas_call | solution.py:190
  843.1 23.3 %collective-permute-done.38 = bf16[288,2304]{1,0:T(8,128)(2,1)} collective-permute-done((bf16[288,2304]{1,0:T(8,128)(2,1)S(1)}, bf16[288,2304]{1,0:T(8,128)(2,1)}, u32[]{:S(2)}, u32[]{:S(2)}) %collective-permute-start.38) | collective-permute-done | bytes 1327136 | tf_op jit(solution)/shard_map/ppermute | solution.py:648
  882.0 4.6 add_convert_fusion
  889.5 4.4 fusion
  903.0 40.4 %reduce-scatter.4.cloned.1.call-done = bf16[512,1024]{1,0:T(8,128)(2,1)} async-done(((bf16[2048,1024]{1,0:T(8,128)(2,1)}), bf16[512,1024]{1,0:T(8,128)(2,1)}) %reduce-scatter.4.cloned.1.call-update) | async-done | bytes 1048592 | tf_op jit(solution)/shard_map/reduce_scatter | solution.py:737
  967.2 11.3 %collective-permute-done.59 = bf16[144,2304]{1,0:T(8,128)(2,1)S(1)} collective-permute-done((bf16[144,2304]{1,0:T(8,128)(2,1)S(1)}, bf16[144,2304]{1,0:T(8,128)(2,1)S(1)}, u32[]{:S(2)}, u32[]{:S(2)}) %collective-permute-start.59) | collective-permute-done | bytes 663584 | tf_op jit(solution)/shard_map/ppermute | solution.py:667
  980.3 10.1 collective-permute-done.48
  997.3 33.0 %collective-permute-done.56 = bf16[144,2304]{1,0:T(8,128)(2,1)S(1)} collective-permute-done((bf16[144,2304]{1,0:T(8,128)(2,1)}, bf16[144,2304]{1,0:T(8,128)(2,1)S(1)}, u32[]{:S(2)}, u32[]{:S(2)}) %collective-permute-start.56) | collective-permute-done | bytes 663584 | tf_op jit(solution)/shard_map/ppermute | solution.py:667
  1039.1 6.0 collective-permute-done.57
  1047.2 13.7 %collective-permute-done.45 = bf16[256,2304]{1,0:T(8,128)(2,1)} collective-permute-done((bf16[256,2304]{1,0:T(8,128)(2,1)}, bf16[256,2304]{1,0:T(8,128)(2,1)}, u32[]{:S(2)}, u32[]{:S(2)}) %collective-permute-start.45) | collective-permute-done | bytes 1179680 | tf_op jit(solution)/shard_map/ppermute | solution.py:775
  1071.5 8.0 collective-permute-done.58
  1081.6 5.1 collective-permute-done.51
  1088.2 8.8 collective-permute-done.46
  (454 shorter events, 265.1 us)
Async XLA Ops:
  7.2 99.1 %all-gather.6.cloned.1.call-start = ((), (), s32[]{:S(2)}) async-start(), calls=%async_computation.3 | async-start | bytes 5640192 | tf_op jit(solution)/shard_map/all_gather | solution.py:480
  14.5 340.5 %all-gather.8.cloned.1.call-start = ((), (), s32[]{:S(2)}) async-start(), calls=%async_computation.4 | async-start | bytes 10027008 | tf_op jit(solution)/shard_map/all_gather | solution.py:482
  16.5 442.7 %all-gather.10.cloned.1.call-start = ((), (), s32[]{:S(2)}) async-start(), calls=%async_computation.5 | async-start | bytes 13271040 | tf_op jit(solution)/shard_map/all_gather | solution.py:544
  17.9 83.7 %collective-permute-start = (bf16[288,2304]{1,0:T(8,128)(2,1)}, bf16[288,2304]{1,0:T(8,128)(2,1)}, u32[]{:S(2)}, u32[]{:S(2)}) collective-permute-start(bf16[288,2304]{1,0:T(8,128)(2,1)} %pad_maximum_fusion.9), channel_id=1, source_target_pairs={{0,2},{2,0},{4,6},{6,4},{1,3},{3,1},{5,7},{7,5},{8,10},{10,8},{12,... | collective-permute-start | bytes 3981320 | tf_op jit(solution)/shard_map/ppermute | solution.py:505
  21.0 75.6 %collective-permute-start.2 = (bf16[144,2304]{1,0:T(8,128)(2,1)S(1)}, bf16[144,2304]{1,0:T(8,128)(2,1)}, u32[]{:S(2)}, u32[]{:S(2)}) collective-permute-start(bf16[144,2304]{1,0:T(8,128)(2,1)S(1)} %broadcast_select_fusion.17), channel_id=1, source_target_pairs={{0,2},{2,0},{4,6},{6,4},{1,3},{3,1},{5,7},{7,5},{8,10},{10,8},{12,... | collective-permute-start | bytes 1990664 | tf_op jit(solution)/shard_map/ppermute | solution.py:504
  99.8 106.2 %collective-permute-start.3 = (bf16[288,2304]{1,0:T(8,128)(2,1)}, bf16[288,2304]{1,0:T(8,128)(2,1)}, u32[]{:S(2)}, u32[]{:S(2)}) collective-permute-start(bf16[288,2304]{1,0:T(8,128)(2,1)} %pad_maximum_fusion.12), channel_id=1, source_target_pairs={{0,4},{2,6},{4,0},{6,2},{1,5},{3,7},{5,1},{7,3},{8,12},{10,14},{12... | collective-permute-start | bytes 3981320 | tf_op jit(solution)/shard_map/ppermute | solution.py:499
  209.6 249.7 %all-gather.12.cloned.1.call-start = ((), (), s32[]{:S(2)}) async-start(), calls=%async_computation.6 | async-start | bytes 13271040 | tf_op jit(solution)/shard_map/all_gather | solution.py:563
  210.8 28.6 %collective-permute-start.5 = (bf16[512,1024]{1,0:T(8,128)(2,1)S(1)}, bf16[512,1024]{1,0:T(8,128)(2,1)S(1)}, u32[]{:S(2)}, u32[]{:S(2)}) collective-permute-start(bf16[512,1024]{1,0:T(8,128)(2,1)S(1)} %copy-done.49), channel_id=1, source_target_pairs={{2,0},{4,2},{6,4},{3,1},{5,3},{7,5},{10,8},{12,10},{14,12},{11,9},... | collective-permute-start | bytes 3145736 | tf_op jit(solution)/shard_map/ppermute | solution.py:539
  212.1 28.6 %collective-permute-start.1 = (bf16[512,1024]{1,0:T(8,128)(2,1)S(1)}, bf16[512,1024]{1,0:T(8,128)(2,1)S(1)}, u32[]{:S(2)}, u32[]{:S(2)}) collective-permute-start(bf16[512,1024]{1,0:T(8,128)(2,1)S(1)} %copy-done.49), channel_id=1, source_target_pairs={{0,2},{2,4},{4,6},{1,3},{3,5},{5,7},{8,10},{10,12},{12,14},{9,11},... | collective-permute-start | bytes 3145736 | tf_op jit(solution)/shard_map/ppermute | solution.py:538
  216.7 80.1 %collective-permute-start.9 = (bf16[288,2304]{1,0:T(8,128)(2,1)}, bf16[288,2304]{1,0:T(8,128)(2,1)S(1)}, u32[]{:S(2)}, u32[]{:S(2)}) collective-permute-start(bf16[288,2304]{1,0:T(8,128)(2,1)} %pad_maximum_fusion.10), channel_id=1, source_target_pairs={{0,4},{2,6},{4,0},{6,2},{1,5},{3,7},{5,1},{7,3},{8,12},{10,14},{12... | collective-permute-start | bytes 3981320 | tf_op jit(solution)/shard_map/ppermute | solution.py:499
  239.4 79.6 %collective-permute-start.6 = (bf16[512,1024]{1,0:T(8,128)(2,1)S(1)}, bf16[512,1024]{1,0:T(8,128)(2,1)}, u32[]{:S(2)}, u32[]{:S(2)}) collective-permute-start(bf16[512,1024]{1,0:T(8,128)(2,1)S(1)} %collective-permute-done.5), channel_id=1, source_target_pairs={{2,0},{4,2},{3,1},{5,3},{10,8},{12,10},{11,9},{13,11},{18,16},{20,... | collective-permute-start | bytes 3145736 | tf_op jit(solution)/shard_map/ppermute | solution.py:539
  240.7 78.3 %collective-permute-start.4 = (bf16[512,1024]{1,0:T(8,128)(2,1)S(1)}, bf16[512,1024]{1,0:T(8,128)(2,1)}, u32[]{:S(2)}, u32[]{:S(2)}) collective-permute-start(bf16[512,1024]{1,0:T(8,128)(2,1)S(1)} %collective-permute-done.1), channel_id=1, source_target_pairs={{2,4},{4,6},{3,5},{5,7},{10,12},{12,14},{11,13},{13,15},{18,20},{2... | collective-permute-start | bytes 3145736 | tf_op jit(solution)/shard_map/ppermute | solution.py:538
  321.2 167.3 %all-gather.14.cloned.1.call-start = ((), (), s32[]{:S(2)}) async-start(), calls=%async_computation.7 | async-start | bytes 13271040 | tf_op jit(solution)/shard_map/all_gather | solution.py:573
  321.3 28.7 %collective-permute-start.8 = (bf16[512,1024]{1,0:T(8,128)(2,1)}, bf16[512,1024]{1,0:T(8,128)(2,1)}, u32[]{:S(2)}, u32[]{:S(2)}) collective-permute-start(bf16[512,1024]{1,0:T(8,128)(2,1)} %collective-permute-done.6), channel_id=1, source_target_pairs={{2,0},{3,1},{10,8},{11,9},{18,16},{19,17},{26,24},{27,25}} | collective-permute-start | bytes 3145736 | tf_op jit(solution)/shard_map/ppermute | solution.py:539
  322.6 27.4 %collective-permute-start.7 = (bf16[512,1024]{1,0:T(8,128)(2,1)}, bf16[512,1024]{1,0:T(8,128)(2,1)}, u32[]{:S(2)}, u32[]{:S(2)}) collective-permute-start(bf16[512,1024]{1,0:T(8,128)(2,1)} %collective-permute-done.4), channel_id=1, source_target_pairs={{4,6},{5,7},{12,14},{13,15},{20,22},{21,23},{28,30},{29,31}} | collective-permute-start | bytes 3145736 | tf_op jit(solution)/shard_map/ppermute | solution.py:538
  326.8 62.2 %collective-permute-start.15 = (bf16[288,2304]{1,0:T(8,128)(2,1)}, bf16[288,2304]{1,0:T(8,128)(2,1)}, u32[]{:S(2)}, u32[]{:S(2)}) collective-permute-start(bf16[288,2304]{1,0:T(8,128)(2,1)} %pad_maximum_fusion.11), channel_id=1, source_target_pairs={{0,4},{2,6},{4,0},{6,2},{1,5},{3,7},{5,1},{7,3},{8,12},{10,14},{12... | collective-permute-start | bytes 3981320 | tf_op jit(solution)/shard_map/ppermute | solution.py:499
  379.4 27.0 %collective-permute-start.10 = (bf16[256,2304]{1,0:T(8,128)(2,1)S(1)}, bf16[256,2304]{1,0:T(8,128)(2,1)}, u32[]{:S(2)}, u32[]{:S(2)}) collective-permute-start(bf16[256,2304]{1,0:T(8,128)(2,1)S(1)} %convolution_convert_fusion.6), channel_id=1, source_target_pairs={{0,1},{1,0},{2,3},{3,2},{4,5},{5,4},{6,7},{7,6},{8,9},{9,8},{10,11... | collective-permute-start | bytes 3538952 | tf_op jit(solution)/shard_map/ppermute | solution.py:570
  409.9 533.5 %reduce-scatter.4.cloned.1.call-start = ((), (), s32[]{:S(2)}) async-start(), calls=%async_computation.8 | async-start | bytes 5242880 | tf_op jit(solution)/shard_map/reduce_scatter | solution.py:737
  418.0 25.9 %collective-permute-start.11 = (bf16[256,2304]{1,0:T(8,128)(2,1)S(1)}, bf16[256,2304]{1,0:T(8,128)(2,1)S(1)}, u32[]{:S(2)}, u32[]{:S(2)}) collective-permute-start(bf16[256,2304]{1,0:T(8,128)(2,1)S(1)} %get-tuple-element.152), channel_id=1, source_target_pairs={{0,1},{1,0},{2,3},{3,2},{4,5},{5,4},{6,7},{7,6},{8,9},{9,8},{10,11... | collective-permute-start | bytes 3538952 | tf_op jit(solution)/shard_map/ppermute | solution.py:438
  419.1 26.8 %collective-permute-start.12 = (bf16[256,2304]{1,0:T(8,128)(2,1)S(1)}, bf16[256,2304]{1,0:T(8,128)(2,1)S(1)}, u32[]{:S(2)}, u32[]{:S(2)}) collective-permute-start(bf16[256,2304]{1,0:T(8,128)(2,1)S(1)} %get-tuple-element.152), channel_id=1, source_target_pairs={{0,2},{1,3},{2,0},{3,1},{4,6},{5,7},{6,4},{7,5},{8,10},{9,11},{10,... | collective-permute-start | bytes 3538952 | tf_op jit(solution)/shard_map/ppermute | solution.py:438
  520.2 24.6 %collective-permute-start.17 = (bf16[256,2304]{1,0:T(8,128)(2,1)}, bf16[256,2304]{1,0:T(8,128)(2,1)}, u32[]{:S(2)}, u32[]{:S(2)}) collective-permute-start(bf16[256,2304]{1,0:T(8,128)(2,1)} %pad_maximum_fusion.13), channel_id=1, source_target_pairs={{0,2},{1,3},{2,0},{3,1},{4,6},{5,7},{6,4},{7,5},{8,10},{9,11},{10,... | collective-permute-start | bytes 3538952 | tf_op jit(solution)/shard_map/ppermute | solution.py:438
  522.0 24.7 %collective-permute-start.19 = (bf16[256,2304]{1,0:T(8,128)(2,1)}, bf16[256,2304]{1,0:T(8,128)(2,1)}, u32[]{:S(2)}, u32[]{:S(2)}) collective-permute-start(bf16[256,2304]{1,0:T(8,128)(2,1)} %pad_maximum_fusion.14), channel_id=1, source_target_pairs={{0,1},{1,0},{2,3},{3,2},{4,5},{5,4},{6,7},{7,6},{8,9},{9,8},{10,11... | collective-permute-start | bytes 3538952 | tf_op jit(solution)/shard_map/ppermute | solution.py:438
  554.9 23.9 %collective-permute-start.21 = (bf16[256,2304]{1,0:T(8,128)(2,1)}, bf16[256,2304]{1,0:T(8,128)(2,1)}, u32[]{:S(2)}, u32[]{:S(2)}) collective-permute-start(bf16[256,2304]{1,0:T(8,128)(2,1)} %get-tuple-element.148), channel_id=1, source_target_pairs={{0,1},{1,0},{2,3},{3,2},{4,5},{5,4},{6,7},{7,6},{8,9},{9,8},{10,11... | collective-permute-start | bytes 3538952 | tf_op jit(solution)/shard_map/ppermute | solution.py:438
  555.2 25.5 %collective-permute-start.22 = (bf16[256,2304]{1,0:T(8,128)(2,1)}, bf16[256,2304]{1,0:T(8,128)(2,1)}, u32[]{:S(2)}, u32[]{:S(2)}) collective-permute-start(bf16[256,2304]{1,0:T(8,128)(2,1)} %get-tuple-element.148), channel_id=1, source_target_pairs={{0,2},{1,3},{2,0},{3,1},{4,6},{5,7},{6,4},{7,5},{8,10},{9,11},{10,... | collective-permute-start | bytes 3538952 | tf_op jit(solution)/shard_map/ppermute | solution.py:438
  613.5 87.6 %collective-permute-start.26 = (bf16[576,2304]{1,0:T(8,128)(2,1)}, bf16[576,2304]{1,0:T(8,128)(2,1)}, u32[]{:S(2)}, u32[]{:S(2)}) collective-permute-start(bf16[576,2304]{1,0:T(8,128)(2,1)} %get-tuple-element.163), channel_id=1, source_target_pairs={{0,8},{8,0},{16,24},{24,16},{1,9},{9,1},{17,25},{25,17},{2,10},{10... | collective-permute-start | bytes 7962632 | tf_op jit(solution)/shard_map/ppermute | solution.py:600
  623.5 77.7 %collective-permute-start.27 = (bf16[576,2304]{1,0:T(8,128)(2,1)}, bf16[576,2304]{1,0:T(8,128)(2,1)}, u32[]{:S(2)}, u32[]{:S(2)}) collective-permute-start(bf16[576,2304]{1,0:T(8,128)(2,1)} %add_convert_fusion.5), channel_id=1, source_target_pairs={{0,16},{8,24},{16,0},{24,8},{1,17},{9,25},{17,1},{25,9},{2,18},{10... | collective-permute-start | bytes 7962632 | tf_op jit(solution)/shard_map/ppermute | solution.py:614
  678.1 53.4 %collective-permute-start.29 = (bf16[256,2304]{1,0:T(8,128)(2,1)}, bf16[256,2304]{1,0:T(8,128)(2,1)}, u32[]{:S(2)}, u32[]{:S(2)}) collective-permute-start(bf16[256,2304]{1,0:T(8,128)(2,1)} %get-tuple-element.97), channel_id=1, source_target_pairs={{0,1},{1,0},{2,3},{3,2},{4,5},{5,4},{6,7},{7,6},{8,9},{9,8},{10,11... | collective-permute-start | bytes 3538952 | tf_op jit(solution)/shard_map/ppermute | solution.py:431
  680.1 51.5 %collective-permute-start.30 = (bf16[256,2304]{1,0:T(8,128)(2,1)}, bf16[256,2304]{1,0:T(8,128)(2,1)}, u32[]{:S(2)}, u32[]{:S(2)}) collective-permute-start(bf16[256,2304]{1,0:T(8,128)(2,1)} %get-tuple-element.98), channel_id=1, source_target_pairs={{0,2},{1,3},{2,0},{3,1},{4,6},{5,7},{6,4},{7,5},{8,10},{9,11},{10,... | collective-permute-start | bytes 3538952 | tf_op jit(solution)/shard_map/ppermute | solution.py:431
  681.5 51.3 %collective-permute-start.31 = (bf16[256,2304]{1,0:T(8,128)(2,1)}, bf16[256,2304]{1,0:T(8,128)(2,1)}, u32[]{:S(2)}, u32[]{:S(2)}) collective-permute-start(bf16[256,2304]{1,0:T(8,128)(2,1)} %get-tuple-element.99), channel_id=1, source_target_pairs={{0,3},{1,2},{2,1},{3,0},{4,7},{5,6},{6,5},{7,4},{8,11},{9,10},{10,... | collective-permute-start | bytes 3538952 | tf_op jit(solution)/shard_map/ppermute | solution.py:431
  738.8 27.5 %collective-permute-start.32 = (bf16[256,2304]{1,0:T(8,128)(2,1)S(1)}, bf16[256,2304]{1,0:T(8,128)(2,1)S(1)}, u32[]{:S(2)}, u32[]{:S(2)}) collective-permute-start(bf16[256,2304]{1,0:T(8,128)(2,1)S(1)} %fusion.16), channel_id=1, source_target_pairs={{0,1},{1,0},{2,3},{3,2},{4,5},{5,4},{6,7},{7,6},{8,9},{9,8},{10,11... | collective-permute-start | bytes 3538952 | tf_op jit(solution)/shard_map/ppermute | solution.py:709
  740.7 60.5 %collective-permute-start.35 = (bf16[576,2304]{1,0:T(8,128)(2,1)S(1)}, bf16[576,2304]{1,0:T(8,128)(2,1)S(1)}, u32[]{:S(2)}, u32[]{:S(2)}) collective-permute-start(bf16[576,2304]{1,0:T(8,128)(2,1)S(1)} %copy-done.54), channel_id=1, source_target_pairs={{0,16},{8,24},{16,0},{24,8},{1,17},{9,25},{17,1},{25,9},{2,18},{10... | collective-permute-start | bytes 7962632 | tf_op jit(solution)/shard_map/ppermute | solution.py:614
  740.8 62.0 %collective-permute-start.34 = (bf16[576,2304]{1,0:T(8,128)(2,1)S(1)}, bf16[576,2304]{1,0:T(8,128)(2,1)}, u32[]{:S(2)}, u32[]{:S(2)}) collective-permute-start(bf16[576,2304]{1,0:T(8,128)(2,1)S(1)} %get-tuple-element.166), channel_id=1, source_target_pairs={{0,8},{8,0},{16,24},{24,16},{1,9},{9,1},{17,25},{25,17},{2,10},{10... | collective-permute-start | bytes 7962632 | tf_op jit(solution)/shard_map/ppermute | solution.py:600
  740.8 71.3 %collective-permute-start.36 = (bf16[288,2304]{1,0:T(8,128)(2,1)}, bf16[288,2304]{1,0:T(8,128)(2,1)S(1)}, u32[]{:S(2)}, u32[]{:S(2)}) collective-permute-start(bf16[288,2304]{1,0:T(8,128)(2,1)} %broadcast_select_fusion.2), channel_id=1, source_target_pairs={{0,4},{2,6},{4,0},{6,2},{1,5},{3,7},{5,1},{7,3},{8,12},{10,14},{12... | collective-permute-start | bytes 3981320 | tf_op jit(solution)/shard_map/ppermute | solution.py:648
  750.2 116.1 %collective-permute-start.39 = (bf16[576,2304]{1,0:T(8,128)(2,1)}, bf16[576,2304]{1,0:T(8,128)(2,1)}, u32[]{:S(2)}, u32[]{:S(2)}) collective-permute-start(bf16[576,2304]{1,0:T(8,128)(2,1)} %add_convert_fusion.2), channel_id=1, source_target_pairs={{0,16},{8,24},{16,0},{24,8},{1,17},{9,25},{17,1},{25,9},{2,18},{10... | collective-permute-start | bytes 7962632 | tf_op jit(solution)/shard_map/ppermute | solution.py:614
  807.2 59.2 %collective-permute-start.38 = (bf16[288,2304]{1,0:T(8,128)(2,1)S(1)}, bf16[288,2304]{1,0:T(8,128)(2,1)}, u32[]{:S(2)}, u32[]{:S(2)}) collective-permute-start(bf16[288,2304]{1,0:T(8,128)(2,1)S(1)} %broadcast_select_fusion.1), channel_id=1, source_target_pairs={{0,4},{2,6},{4,0},{6,2},{1,5},{3,7},{5,1},{7,3},{8,12},{10,14},{12... | collective-permute-start | bytes 3981320 | tf_op jit(solution)/shard_map/ppermute | solution.py:648
  866.4 235.5 %reduce-scatter.8.cloned.1.call-start = ((), (), s32[]{:S(2)}) async-start(), calls=%async_computation.10 | async-start | bytes 1474560 | tf_op jit(solution)/shard_map/reduce_scatter | solution.py:626
  867.2 86.2 %collective-permute-start.20 = (bf16[256,2304]{1,0:T(8,128)(2,1)}, bf16[256,2304]{1,0:T(8,128)(2,1)}, u32[]{:S(2)}, u32[]{:S(2)}) collective-permute-start(bf16[256,2304]{1,0:T(8,128)(2,1)} %get-tuple-element.194), channel_id=1, source_target_pairs={{0,1},{1,0},{2,3},{3,2},{4,5},{5,4},{6,7},{7,6},{8,9},{9,8},{10,11... | collective-permute-start | bytes 3538952 | tf_op jit(solution)/shard_map/ppermute | solution.py:415
  869.1 31.0 %collective-permute-start.42 = (bf16[576,1024]{1,0:T(8,128)(2,1)}, bf16[576,1024]{1,0:T(8,128)(2,1)S(1)}, u32[]{:S(2)}, u32[]{:S(2)}) collective-permute-start(bf16[576,1024]{1,0:T(8,128)(2,1)} %get-tuple-element.172), channel_id=1, source_target_pairs={{0,8},{8,0},{16,24},{24,16},{1,9},{9,1},{17,25},{25,17},{2,10},{10... | collective-permute-start | bytes 3538952 | tf_op jit(solution)/shard_map/ppermute | solution.py:600
  872.0 28.1 %collective-permute-start.43 = (bf16[576,1024]{1,0:T(8,128)(2,1)S(1)}, bf16[576,1024]{1,0:T(8,128)(2,1)S(1)}, u32[]{:S(2)}, u32[]{:S(2)}) collective-permute-start(bf16[576,1024]{1,0:T(8,128)(2,1)S(1)} %add_convert_fusion.11), channel_id=1, source_target_pairs={{0,16},{8,24},{16,0},{24,8},{1,17},{9,25},{17,1},{25,9},{2,18},{10... | collective-permute-start | bytes 3538952 | tf_op jit(solution)/shard_map/ppermute | solution.py:614
  962.2 28.2 %collective-permute-start.48 = (bf16[576,1024]{1,0:T(8,128)(2,1)S(1)}, bf16[576,1024]{1,0:T(8,128)(2,1)S(1)}, u32[]{:S(2)}, u32[]{:S(2)}) collective-permute-start(bf16[576,1024]{1,0:T(8,128)(2,1)S(1)} %add_convert_fusion.8), channel_id=1, source_target_pairs={{0,16},{8,24},{16,0},{24,8},{1,17},{9,25},{17,1},{25,9},{2,18},{10... | collective-permute-start | bytes 3538952 | tf_op jit(solution)/shard_map/ppermute | solution.py:614
  965.3 79.8 %collective-permute-start.57 = (bf16[288,2304]{1,0:T(8,128)(2,1)}, bf16[288,2304]{1,0:T(8,128)(2,1)}, u32[]{:S(2)}, u32[]{:S(2)}) collective-permute-start(bf16[288,2304]{1,0:T(8,128)(2,1)} %broadcast_select_fusion), channel_id=1, source_target_pairs={{0,4},{2,6},{4,0},{6,2},{1,5},{3,7},{5,1},{7,3},{8,12},{10,14},{12... | collective-permute-start | bytes 3981320 | tf_op jit(solution)/shard_map/ppermute | solution.py:648
  967.2 67.9 %collective-permute-start.54 = (bf16[576,1024]{1,0:T(8,128)(2,1)}, bf16[576,1024]{1,0:T(8,128)(2,1)}, u32[]{:S(2)}, u32[]{:S(2)}) collective-permute-start(bf16[576,1024]{1,0:T(8,128)(2,1)} %get-tuple-element.169), channel_id=1, source_target_pairs={{0,8},{8,0},{16,24},{24,16},{1,9},{9,1},{17,25},{25,17},{2,10},{10... | collective-permute-start | bytes 3538952 | tf_op jit(solution)/shard_map/ppermute | solution.py:600
  980.3 50.0 %collective-permute-start.56 = (bf16[144,2304]{1,0:T(8,128)(2,1)}, bf16[144,2304]{1,0:T(8,128)(2,1)S(1)}, u32[]{:S(2)}, u32[]{:S(2)}) collective-permute-start(bf16[144,2304]{1,0:T(8,128)(2,1)} %select_convert_fusion.1), channel_id=1, source_target_pairs={{0,2},{2,0},{4,6},{6,4},{1,3},{3,1},{5,7},{7,5},{8,10},{10,8},{12,... | collective-permute-start | bytes 1990664 | tf_op jit(solution)/shard_map/ppermute | solution.py:667
  992.2 112.3 %reduce-scatter.6.cloned.1.call-start = ((), (), s32[]{:S(2)}) async-start(), calls=%async_computation.9 | async-start | bytes 2949120 | tf_op jit(solution)/shard_map/reduce_scatter | solution.py:783
  995.8 39.3 %collective-permute-start.55 = (bf16[576,1024]{1,0:T(8,128)(2,1)}, bf16[576,1024]{1,0:T(8,128)(2,1)S(1)}, u32[]{:S(2)}, u32[]{:S(2)}) collective-permute-start(bf16[576,1024]{1,0:T(8,128)(2,1)} %add_convert_fusion.10), channel_id=1, source_target_pairs={{0,16},{8,24},{16,0},{24,8},{1,17},{9,25},{17,1},{25,9},{2,18},{10... | collective-permute-start | bytes 3538952 | tf_op jit(solution)/shard_map/ppermute | solution.py:614
  1033.9 27.1 %collective-permute-start.45 = (bf16[256,2304]{1,0:T(8,128)(2,1)}, bf16[256,2304]{1,0:T(8,128)(2,1)}, u32[]{:S(2)}, u32[]{:S(2)}) collective-permute-start(bf16[256,2304]{1,0:T(8,128)(2,1)} %slice.526), channel_id=1, source_target_pairs={{0,1},{1,0},{2,3},{3,2},{4,5},{5,4},{6,7},{7,6},{8,9},{9,8},{10,11... | collective-permute-start | bytes 3538952 | tf_op jit(solution)/shard_map/ppermute | solution.py:775
  1047.1 32.4 %collective-permute-start.58 = (bf16[144,2304]{1,0:T(8,128)(2,1)S(1)}, bf16[144,2304]{1,0:T(8,128)(2,1)S(1)}, u32[]{:S(2)}, u32[]{:S(2)}) collective-permute-start(bf16[144,2304]{1,0:T(8,128)(2,1)S(1)} %select_convert_fusion), channel_id=1, source_target_pairs={{0,2},{2,0},{4,6},{6,4},{1,3},{3,1},{5,7},{7,5},{8,10},{10,8},{12,... | collective-permute-start | bytes 1990664 | tf_op jit(solution)/shard_map/ppermute | solution.py:667
  1068.6 28.4 %collective-permute-start.46 = (bf16[256,2304]{1,0:T(8,128)(2,1)S(1)}, bf16[256,2304]{1,0:T(8,128)(2,1)S(1)}, u32[]{:S(2)}, u32[]{:S(2)}) collective-permute-start(bf16[256,2304]{1,0:T(8,128)(2,1)S(1)} %fusion.18), channel_id=1, source_target_pairs={{0,1},{1,0},{2,3},{3,2},{4,5},{5,4},{6,7},{7,6},{8,9},{9,8},{10,11... | collective-permute-start | bytes 3538952 | tf_op jit(solution)/shard_map/ppermute | solution.py:415
  (109 other events, 2333.6 us)
Sparse Core Ops, SparseCore 0:
  14.6 81.2 all-gather.5
  98.8 122.8 all-gather.7
  223.8 69.6 all-gather.9
  321.4 70.8 all-gather.11
  410.0 73.1 all-gather.13
  866.5 76.8 reduce-scatter.3
  992.3 44.5 reduce-scatter.7
  1039.3 64.4 reduce-scatter.5
